TPU v7x, 256 devices: a whole 4x4x8 slice. The times are simulated.
256 devices in a mesh: nodes: 8 (over x, core), batch: 32 (over z, y).
Axes of the slice: x: 4, y: 4, z: 8, core: 2. Of those that a mesh axis runs over, the one named last changes fastest.
Arguments:
- leaves: float32 [16, 128, 4096], P('nodes', None, 'batch'), may hold values from -340 to 8
- prod_child: int32 [16, 2], replicated, may hold values from 0 to 15
- block_weight: float32 [1024, 128, 128], P('nodes'), may hold values from 0.0001 to 0.01
- block_child: int32 [8, 128], P('nodes'), may hold values from 0 to 15
- block_parent: int32 [8, 128], P('nodes'), may hold values from 0 to 3, as said below
- block_count: int32 [8], P('nodes'), may hold values from 32 to 128, as said below
- upper_flow: float32 [32, 128, 4096], P('nodes', None, 'batch'), may hold values from 0.1 to 1
Outputs:
- sum_values: float32 [32, 128, 4096], P('nodes', None, 'batch')
- leaf_flow: float32 [16, 128, 4096], P('nodes', None, 'batch')
- param_flow: float32 [1024, 128, 128], P(('nodes', 'batch'))
Inputs may be any that keep to these rules, and one draw needn't show every extreme that they name: `block_parent`: every owner's first 4 slots name its sum groups 0 to 3 in order. `block_count`: some owner has all 128 slots live.
All inputs are finite; a program needn't handle non-finite values.
Results may differ from a plain program's by a relative error of at most 0.0003.
Values sent between devices are 32-bit elements; how exact they have to be, the bound alone decides.
No kernel may reach another device: no remote copies, remote signals or barrier semaphores. Data moves between devices by JAX's collectives and lax.ppermute only.
A program may use at most 128 MiB of HBM per device.

v0:
```python
import functools

import jax
import jax.numpy as jnp
from jax import lax
from jax.experimental import pallas as pl
from jax.experimental.pallas import tpu as pltpu
from jax.sharding import PartitionSpec as P


very_low = -1e30
f32, bf16 = jnp.float32, jnp.bfloat16
CORES = 2
ROWS = 4
VMEM = pltpu.VMEM
SMEM = pltpu.SMEM


def parts(x):
    hi = x.astype(bf16)
    lo = (x - hi.astype(f32)).astype(bf16)
    return hi, lo


def quadrants(x):
    g = x.shape[0] // 2
    return (x[:g, :g] + x[:g, g:]) + (x[g:, :g] + x[g:, g:])


def node_at(dx, dc, nodes):
    me = lax.axis_index("nodes")
    x, core = me // CORES, me % CORES
    chips = nodes // CORES
    return ((x + dx) % chips) * CORES + (core + dc) % CORES


def hops(nodes):
    return [(dx, dc) for dx in range(nodes // CORES) for dc in range(CORES)]


def vmem_specs(n):
    return [pl.BlockSpec(memory_space=VMEM)] * n


def fold_kernel(child, parent, count, w_ref, acc, bias):
    step = pl.program_id(0)
    each = w_ref.shape[0]
    pg = acc.shape[1]

    @pl.when(step == 0)
    def _():
        bias[...] = jnp.full(bias.shape, very_low, f32)

        def clear(c, carry):
            for q in range(acc.shape[0]):
                acc[q, c] = jnp.zeros(acc.shape[2:], f32)
            return carry

        lax.fori_loop(0, pg, clear, 0)

    def add(t, carry):
        b = step * each + t

        @pl.when(b < count[0])
        def _():
            c, q = child[0, b], parent[0, b]
            acc[q, c] += w_ref[t]
            bias[pl.ds(q * pg + c, 1), :] = jnp.zeros((1, bias.shape[1]), f32)

        return carry

    lax.fori_loop(0, each, add, 0)


def fold(block_child, block_parent, block_count, block_weight, pg, qd):
    blocks, g, _ = block_weight.shape
    each = 16
    return pl.pallas_call(
        fold_kernel,
        out_shape=(
            jax.ShapeDtypeStruct((qd, pg, g, g), f32),
            jax.ShapeDtypeStruct((qd * pg, g), f32),
        ),
        grid_spec=pltpu.PrefetchScalarGridSpec(
            num_scalar_prefetch=3,
            grid=(blocks // each,),
            in_specs=[pl.BlockSpec((each, g, g), lambda i, *_: (i, 0, 0))],
            out_specs=(
                pl.BlockSpec((qd, pg, g, g), lambda i, *_: (0, 0, 0, 0)),
                pl.BlockSpec((qd * pg, g), lambda i, *_: (0, 0)),
            ),
        ),
        compiler_params=pltpu.CompilerParams(vmem_limit_bytes=46 << 20),
        cost_estimate=pl.CostEstimate(flops=20_000_000, bytes_accessed=16 << 20, transcendentals=0),
        name="fold",
    )(block_child, block_parent, block_count, block_weight)


def forward_kernel(nodes, prod_child, *refs):
    n = nodes
    got = refs[:n]
    w_ref, bias, up, sv, fx, e_ref, r_ref, pk_ref, lv, whl, shl, peak = refs[n:]
    pg, g, s = e_ref.shape
    q = pl.program_id(0)

    @pl.when(q == 0)
    def _():
        for k, (dx, dc) in enumerate(hops(n)):
            src = node_at(-dx, -dc, n)
            each = got[k].shape[0]
            lv[pl.ds(src * each, each)] = got[k][...]

        def product(p, carry):
            x = lv[prod_child[0, p]] + lv[prod_child[1, p]]
            m = jnp.max(x, axis=0, keepdims=True)
            peak[pl.ds(p, 1), :] = m
            e_ref[p] = jnp.exp(x - m)
            return carry

        lax.fori_loop(0, pg, product, 0, unroll=2)
        pk_ref[...] = peak[...]

    biased = peak[...] + bias[...]
    top = jnp.max(biased, axis=0, keepdims=True)
    r_ref[...] = jnp.exp(biased - top)

    def scaled(c, carry):
        at = pl.ds(pl.multiple_of(c * g, g), g)
        hi, lo = parts(w_ref[0, c])
        whl[0:g, at] = hi
        whl[g : 2 * g, at] = lo
        hi, lo = parts(e_ref[c] * r_ref[pl.ds(c, 1), :])
        shl[at, 0:s] = hi
        shl[at, s : 2 * s] = lo
        return carry

    lax.fori_loop(0, pg, scaled, 0, unroll=2)
    total = quadrants(jnp.dot(whl[...], shl[...], preferred_element_type=f32))
    sv[0] = top + jnp.log(total)
    fx[0, 0:g] = up[0] / total
    fx[0, g:] = jnp.broadcast_to(top, (8, s))


def forward(prod_child, got, w, bias, up):
    nodes = len(got)
    qd, g, s = up.shape
    pg = prod_child.shape[1]
    one = lambda *shape: pl.BlockSpec(shape, lambda q, *_: (q,) + (0,) * (len(shape) - 1))
    whole = lambda *shape: pl.BlockSpec(shape, lambda q, *_: (0,) * len(shape))
    return pl.pallas_call(
        functools.partial(forward_kernel, nodes),
        out_shape=(
            jax.ShapeDtypeStruct((qd, g, s), f32),
            jax.ShapeDtypeStruct((qd, g + 8, s), f32),
            jax.ShapeDtypeStruct((pg, g, s), f32),
            jax.ShapeDtypeStruct((qd * pg, s), f32),
            jax.ShapeDtypeStruct((pg, s), f32),
        ),
        grid_spec=pltpu.PrefetchScalarGridSpec(
            num_scalar_prefetch=1,
            grid=(qd,),
            in_specs=[whole(*got[0].shape)] * nodes
            + [one(1, pg, g, g), one(pg, g), one(1, g, s)],
            out_specs=(one(1, g, s), one(1, g + 8, s), whole(pg, g, s), one(pg, s), whole(pg, s)),
            scratch_shapes=[
                VMEM((got[0].shape[0] * nodes, g, s), f32),
                VMEM((2 * g, pg * g), bf16),
                VMEM((pg * g, 2 * s), bf16),
                VMEM((pg, s), f32),
            ],
        ),
        compiler_params=pltpu.CompilerParams(vmem_limit_bytes=20 << 20),
        cost_estimate=pl.CostEstimate(
            flops=2 * qd * 4 * g * s * pg * g, bytes_accessed=8 << 20, transcendentals=pg * g * s
        ),
        name="forward",
    )(prod_child, *got, w, bias, up)


def backward_kernel(nodes, prod_child, w_ref, fx, r_ref, e_ref, token, *refs):
    chips = nodes // CORES
    keep, give, (lf, thl, ghl) = refs[:chips], refs[chips], refs[chips + 1 :]
    step = pl.program_id(0)
    qd = fx.shape[0]
    each, g, s = e_ref.shape
    pg = each * pl.num_programs(0)

    @pl.when(step == 0)
    def _():
        lf[...] = jnp.zeros(lf.shape, f32)

    for t in range(each):
        c = step * each + t
        for q in range(qd):
            at = slice(q * g, (q + 1) * g)
            hi, lo = parts(w_ref[q, t].T)
            thl[t, 0:g, at] = hi
            thl[t, g : 2 * g, at] = lo
            hi, lo = parts(fx[q, 0:g] * r_ref[pl.ds(q * pg + c, 1), :])
            ghl[t, at, 0:s] = hi
            ghl[t, at, s : 2 * s] = lo
    for t in range(each):
        c = step * each + t
        back = quadrants(jnp.dot(thl[t], ghl[t], preferred_element_type=f32))
        flow = back * e_ref[t]
        lf[prod_child[0, c]] += flow
        lf[prod_child[1, c]] += flow

    @pl.when(step == pl.num_programs(0) - 1)
    def _():
        for dx in range(chips):
            k = keep[0].shape[0]
            keep[dx][...] = lf[pl.ds(node_at(dx, 0, nodes) * k, k)]
            give[dx * k : (dx + 1) * k] = lf[pl.ds(node_at(dx, 1, nodes) * k, k)]


def backward(prod_child, w, fx, r, e, token, nodes, ng):
    pg, g, s = e.shape
    qd = fx.shape[0]
    chips = nodes // CORES
    each = 4
    whole = lambda *shape: pl.BlockSpec(shape, lambda q, *_: (0,) * len(shape))
    one = lambda *shape: pl.BlockSpec(shape, lambda q, *_: (q,) + (0,) * (len(shape) - 1))
    k = ng // nodes
    return pl.pallas_call(
        functools.partial(backward_kernel, nodes),
        out_shape=[jax.ShapeDtypeStruct((k, g, s), f32)] * chips
        + [jax.ShapeDtypeStruct((k * chips, g, s), f32)],
        grid_spec=pltpu.PrefetchScalarGridSpec(
            num_scalar_prefetch=1,
            grid=(pg // each,),
            in_specs=[
                pl.BlockSpec((qd, each, g, g), lambda i, *_: (0, i, 0, 0)),
                whole(*fx.shape),
                whole(*r.shape),
                one(each, g, s),
                pl.BlockSpec(memory_space=pl.ANY),
            ],
            out_specs=[whole(k, g, s)] * chips + [whole(k * chips, g, s)],
            scratch_shapes=[
                VMEM((ng, g, s), f32),
                VMEM((each, 2 * g, qd * g), bf16),
                VMEM((each, qd * g, 2 * s), bf16),
            ],
        ),
        compiler_params=pltpu.CompilerParams(vmem_limit_bytes=20 << 20),
        cost_estimate=pl.CostEstimate(
            flops=2 * qd * 4 * g * s * pg * g, bytes_accessed=8 << 20, transcendentals=0
        ),
        name="backward",
    )(prod_child, w, fx, r, e, token)


def pack_kernel(*refs):
    for t, a in enumerate(refs[:-1]):
        refs[-1][t] = a[...]


def pack(arrays):
    return pl.pallas_call(
        pack_kernel,
        out_shape=jax.ShapeDtypeStruct((len(arrays),) + arrays[0].shape, f32),
        in_specs=vmem_specs(len(arrays)),
        out_specs=vmem_specs(1)[0],
        compiler_params=pltpu.CompilerParams(vmem_limit_bytes=4 << 20),
        cost_estimate=pl.CostEstimate(flops=0, bytes_accessed=1 << 20, transcendentals=0),
        name="pack",
    )(*arrays)


def spread_kernel(offsets, prod_child, e_own, pk_own, *refs):
    pieces, (ehl, pk) = refs[: len(offsets)], refs[len(offsets) : -1]
    lv = refs[-1]
    pg, g, s = e_own.shape
    sets, each = pieces[0].shape[:2]
    nodes = lv.shape[1] // each
    for (dx, dc), piece in zip(offsets, pieces):
        src = node_at(-dx, -dc, nodes)
        for t in range(sets):
            lv[t, pl.ds(src * each, each)] = piece[t]

    def product(p, carry):
        hi, lo = parts(e_own[p])
        ehl[p, 0:g, 0:s] = hi
        ehl[p, g : 2 * g, 0:s] = lo
        pk[0, pl.ds(p, 1), :] = pk_own[pl.ds(p, 1), :]
        a, b = prod_child[0, p], prod_child[1, p]
        for t in range(sets):
            x = lv[t, a] + lv[t, b]
            m = jnp.max(x, axis=0, keepdims=True)
            at = slice((t + 1) * s, (t + 2) * s)
            pk[t + 1, pl.ds(p, 1), :] = m
            hi, lo = parts(jnp.exp(x - m))
            ehl[p, 0:g, at] = hi
            ehl[p, g : 2 * g, at] = lo
        return carry

    lax.fori_loop(0, pg, product, 0)


def spread(prod_child, e, pk, pieces, offsets, nodes):
    pg, g, s = e.shape
    sets, each = pieces[0].shape[:2]

    def kernel(*refs):
        spread_kernel(offsets, *refs)

    return pl.pallas_call(
        kernel,
        out_shape=(
            jax.ShapeDtypeStruct((pg, 2 * g, (sets + 1) * s), bf16),
            jax.ShapeDtypeStruct((sets + 1, pg, s), f32),
        ),
        in_specs=[pl.BlockSpec(memory_space=SMEM)] + vmem_specs(2 + len(pieces)),
        out_specs=tuple(vmem_specs(2)),
        scratch_shapes=[VMEM((sets, nodes * each, g, s), f32)],
        compiler_params=pltpu.CompilerParams(vmem_limit_bytes=20 << 20),
        cost_estimate=pl.CostEstimate(
            flops=10_000_000, bytes_accessed=10 << 20, transcendentals=pg * g * s * sets
        ),
        name="spread",
    )(prod_child, e, pk, *pieces)


def edges_kernel(plan, child, parent, count, ehl, pk, bias, *refs):
    rows = ROWS
    fxs, refs = refs[:rows], refs[rows:]
    outs, (r, lhs) = refs[1:-2], refs[-2:]
    qd, s = fxs[0].shape[0], fxs[0].shape[2]
    g = fxs[0].shape[1] - 8
    pg = pk.shape[1]
    batch = lax.axis_index("batch")
    z, y = batch // ROWS, batch % ROWS
    depth = lax.axis_size("batch") // ROWS
    for q in range(qd):
        for t in range(rows):
            top = fxs[t][q, g : g + 1]
            here = slice(q * pg, (q + 1) * pg)
            r[t, here, :] = jnp.exp((pk[t] + bias[here, :]) - top)
    for (d, k0, n, keep), out in zip(plan, outs):
        base = ((z + d + depth) % depth * ROWS + y) * keep + k0
        for k in range(n):
            b = base + k
            c, q = child[0, b], parent[0, b]
            live = (b < count[0]).astype(f32)
            for t in range(rows):
                at = slice(t * s, (t + 1) * s)
                hi, lo = parts(fxs[t][q, 0:g] * (r[t, pl.ds(q * pg + c, 1), :] * live))
                lhs[k, 0:g, at] = hi
                lhs[k, g : 2 * g, at] = lo
        for k in range(n):
            c = child[0, base + k]
            out[k] = quadrants(
                lax.dot_general(
                    lhs[k], ehl[c], (((1,), (1,)), ((), ())), preferred_element_type=f32
                )
            )


def edges(child, parent, count, ehl, pk, bias, fxs, token, plan):
    g = ehl.shape[1] // 2
    pg, width = pk.shape[1], ehl.shape[2]
    qd = fxs[0].shape[0]
    slots = sum(n for _, _, n, _ in plan)

    def kernel(*refs):
        edges_kernel(plan, *refs)

    return pl.pallas_call(
        kernel,
        out_shape=[jax.ShapeDtypeStruct((n, g, g), f32) for _, _, n, _ in plan],
        in_specs=[pl.BlockSpec(memory_space=SMEM)] * 3
        + vmem_specs(3 + len(fxs))
        + [pl.BlockSpec(memory_space=pl.ANY)],
        out_specs=vmem_specs(len(plan)),
        scratch_shapes=[
            VMEM((len(fxs), qd * pg, width // len(fxs)), f32),
            VMEM((max(n for _, _, n, _ in plan), 2 * g, width), bf16),
        ],
        compiler_params=pltpu.CompilerParams(vmem_limit_bytes=20 << 20),
        cost_estimate=pl.CostEstimate(
            flops=2 * slots * 4 * g * g * width, bytes_accessed=6 << 20, transcendentals=0
        ),
        name="edges",
    )(child, parent, count, ehl, pk, bias, *fxs, token)


def join_kernel(at, a_ref, b_ref, c_ref, token, out):
    n = c_ref.shape[0]
    out[...] = a_ref[...] + b_ref[...]
    out[at : at + n] += c_ref[...]


def join(a, b, c, token, at):
    return pl.pallas_call(
        functools.partial(join_kernel, at),
        out_shape=jax.ShapeDtypeStruct(a.shape, f32),
        in_specs=vmem_specs(3) + [pl.BlockSpec(memory_space=pl.ANY)],
        out_specs=vmem_specs(1)[0],
        compiler_params=pltpu.CompilerParams(vmem_limit_bytes=4 << 20),
        cost_estimate=pl.CostEstimate(flops=200_000, bytes_accessed=1 << 20, transcendentals=0),
        name="join",
    )(a, b, c, token)


def body(leaves, prod_child, block_weight, block_child, block_parent, block_count, upper_flow):
    prod_child = prod_child.T
    nodes = lax.axis_size("nodes")
    batch = lax.axis_size("batch")
    chips, depth = nodes // CORES, batch // ROWS
    ng = leaves.shape[0] * nodes
    pg = prod_child.shape[1]
    qd = upper_flow.shape[0]
    keep = block_weight.shape[0] // batch
    half = keep // 2
    far = depth // 2

    def move(a, dx=0, dc=0):
        to = lambda n: ((n // CORES + dx) % chips) * CORES + (n % CORES + dc) % CORES
        return lax.ppermute(a, "nodes", [(n, to(n)) for n in range(nodes)])

    def shift(a, dz=0, dy=0):
        to = lambda b: ((b // ROWS + dz) % depth) * ROWS + (b % ROWS + dy) % ROWS
        return lax.ppermute(a, "batch", [(b, to(b)) for b in range(batch)])

    def gather(a):
        out = []
        for dx in range(chips):
            got = move(a, dx) if dx else a
            out += [got, move(got, 0, 1)]
        return out

    got = gather(leaves)
    row = [shift(leaves, dy=t) for t in range(1, ROWS)]
    packed = pack(row)
    pieces = gather(packed)

    w, bias = fold(block_child, block_parent, block_count, block_weight, pg, qd)
    sum_values, fx, e, r, pk = forward(prod_child, got, w, bias, upper_flow)
    fxs = [fx] + [shift(fx, dy=t) for t in range(1, ROWS)]
    ehl, pks = spread(prod_child, e, pk, pieces, hops(nodes), nodes)

    def part(token, *plan):
        return edges(
            block_child, block_parent, block_count, ehl, pks, bias, fxs, token, plan
        )

    e4p, e4m, e3p, e3m = part(
        pks, (far, 0, half, keep), (-far, half, half, keep), (3, 0, keep, keep), (-3, 0, keep, keep)
    )
    r4p, r4m = shift(e4p, dz=2), shift(e4m, dz=-2)
    r3p, r3m = shift(e3p, dz=1), shift(e3m, dz=-1)
    e1p, e1m = part(e3m, (1, 0, keep, keep), (-1, 0, keep, keep))
    r1p, r1m = shift(e1p, dz=1), shift(e1m, dz=-1)
    e2p, e2m, e0 = part(e1m, (2, 0, keep, keep), (-2, 0, keep, keep), (0, 0, keep, keep))
    *mine, give = backward(prod_child, w, fx, r, e, e0, nodes, ng)
    c2p = join(e2p, r3p, r4p, give, 0)
    c2m = join(e2m, r3m, r4m, give, half)
    r2p, r2m = shift(c2p, dz=2), shift(c2m, dz=-2)
    given = move(give, 0, 1)
    k = leaves.shape[0]
    flows = [a + given[dx * k : (dx + 1) * k] for dx, a in enumerate(mine)]
    leaf_flow = functools.reduce(
        jnp.add, [flows[0]] + [move(flows[dx], dx) for dx in range(1, chips)]
    )
    wt = lax.dynamic_slice_in_dim(block_weight, lax.axis_index("batch") * keep, keep, 0)
    param_flow = wt * ((e0 + r1p + r1m) + (r2p + r2m))
    return sum_values, leaf_flow, param_flow


def solution(mesh):
    placed = (
        P("nodes", None, "batch"),
        P(),
        P("nodes", None, None),
        P("nodes", None),
        P("nodes", None),
        P("nodes"),
        P("nodes", None, "batch"),
    )
    return jax.shard_map(
        body,
        mesh=mesh,
        in_specs=placed,
        out_specs=(
            P("nodes", None, "batch"),
            P("nodes", None, "batch"),
            P(("nodes", "batch"), None, None),
        ),
        check_vma=False,
    )
```

profile of v0, /device:TPU:2, one launch (start us, length us, event | category | flops | bytes accessed | tf_op | source)
XLA Modules:
  0.0 126.0 jit_solution(4125158124554576683)
XLA Ops:
  0.7 1.7 %collective-permute-start.7 = (f32[2,128,128]{2,1,0:T(8,128)}, f32[2,128,128]{2,1,0:T(8,128)S(1)}, u32[]{:S(2)}, u32[]{:S(2)}) collective-permute-start(f32[2,128,128]{2,1,0:T(8,128)} %refs_0_.4), channel_id=1, source_target_pairs={{0,1},{1,2},{2,3},{3,0},{4,5},{5,6},{6,7},{7,4},{8,9},{9,10},{10,1... | collective-permute-start | bytes 393224 | tf_op jit(solution)/shard_map/ppermute | solution.py:424
  2.3 2.9 %collective-permute-start.8 = (f32[2,128,128]{2,1,0:T(8,128)}, f32[2,128,128]{2,1,0:T(8,128)S(1)}, u32[]{:S(2)}, u32[]{:S(2)}) collective-permute-start(f32[2,128,128]{2,1,0:T(8,128)} %refs_0_.4), channel_id=1, source_target_pairs={{0,2},{1,3},{2,0},{3,1},{4,6},{5,7},{6,4},{7,5},{8,10},{9,11},{10,... | collective-permute-start | bytes 393224 | tf_op jit(solution)/shard_map/ppermute | solution.py:424
  5.2 1.3 %collective-permute-start.9 = (f32[2,128,128]{2,1,0:T(8,128)}, f32[2,128,128]{2,1,0:T(8,128)S(1)}, u32[]{:S(2)}, u32[]{:S(2)}) collective-permute-start(f32[2,128,128]{2,1,0:T(8,128)} %refs_0_.4), channel_id=1, source_target_pairs={{0,3},{1,0},{2,1},{3,2},{4,7},{5,4},{6,5},{7,6},{8,11},{9,8},{10,9... | collective-permute-start | bytes 393224 | tf_op jit(solution)/shard_map/ppermute | solution.py:424
  7.5 4.0 %collective-permute-done.8.refs_1_ = f32[2,128,128]{2,1,0:T(8,128)S(1)} collective-permute-done((f32[2,128,128]{2,1,0:T(8,128)}, f32[2,128,128]{2,1,0:T(8,128)S(1)}, u32[]{:S(2)}, u32[]{:S(2)}) %collective-permute-start.8) | collective-permute-done | bytes 131104 | tf_op jit(solution)/shard_map/ppermute | solution.py:424
  11.5 1.6 %collective-permute-start.11 = (f32[3,2,128,128]{3,2,1,0:T(8,128)S(1)}, f32[3,2,128,128]{3,2,1,0:T(8,128)S(1)}, u32[]{:S(2)}, u32[]{:S(2)}) collective-permute-start(f32[3,2,128,128]{3,2,1,0:T(8,128)S(1)} %pack.1.refs_3_), channel_id=1, source_target_pairs={{0,64},{32,96},{64,128},{96,160},{128,192},{160,224},{192,0},{224,... | collective-permute-start | bytes 1179656 | tf_op jit(solution)/shard_map/ppermute | solution.py:420
  14.3 1.4 %collective-permute-start.3 = (f32[2,128,128]{2,1,0:T(8,128)}, f32[2,128,128]{2,1,0:T(8,128)S(1)}, u32[]{:S(2)}, u32[]{:S(2)}) collective-permute-start(f32[2,128,128]{2,1,0:T(8,128)} %refs_0_.4), channel_id=1, source_target_pairs={{0,128},{32,160},{64,192},{96,224},{128,0},{160,32},{192,64},{224,... | collective-permute-start | bytes 393224 | tf_op jit(solution)/shard_map/ppermute | solution.py:420
  15.7 1.3 %collective-permute-start.5 = (f32[2,128,128]{2,1,0:T(8,128)}, f32[2,128,128]{2,1,0:T(8,128)S(1)}, u32[]{:S(2)}, u32[]{:S(2)}) collective-permute-start(f32[2,128,128]{2,1,0:T(8,128)} %refs_0_.4), channel_id=1, source_target_pairs={{0,192},{32,224},{64,0},{96,32},{128,64},{160,96},{192,128},{224,1... | collective-permute-start | bytes 393224 | tf_op jit(solution)/shard_map/ppermute | solution.py:420
  18.0 8.3 %collective-permute-done.1.refs_2_ = f32[2,128,128]{2,1,0:T(8,128)S(1)} collective-permute-done((f32[2,128,128]{2,1,0:T(8,128)}, f32[2,128,128]{2,1,0:T(8,128)S(1)}, u32[]{:S(2)}, u32[]{:S(2)}) %collective-permute-start.1) | collective-permute-done | bytes 131104 | tf_op jit(solution)/shard_map/ppermute | solution.py:420
  30.1 3.6 %collective-permute-done.13.refs_7_ = f32[3,2,128,128]{3,2,1,0:T(8,128)S(1)} collective-permute-done((f32[3,2,128,128]{3,2,1,0:T(8,128)S(1)}, f32[3,2,128,128]{3,2,1,0:T(8,128)S(1)}, u32[]{:S(2)}, u32[]{:S(2)}) %collective-permute-start.13) | collective-permute-done | bytes 393248 | tf_op jit(solution)/shard_map/ppermute | solution.py:420
  33.7 7.6 %collective-permute-done.15.refs_9_ = f32[3,2,128,128]{3,2,1,0:T(8,128)S(1)} collective-permute-done((f32[3,2,128,128]{3,2,1,0:T(8,128)S(1)}, f32[3,2,128,128]{3,2,1,0:T(8,128)S(1)}, u32[]{:S(2)}, u32[]{:S(2)}) %collective-permute-start.15) | collective-permute-done | bytes 393248 | tf_op jit(solution)/shard_map/ppermute | solution.py:420
  43.2 7.3 %fold.1 = (f32[4,16,128,128]{3,2,1,0:T(8,128)S(1)}, f32[64,128]{1,0:T(8,128)S(1)}) custom-call(s32[1,128]{1,0:T(1,128)S(1)} %copy-done.3, s32[1,128]{1,0:T(1,128)S(1)} %copy-done.4, s32[1]{0:T(128)S(6)} %copy.10.count.refs_2_, f32[128,128,128]{2,1,0:T(8,128)} %w_ref.1), custom_call_target="tpu_custom_call" | custom-call | flops 20000000 | bytes 16777216 | tf_op jit(solution)/shard_map/fold/pallas_call | solution.py:78
  50.6 5.6 %forward.1 = (f32[4,128,128]{2,1,0:T(8,128)}, f32[4,136,128]{2,1,0:T(8,128)S(1)}, f32[16,128,128]{2,1,0:T(8,128)S(1)}, f32[64,128]{1,0:T(8,128)S(1)}, f32[16,128]{1,0:T(8,128)S(1)}) custom-call(s32[2,16]{1,0:T(2,128)S(1)} %bitcast.1, f32[2,128,128]{2,1,0:T(8,128)S(1)} %copy-done.1, f32[2,128,128]{2,1,0:T(8,128)S(1)} %collective-permute-done.refs_1_, ...), custom_call_target="tpu_custom_call" | custom-call | flops 1073741824 | bytes 8388608 | tf_op jit(solution)/shard_map/forward/pallas_call | solution.py:150
  56.2 1.3 %collective-permute-start.17 = (f32[4,136,128]{2,1,0:T(8,128)S(1)}, f32[4,136,128]{2,1,0:T(8,128)S(1)}, u32[]{:S(2)}, u32[]{:S(2)}) collective-permute-start(f32[4,136,128]{2,1,0:T(8,128)S(1)} %get-tuple-element.29.refs_6_.fx), channel_id=1, source_target_pairs={{0,1},{1,2},{2,3},{3,0},{4,5},{5,6},{6,7},{7,4},{8,9},{9,10},{10,1... | collective-permute-start | bytes 835592 | tf_op jit(solution)/shard_map/ppermute | solution.py:424
  57.5 2.4 %collective-permute-start.18 = (f32[4,136,128]{2,1,0:T(8,128)S(1)}, f32[4,136,128]{2,1,0:T(8,128)S(1)}, u32[]{:S(2)}, u32[]{:S(2)}) collective-permute-start(f32[4,136,128]{2,1,0:T(8,128)S(1)} %get-tuple-element.29.refs_6_.fx), channel_id=1, source_target_pairs={{0,2},{1,3},{2,0},{3,1},{4,6},{5,7},{6,4},{7,5},{8,10},{9,11},{10,... | collective-permute-start | bytes 835592 | tf_op jit(solution)/shard_map/ppermute | solution.py:424
  61.2 2.1 %spread.1 = (bf16[16,256,512]{2,1,0:T(8,128)(2,1)S(1)}, f32[4,16,128]{2,1,0:T(8,128)S(1)}) custom-call(s32[2,16]{1,0:T(2,128)S(1)} %bitcast.2, f32[16,128,128]{2,1,0:T(8,128)S(1)} %get-tuple-element.31.refs_1_.e_ref, f32[16,128]{1,0:T(8,128)S(1)} %get-tuple-element.32.refs_2_, f32[3,2,128,128]{3,2,1,0:T(8,128)S(1)} %pack.1.refs_3_, ...), custom_call_target="tpu_custom_call" | custom-call | flops 10000000 | bytes 10485760 | tf_op jit(solution)/shard_map/spread/pallas_call | solution.py:308
  63.3 3.5 %collective-permute-done.17.refs_7_ = f32[4,136,128]{2,1,0:T(8,128)S(1)} collective-permute-done((f32[4,136,128]{2,1,0:T(8,128)S(1)}, f32[4,136,128]{2,1,0:T(8,128)S(1)}, u32[]{:S(2)}, u32[]{:S(2)}) %collective-permute-start.17) | collective-permute-done | bytes 278560 | tf_op jit(solution)/shard_map/ppermute | solution.py:424
  66.9 6.4 %collective-permute-done.18.refs_8_ = f32[4,136,128]{2,1,0:T(8,128)S(1)} collective-permute-done((f32[4,136,128]{2,1,0:T(8,128)S(1)}, f32[4,136,128]{2,1,0:T(8,128)S(1)}, u32[]{:S(2)}, u32[]{:S(2)}) %collective-permute-start.18) | collective-permute-done | bytes 278560 | tf_op jit(solution)/shard_map/ppermute | solution.py:424
  73.5 2.2 %edges.3 = (f32[2,128,128]{2,1,0:T(8,128)S(1)}, f32[2,128,128]{2,1,0:T(8,128)S(1)}, f32[4,128,128]{2,1,0:T(8,128)S(1)}, f32[4,128,128]{2,1,0:T(8,128)S(1)}) custom-call(s32[1,128]{1,0:T(1,128)S(1)} %copy-done.3, s32[1,128]{1,0:T(1,128)S(1)} %copy-done.4, s32[1]{0:T(128)S(6)} %copy.10.count.refs_2_, bf16[16,256,512]{2,1,0:T(8,128)(2,1)S(1)} %get-tuple-element.33.refs_3_, ...), custom_call_target="tpu_custom_call" | custom-call | flops 805306368 | bytes 6291456 | tf_op jit(solution)/shard_map/edges/pallas_call | solution.py:369
  75.7 1.8 %edges.4 = (f32[4,128,128]{2,1,0:T(8,128)S(1)}, f32[4,128,128]{2,1,0:T(8,128)S(1)}) custom-call(s32[1,128]{1,0:T(1,128)S(1)} %copy-done.3, s32[1,128]{1,0:T(1,128)S(1)} %copy-done.4, s32[1]{0:T(128)S(6)} %copy.10.count.refs_2_, bf16[16,256,512]{2,1,0:T(8,128)(2,1)S(1)} %get-tuple-element.33.refs_3_, f32[4,16,128]{2,1,0:T(8,128)S(1)} %get-tuple-element.34.refs_4_.refs_10_, ...), custom_call_target="tpu_custom_call" | custom-call | flops 536870912 | bytes 6291456 | tf_op jit(solution)/shard_map/edges/pallas_call | solution.py:369
  77.5 2.1 %edges.5 = (f32[4,128,128]{2,1,0:T(8,128)S(1)}, f32[4,128,128]{2,1,0:T(8,128)S(1)}, f32[4,128,128]{2,1,0:T(8,128)S(1)}) custom-call(s32[1,128]{1,0:T(1,128)S(1)} %copy-done.3, s32[1,128]{1,0:T(1,128)S(1)} %copy-done.4, s32[1]{0:T(128)S(6)} %copy.10.count.refs_2_, bf16[16,256,512]{2,1,0:T(8,128)(2,1)S(1)} %get-tuple-element.33.refs_3_, ...), custom_call_target="tpu_custom_call" | custom-call | flops 805306368 | bytes 6291456 | tf_op jit(solution)/shard_map/edges/pallas_call | solution.py:369
  79.6 4.0 %backward.1 = (f32[2,128,128]{2,1,0:T(8,128)S(1)}, f32[2,128,128]{2,1,0:T(8,128)S(1)}, f32[2,128,128]{2,1,0:T(8,128)S(1)}, f32[2,128,128]{2,1,0:T(8,128)S(1)}, f32[8,128,128]{2,1,0:T(8,128)S(1)}) custom-call(s32[2,16]{1,0:T(2,128)S(1)} %bitcast.3, f32[4,16,128,128]{3,2,1,0:T(8,128)S(1)} %get-tuple-element.26.refs_8_.w_ref, ...), custom_call_target="tpu_custom_call" | custom-call | flops 1073741824 | bytes 8388608 | tf_op jit(solution)/shard_map/backward/pallas_call | solution.py:225
  83.7 1.9 %collective-permute-start.26 = (f32[4,128,128]{2,1,0:T(8,128)S(1)}, f32[4,128,128]{2,1,0:T(8,128)S(1)}, u32[]{:S(2)}, u32[]{:S(2)}) collective-permute-start(f32[4,128,128]{2,1,0:T(8,128)S(1)} %get-tuple-element.45), channel_id=1, source_target_pairs={{0,4},{1,5},{2,6},{3,7},{4,8},{5,9},{6,10},{7,11},{8,12},{9,13},{1... | collective-permute-start | bytes 786440 | tf_op jit(solution)/shard_map/ppermute | solution.py:424
  85.7 4.1 %collective-permute-start.29 = (f32[4,128,128]{2,1,0:T(8,128)S(1)}, f32[4,128,128]{2,1,0:T(8,128)S(1)}, u32[]{:S(2)}, u32[]{:S(2)}) collective-permute-start(f32[4,128,128]{2,1,0:T(8,128)S(1)} %get-tuple-element.35.refs_10_), channel_id=1, source_target_pairs={{0,28},{1,29},{2,30},{3,31},{4,0},{5,1},{6,2},{7,3},{8,4},{9,5},{1... | collective-permute-start | bytes 786440 | tf_op jit(solution)/shard_map/ppermute | solution.py:424
  89.7 4.1 %collective-permute-start.30 = (f32[2,128,128]{2,1,0:T(8,128)S(1)}, f32[2,128,128]{2,1,0:T(8,128)S(1)}, u32[]{:S(2)}, u32[]{:S(2)}) collective-permute-start(f32[2,128,128]{2,1,0:T(8,128)S(1)} %get-tuple-element.48), channel_id=1, source_target_pairs={{0,24},{1,25},{2,26},{3,27},{4,28},{5,29},{6,30},{7,31},{8,0},{9,1... | collective-permute-start | bytes 393224 | tf_op jit(solution)/shard_map/ppermute | solution.py:424
  93.9 7.2 %collective-permute-done.27.c_ref = f32[2,128,128]{2,1,0:T(8,128)S(1)} collective-permute-done((f32[2,128,128]{2,1,0:T(8,128)S(1)}, f32[2,128,128]{2,1,0:T(8,128)S(1)}, u32[]{:S(2)}, u32[]{:S(2)}) %collective-permute-start.27) | collective-permute-done | bytes 131104 | tf_op jit(solution)/shard_map/ppermute | solution.py:424
  101.1 3.3 %collective-permute-start.25 = (f32[4,128,128]{2,1,0:T(8,128)S(1)}, f32[4,128,128]{2,1,0:T(8,128)S(1)}, u32[]{:S(2)}, u32[]{:S(2)}) collective-permute-start(f32[4,128,128]{2,1,0:T(8,128)S(1)} %get-tuple-element.36.refs_10_), channel_id=1, source_target_pairs={{0,28},{1,29},{2,30},{3,31},{4,0},{5,1},{6,2},{7,3},{8,4},{9,5},{1... | collective-permute-start | bytes 786440 | tf_op jit(solution)/shard_map/ppermute | solution.py:424
  104.4 2.5 %collective-permute-start.28 = (f32[4,128,128]{2,1,0:T(8,128)S(1)}, f32[4,128,128]{2,1,0:T(8,128)}, u32[]{:S(2)}, u32[]{:S(2)}) collective-permute-start(f32[4,128,128]{2,1,0:T(8,128)S(1)} %join.2), channel_id=1, source_target_pairs={{0,8},{1,9},{2,10},{3,11},{4,12},{5,13},{6,14},{7,15},{8,16},{9,17... | collective-permute-start | bytes 786440 | tf_op jit(solution)/shard_map/ppermute | solution.py:424
  106.9 1.8 %collective-permute-start.31 = (f32[4,128,128]{2,1,0:T(8,128)S(1)}, f32[4,128,128]{2,1,0:T(8,128)}, u32[]{:S(2)}, u32[]{:S(2)}) collective-permute-start(f32[4,128,128]{2,1,0:T(8,128)S(1)} %join.3), channel_id=1, source_target_pairs={{0,24},{1,25},{2,26},{3,27},{4,28},{5,29},{6,30},{7,31},{8,0},{9,1... | collective-permute-start | bytes 786440 | tf_op jit(solution)/shard_map/ppermute | solution.py:424
  108.9 3.8 %collective-permute-done.25 = f32[4,128,128]{2,1,0:T(8,128)S(1)} collective-permute-done((f32[4,128,128]{2,1,0:T(8,128)S(1)}, f32[4,128,128]{2,1,0:T(8,128)S(1)}, u32[]{:S(2)}, u32[]{:S(2)}) %collective-permute-start.25) | collective-permute-done | bytes 262176 | tf_op jit(solution)/shard_map/ppermute | solution.py:424
  113.7 6.7 %collective-permute-done.24 = f32[4,128,128]{2,1,0:T(8,128)S(1)} collective-permute-done((f32[4,128,128]{2,1,0:T(8,128)S(1)}, f32[4,128,128]{2,1,0:T(8,128)S(1)}, u32[]{:S(2)}, u32[]{:S(2)}) %collective-permute-start.24) | collective-permute-done | bytes 262176 | tf_op jit(solution)/shard_map/ppermute | solution.py:424
  120.9 1.5 %collective-permute-done.31 = f32[4,128,128]{2,1,0:T(8,128)} collective-permute-done((f32[4,128,128]{2,1,0:T(8,128)S(1)}, f32[4,128,128]{2,1,0:T(8,128)}, u32[]{:S(2)}, u32[]{:S(2)}) %collective-permute-start.31) | collective-permute-done | bytes 262176 | tf_op jit(solution)/shard_map/ppermute | solution.py:424
  122.4 1.9 %add_multiply_fusion = f32[4,128,128]{2,1,0:T(8,128)} fusion(f32[4,128,128]{2,1,0:T(8,128)} %collective-permute-done.28, f32[4,128,128]{2,1,0:T(8,128)} %collective-permute-done.31, f32[4,128,128]{2,1,0:T(8,128)S(1)} %collective-permute-done.25, f32[4,128,128]{2,1,0:T(8,128)S(1)} %get-tuple-element.37.token, f32[4,128,128]{2,1,0:T(8,128)S(1)} %collective-permute-done.24, ...), kind=kLoop, calls=%fused_computation | loop fusion | flops 327680 | bytes 1835012 | tf_op jit(solution)/shard_map/mul | solution.py:467
  (55 shorter events, 13.2 us)
Async XLA Ops:
  0.7 6.8 %collective-permute-start.7 = (f32[2,128,128]{2,1,0:T(8,128)}, f32[2,128,128]{2,1,0:T(8,128)S(1)}, u32[]{:S(2)}, u32[]{:S(2)}) collective-permute-start(f32[2,128,128]{2,1,0:T(8,128)} %refs_0_.4), channel_id=1, source_target_pairs={{0,1},{1,2},{2,3},{3,0},{4,5},{5,6},{6,7},{7,4},{8,9},{9,10},{10,1... | collective-permute-start | bytes 393224 | tf_op jit(solution)/shard_map/ppermute | solution.py:424
  2.3 9.1 %collective-permute-start.8 = (f32[2,128,128]{2,1,0:T(8,128)}, f32[2,128,128]{2,1,0:T(8,128)S(1)}, u32[]{:S(2)}, u32[]{:S(2)}) collective-permute-start(f32[2,128,128]{2,1,0:T(8,128)} %refs_0_.4), channel_id=1, source_target_pairs={{0,2},{1,3},{2,0},{3,1},{4,6},{5,7},{6,4},{7,5},{8,10},{9,11},{10,... | collective-permute-start | bytes 393224 | tf_op jit(solution)/shard_map/ppermute | solution.py:424
  5.2 6.2 %collective-permute-start.9 = (f32[2,128,128]{2,1,0:T(8,128)}, f32[2,128,128]{2,1,0:T(8,128)S(1)}, u32[]{:S(2)}, u32[]{:S(2)}) collective-permute-start(f32[2,128,128]{2,1,0:T(8,128)} %refs_0_.4), channel_id=1, source_target_pairs={{0,3},{1,0},{2,1},{3,2},{4,7},{5,4},{6,5},{7,6},{8,11},{9,8},{10,9... | collective-permute-start | bytes 393224 | tf_op jit(solution)/shard_map/ppermute | solution.py:424
  11.5 16.2 %collective-permute-start.11 = (f32[3,2,128,128]{3,2,1,0:T(8,128)S(1)}, f32[3,2,128,128]{3,2,1,0:T(8,128)S(1)}, u32[]{:S(2)}, u32[]{:S(2)}) collective-permute-start(f32[3,2,128,128]{3,2,1,0:T(8,128)S(1)} %pack.1.refs_3_), channel_id=1, source_target_pairs={{0,64},{32,96},{64,128},{96,160},{128,192},{160,224},{192,0},{224,... | collective-permute-start | bytes 1179656 | tf_op jit(solution)/shard_map/ppermute | solution.py:420
  13.1 4.0 %collective-permute-start = (f32[2,128,128]{2,1,0:T(8,128)}, f32[2,128,128]{2,1,0:T(8,128)S(1)}, u32[]{:S(2)}, u32[]{:S(2)}) collective-permute-start(f32[2,128,128]{2,1,0:T(8,128)} %refs_0_.4), channel_id=1, source_target_pairs={{0,32},{32,0},{64,96},{96,64},{128,160},{160,128},{192,224},{224,1... | collective-permute-start | bytes 393224 | tf_op jit(solution)/shard_map/ppermute | solution.py:420
  13.1 13.3 %collective-permute-start.1 = (f32[2,128,128]{2,1,0:T(8,128)}, f32[2,128,128]{2,1,0:T(8,128)S(1)}, u32[]{:S(2)}, u32[]{:S(2)}) collective-permute-start(f32[2,128,128]{2,1,0:T(8,128)} %refs_0_.4), channel_id=1, source_target_pairs={{0,64},{32,96},{64,128},{96,160},{128,192},{160,224},{192,0},{224,... | collective-permute-start | bytes 393224 | tf_op jit(solution)/shard_map/ppermute | solution.py:420
  14.3 12.9 %collective-permute-start.3 = (f32[2,128,128]{2,1,0:T(8,128)}, f32[2,128,128]{2,1,0:T(8,128)S(1)}, u32[]{:S(2)}, u32[]{:S(2)}) collective-permute-start(f32[2,128,128]{2,1,0:T(8,128)} %refs_0_.4), channel_id=1, source_target_pairs={{0,128},{32,160},{64,192},{96,224},{128,0},{160,32},{192,64},{224,... | collective-permute-start | bytes 393224 | tf_op jit(solution)/shard_map/ppermute | solution.py:420
  15.7 11.5 %collective-permute-start.5 = (f32[2,128,128]{2,1,0:T(8,128)}, f32[2,128,128]{2,1,0:T(8,128)S(1)}, u32[]{:S(2)}, u32[]{:S(2)}) collective-permute-start(f32[2,128,128]{2,1,0:T(8,128)} %refs_0_.4), channel_id=1, source_target_pairs={{0,192},{32,224},{64,0},{96,32},{128,64},{160,96},{192,128},{224,1... | collective-permute-start | bytes 393224 | tf_op jit(solution)/shard_map/ppermute | solution.py:420
  17.0 16.7 %collective-permute-start.13 = (f32[3,2,128,128]{3,2,1,0:T(8,128)S(1)}, f32[3,2,128,128]{3,2,1,0:T(8,128)S(1)}, u32[]{:S(2)}, u32[]{:S(2)}) collective-permute-start(f32[3,2,128,128]{3,2,1,0:T(8,128)S(1)} %pack.1.refs_3_), channel_id=1, source_target_pairs={{0,128},{32,160},{64,192},{96,224},{128,0},{160,32},{192,64},{224,... | collective-permute-start | bytes 1179656 | tf_op jit(solution)/shard_map/ppermute | solution.py:420
  26.4 14.9 %collective-permute-start.15 = (f32[3,2,128,128]{3,2,1,0:T(8,128)S(1)}, f32[3,2,128,128]{3,2,1,0:T(8,128)S(1)}, u32[]{:S(2)}, u32[]{:S(2)}) collective-permute-start(f32[3,2,128,128]{3,2,1,0:T(8,128)S(1)} %pack.1.refs_3_), channel_id=1, source_target_pairs={{0,192},{32,224},{64,0},{96,32},{128,64},{160,96},{192,128},{224,1... | collective-permute-start | bytes 1179656 | tf_op jit(solution)/shard_map/ppermute | solution.py:420
  27.1 1.3 %collective-permute-start.2 = (f32[2,128,128]{2,1,0:T(8,128)S(1)}, f32[2,128,128]{2,1,0:T(8,128)S(1)}, u32[]{:S(2)}, u32[]{:S(2)}) collective-permute-start(f32[2,128,128]{2,1,0:T(8,128)S(1)} %collective-permute-done.1.refs_2_), channel_id=1, source_target_pairs={{0,32},{32,0},{64,96},{96,64},{128,160},{160,128},{192,224},{224,1... | collective-permute-start | bytes 393224 | tf_op jit(solution)/shard_map/ppermute | solution.py:420
  27.1 30.4 %collective-permute-start.10 = (f32[3,2,128,128]{3,2,1,0:T(8,128)S(1)}, f32[3,2,128,128]{3,2,1,0:T(8,128)S(1)}, u32[]{:S(2)}, u32[]{:S(2)}) collective-permute-start(f32[3,2,128,128]{3,2,1,0:T(8,128)S(1)} %pack.1.refs_3_), channel_id=1, source_target_pairs={{0,32},{32,0},{64,96},{96,64},{128,160},{160,128},{192,224},{224,1... | collective-permute-start | bytes 1179656 | tf_op jit(solution)/shard_map/ppermute | solution.py:420
  27.6 32.3 %collective-permute-start.12 = (f32[3,2,128,128]{3,2,1,0:T(8,128)S(1)}, f32[3,2,128,128]{3,2,1,0:T(8,128)S(1)}, u32[]{:S(2)}, u32[]{:S(2)}) collective-permute-start(f32[3,2,128,128]{3,2,1,0:T(8,128)S(1)} %collective-permute-done.11.refs_5_), channel_id=1, source_target_pairs={{0,32},{32,0},{64,96},{96,64},{128,160},{160,128},{192,224},{224,1... | collective-permute-start | bytes 1179656 | tf_op jit(solution)/shard_map/ppermute | solution.py:420
  28.5 1.3 %collective-permute-start.4 = (f32[2,128,128]{2,1,0:T(8,128)S(1)}, f32[2,128,128]{2,1,0:T(8,128)S(1)}, u32[]{:S(2)}, u32[]{:S(2)}) collective-permute-start(f32[2,128,128]{2,1,0:T(8,128)S(1)} %collective-permute-done.3.refs_4_), channel_id=1, source_target_pairs={{0,32},{32,0},{64,96},{96,64},{128,160},{160,128},{192,224},{224,1... | collective-permute-start | bytes 393224 | tf_op jit(solution)/shard_map/ppermute | solution.py:420
  29.8 20.7 %collective-permute-start.6 = (f32[2,128,128]{2,1,0:T(8,128)S(1)}, f32[2,128,128]{2,1,0:T(8,128)S(1)}, u32[]{:S(2)}, u32[]{:S(2)}) collective-permute-start(f32[2,128,128]{2,1,0:T(8,128)S(1)} %collective-permute-done.5.refs_6_), channel_id=1, source_target_pairs={{0,32},{32,0},{64,96},{96,64},{128,160},{160,128},{192,224},{224,1... | collective-permute-start | bytes 393224 | tf_op jit(solution)/shard_map/ppermute | solution.py:420
  33.7 27.5 %collective-permute-start.14 = (f32[3,2,128,128]{3,2,1,0:T(8,128)S(1)}, f32[3,2,128,128]{3,2,1,0:T(8,128)S(1)}, u32[]{:S(2)}, u32[]{:S(2)}) collective-permute-start(f32[3,2,128,128]{3,2,1,0:T(8,128)S(1)} %collective-permute-done.13.refs_7_), channel_id=1, source_target_pairs={{0,32},{32,0},{64,96},{96,64},{128,160},{160,128},{192,224},{224,1... | collective-permute-start | bytes 1179656 | tf_op jit(solution)/shard_map/ppermute | solution.py:420
  41.2 20.0 %collective-permute-start.16 = (f32[3,2,128,128]{3,2,1,0:T(8,128)S(1)}, f32[3,2,128,128]{3,2,1,0:T(8,128)S(1)}, u32[]{:S(2)}, u32[]{:S(2)}) collective-permute-start(f32[3,2,128,128]{3,2,1,0:T(8,128)S(1)} %collective-permute-done.15.refs_9_), channel_id=1, source_target_pairs={{0,32},{32,0},{64,96},{96,64},{128,160},{160,128},{192,224},{224,1... | collective-permute-start | bytes 1179656 | tf_op jit(solution)/shard_map/ppermute | solution.py:420
  56.2 10.6 %collective-permute-start.17 = (f32[4,136,128]{2,1,0:T(8,128)S(1)}, f32[4,136,128]{2,1,0:T(8,128)S(1)}, u32[]{:S(2)}, u32[]{:S(2)}) collective-permute-start(f32[4,136,128]{2,1,0:T(8,128)S(1)} %get-tuple-element.29.refs_6_.fx), channel_id=1, source_target_pairs={{0,1},{1,2},{2,3},{3,0},{4,5},{5,6},{6,7},{7,4},{8,9},{9,10},{10,1... | collective-permute-start | bytes 835592 | tf_op jit(solution)/shard_map/ppermute | solution.py:424
  57.5 15.7 %collective-permute-start.18 = (f32[4,136,128]{2,1,0:T(8,128)S(1)}, f32[4,136,128]{2,1,0:T(8,128)S(1)}, u32[]{:S(2)}, u32[]{:S(2)}) collective-permute-start(f32[4,136,128]{2,1,0:T(8,128)S(1)} %get-tuple-element.29.refs_6_.fx), channel_id=1, source_target_pairs={{0,2},{1,3},{2,0},{3,1},{4,6},{5,7},{6,4},{7,5},{8,10},{9,11},{10,... | collective-permute-start | bytes 835592 | tf_op jit(solution)/shard_map/ppermute | solution.py:424
  59.9 13.5 %collective-permute-start.19 = (f32[4,136,128]{2,1,0:T(8,128)S(1)}, f32[4,136,128]{2,1,0:T(8,128)S(1)}, u32[]{:S(2)}, u32[]{:S(2)}) collective-permute-start(f32[4,136,128]{2,1,0:T(8,128)S(1)} %get-tuple-element.29.refs_6_.fx), channel_id=1, source_target_pairs={{0,3},{1,0},{2,1},{3,2},{4,7},{5,4},{6,5},{7,6},{8,11},{9,8},{10,9... | collective-permute-start | bytes 835592 | tf_op jit(solution)/shard_map/ppermute | solution.py:424
  83.6 25.1 %collective-permute-start.20 = (f32[8,128,128]{2,1,0:T(8,128)S(1)}, f32[8,128,128]{2,1,0:T(8,128)S(1)}, u32[]{:S(2)}, u32[]{:S(2)}) collective-permute-start(f32[8,128,128]{2,1,0:T(8,128)S(1)} %get-tuple-element.39.token), channel_id=1, source_target_pairs={{0,32},{32,0},{64,96},{96,64},{128,160},{160,128},{192,224},{224,1... | collective-permute-start | bytes 1572872 | tf_op jit(solution)/shard_map/ppermute | solution.py:420
  83.7 20.6 %collective-permute-start.26 = (f32[4,128,128]{2,1,0:T(8,128)S(1)}, f32[4,128,128]{2,1,0:T(8,128)S(1)}, u32[]{:S(2)}, u32[]{:S(2)}) collective-permute-start(f32[4,128,128]{2,1,0:T(8,128)S(1)} %get-tuple-element.45), channel_id=1, source_target_pairs={{0,4},{1,5},{2,6},{3,7},{4,8},{5,9},{6,10},{7,11},{8,12},{9,13},{1... | collective-permute-start | bytes 786440 | tf_op jit(solution)/shard_map/ppermute | solution.py:424
  85.7 21.2 %collective-permute-start.29 = (f32[4,128,128]{2,1,0:T(8,128)S(1)}, f32[4,128,128]{2,1,0:T(8,128)S(1)}, u32[]{:S(2)}, u32[]{:S(2)}) collective-permute-start(f32[4,128,128]{2,1,0:T(8,128)S(1)} %get-tuple-element.35.refs_10_), channel_id=1, source_target_pairs={{0,28},{1,29},{2,30},{3,31},{4,0},{5,1},{6,2},{7,3},{8,4},{9,5},{1... | collective-permute-start | bytes 786440 | tf_op jit(solution)/shard_map/ppermute | solution.py:424
  89.7 11.3 %collective-permute-start.27 = (f32[2,128,128]{2,1,0:T(8,128)S(1)}, f32[2,128,128]{2,1,0:T(8,128)S(1)}, u32[]{:S(2)}, u32[]{:S(2)}) collective-permute-start(f32[2,128,128]{2,1,0:T(8,128)S(1)} %get-tuple-element.46), channel_id=1, source_target_pairs={{0,8},{1,9},{2,10},{3,11},{4,12},{5,13},{6,14},{7,15},{8,16},{9,17... | collective-permute-start | bytes 393224 | tf_op jit(solution)/shard_map/ppermute | solution.py:424
  89.7 14.7 %collective-permute-start.30 = (f32[2,128,128]{2,1,0:T(8,128)S(1)}, f32[2,128,128]{2,1,0:T(8,128)S(1)}, u32[]{:S(2)}, u32[]{:S(2)}) collective-permute-start(f32[2,128,128]{2,1,0:T(8,128)S(1)} %get-tuple-element.48), channel_id=1, source_target_pairs={{0,24},{1,25},{2,26},{3,27},{4,28},{5,29},{6,30},{7,31},{8,0},{9,1... | collective-permute-start | bytes 393224 | tf_op jit(solution)/shard_map/ppermute | solution.py:424
  101.1 11.6 %collective-permute-start.25 = (f32[4,128,128]{2,1,0:T(8,128)S(1)}, f32[4,128,128]{2,1,0:T(8,128)S(1)}, u32[]{:S(2)}, u32[]{:S(2)}) collective-permute-start(f32[4,128,128]{2,1,0:T(8,128)S(1)} %get-tuple-element.36.refs_10_), channel_id=1, source_target_pairs={{0,28},{1,29},{2,30},{3,31},{4,0},{5,1},{6,2},{7,3},{8,4},{9,5},{1... | collective-permute-start | bytes 786440 | tf_op jit(solution)/shard_map/ppermute | solution.py:424
  104.3 16.0 %collective-permute-start.24 = (f32[4,128,128]{2,1,0:T(8,128)S(1)}, f32[4,128,128]{2,1,0:T(8,128)S(1)}, u32[]{:S(2)}, u32[]{:S(2)}) collective-permute-start(f32[4,128,128]{2,1,0:T(8,128)S(1)} %get-tuple-element.43), channel_id=1, source_target_pairs={{0,4},{1,5},{2,6},{3,7},{4,8},{5,9},{6,10},{7,11},{8,12},{9,13},{1... | collective-permute-start | bytes 786440 | tf_op jit(solution)/shard_map/ppermute | solution.py:424
  104.4 16.5 %collective-permute-start.28 = (f32[4,128,128]{2,1,0:T(8,128)S(1)}, f32[4,128,128]{2,1,0:T(8,128)}, u32[]{:S(2)}, u32[]{:S(2)}) collective-permute-start(f32[4,128,128]{2,1,0:T(8,128)S(1)} %join.2), channel_id=1, source_target_pairs={{0,8},{1,9},{2,10},{3,11},{4,12},{5,13},{6,14},{7,15},{8,16},{9,17... | collective-permute-start | bytes 786440 | tf_op jit(solution)/shard_map/ppermute | solution.py:424
  106.9 15.5 %collective-permute-start.31 = (f32[4,128,128]{2,1,0:T(8,128)S(1)}, f32[4,128,128]{2,1,0:T(8,128)}, u32[]{:S(2)}, u32[]{:S(2)}) collective-permute-start(f32[4,128,128]{2,1,0:T(8,128)S(1)} %join.3), channel_id=1, source_target_pairs={{0,24},{1,25},{2,26},{3,27},{4,28},{5,29},{6,30},{7,31},{8,0},{9,1... | collective-permute-start | bytes 786440 | tf_op jit(solution)/shard_map/ppermute | solution.py:424
  108.8 15.6 %collective-permute-start.23 = (f32[2,128,128]{2,1,0:T(8,128)S(1)}, f32[2,128,128]{2,1,0:T(8,128)S(1)}, u32[]{:S(2)}, u32[]{:S(2)}) collective-permute-start(f32[2,128,128]{2,1,0:T(8,128)S(1)} %get-tuple-element.50), channel_id=1, source_target_pairs={{0,192},{32,224},{64,0},{96,32},{128,64},{160,96},{192,128},{224,1... | collective-permute-start | bytes 393224 | tf_op jit(solution)/shard_map/ppermute | solution.py:420
  112.7 11.6 %collective-permute-start.22 = (f32[2,128,128]{2,1,0:T(8,128)S(1)}, f32[2,128,128]{2,1,0:T(8,128)S(1)}, u32[]{:S(2)}, u32[]{:S(2)}) collective-permute-start(f32[2,128,128]{2,1,0:T(8,128)S(1)} %get-tuple-element.51), channel_id=1, source_target_pairs={{0,128},{32,160},{64,192},{96,224},{128,0},{160,32},{192,64},{224,... | collective-permute-start | bytes 393224 | tf_op jit(solution)/shard_map/ppermute | solution.py:420
  120.3 5.0 %collective-permute-start.21 = (f32[2,128,128]{2,1,0:T(8,128)S(1)}, f32[2,128,128]{2,1,0:T(8,128)S(1)}, u32[]{:S(2)}, u32[]{:S(2)}) collective-permute-start(f32[2,128,128]{2,1,0:T(8,128)S(1)} %get-tuple-element.49), channel_id=1, source_target_pairs={{0,64},{32,96},{64,128},{96,160},{128,192},{160,224},{192,0},{224,... | collective-permute-start | bytes 393224 | tf_op jit(solution)/shard_map/ppermute | solution.py:420
  (5 other events, 151.1 us)
where the time goes:
time: 127 us; the launch traced here: 126 us
  waiting for transfers between devices  56.6 us (45%)
  starting transfers between devices  38.6 us (30%)
  Pallas kernels  25.3 us (20%)
  other arithmetic  2.62 us (2%)
  between operations  1.47 us (1%)
  local copies, waits for them, and re-layouts  1.32 us (1%)
    ppermute x14, waiting for transfers between devices, shift(): return lax.ppermute(a, 'batch', [(b, to(b)) for b in range(batch)])  34.2 us
    ppermute x14, starting transfers between devices, shift(): return lax.ppermute(a, 'batch', [(b, to(b)) for b in range(batch)])  28.6 us
    ppermute x18, waiting for transfers between devices, move(): return lax.ppermute(a, 'nodes', [(n, to(n)) for n in range(nodes)])  22.4 us
    ppermute x18, starting transfers between devices, move(): return lax.ppermute(a, 'nodes', [(n, to(n)) for n in range(nodes)])  10 us
    pallas_call x1, Pallas kernels, fold(): pl.pallas_call(fold_kernel, out_shape=(jax.ShapeDtypeStruct((qd, pg, g, g...  7.32 us
    pallas_call x3, Pallas kernels, edges(): pl.pallas_call(kernel, out_shape=[jax.ShapeDtypeStruct((n, g, g), f32) fo...  6.13 us
    pallas_call x1, Pallas kernels, forward(): pl.pallas_call(functools.partial(forward_kernel, nodes), out_shape=(jax.S...  5.63 us
    pallas_call x1, Pallas kernels, backward(): pl.pallas_call(functools.partial(backward_kernel, nodes), out_shape=[jax....  3.99 us
  transfers between devices with their start and end apart: 32, of which 15 were waited for; matrix products, arithmetic and copies ran while one was open for 2% of the time, Pallas kernels for 12%

commit v1 on v0

--- a/solution.py
+++ b/solution.py
@@ -252,14 +252,18 @@
 
 
 def pack_kernel(*refs):
-    for t, a in enumerate(refs[:-1]):
-        refs[-1][t] = a[...]
+    at = 0
+    for a in refs[:-1]:
+        n = a.shape[0]
+        refs[-1][at : at + n] = a[...]
+        at += n
 
 
 def pack(arrays):
+    n = sum(a.shape[0] for a in arrays)
     return pl.pallas_call(
         pack_kernel,
-        out_shape=jax.ShapeDtypeStruct((len(arrays),) + arrays[0].shape, f32),
+        out_shape=jax.ShapeDtypeStruct((n,) + arrays[0].shape[1:], f32),
         in_specs=vmem_specs(len(arrays)),
         out_specs=vmem_specs(1)[0],
         compiler_params=pltpu.CompilerParams(vmem_limit_bytes=4 << 20),
@@ -272,12 +276,13 @@
     pieces, (ehl, pk) = refs[: len(offsets)], refs[len(offsets) : -1]
     lv = refs[-1]
     pg, g, s = e_own.shape
-    sets, each = pieces[0].shape[:2]
+    sets = lv.shape[0]
+    each = pieces[0].shape[0] // sets
     nodes = lv.shape[1] // each
     for (dx, dc), piece in zip(offsets, pieces):
         src = node_at(-dx, -dc, nodes)
         for t in range(sets):
-            lv[t, pl.ds(src * each, each)] = piece[t]
+            lv[t, pl.ds(src * each, each)] = piece[t * each : (t + 1) * each]
 
     def product(p, carry):
         hi, lo = parts(e_own[p])
@@ -300,7 +305,8 @@
 
 def spread(prod_child, e, pk, pieces, offsets, nodes):
     pg, g, s = e.shape
-    sets, each = pieces[0].shape[:2]
+    sets = ROWS - 1
+    each = pieces[0].shape[0] // sets
 
     def kernel(*refs):
         spread_kernel(offsets, *refs)
@@ -385,22 +391,22 @@
     )(child, parent, count, ehl, pk, bias, *fxs, token)
 
 
-def join_kernel(at, a_ref, b_ref, c_ref, token, out):
-    n = c_ref.shape[0]
-    out[...] = a_ref[...] + b_ref[...]
-    out[at : at + n] += c_ref[...]
-
-
-def join(a, b, c, token, at):
-    return pl.pallas_call(
-        functools.partial(join_kernel, at),
-        out_shape=jax.ShapeDtypeStruct(a.shape, f32),
-        in_specs=vmem_specs(3) + [pl.BlockSpec(memory_space=pl.ANY)],
-        out_specs=vmem_specs(1)[0],
+def join_kernel(ap, am, bp, bm, c_ref, outp, outm):
+    first = (lax.axis_index("nodes") % CORES == 0).astype(f32)
+    outp[...] = (ap[...] + bp[...]) + c_ref[...] * first
+    outm[...] = (am[...] + bm[...]) + c_ref[...] * (1.0 - first)
+
+
+def join(ap, am, bp, bm, c):
+    return pl.pallas_call(
+        join_kernel,
+        out_shape=[jax.ShapeDtypeStruct(ap.shape, f32)] * 2,
+        in_specs=vmem_specs(5),
+        out_specs=vmem_specs(2),
         compiler_params=pltpu.CompilerParams(vmem_limit_bytes=4 << 20),
-        cost_estimate=pl.CostEstimate(flops=200_000, bytes_accessed=1 << 20, transcendentals=0),
+        cost_estimate=pl.CostEstimate(flops=400_000, bytes_accessed=2 << 20, transcendentals=0),
         name="join",
-    )(a, b, c, token)
+    )(ap, am, bp, bm, c)
 
 
 def body(leaves, prod_child, block_weight, block_child, block_parent, block_count, upper_flow):
@@ -412,16 +418,26 @@
     pg = prod_child.shape[1]
     qd = upper_flow.shape[0]
     keep = block_weight.shape[0] // batch
-    half = keep // 2
     far = depth // 2
 
     def move(a, dx=0, dc=0):
         to = lambda n: ((n // CORES + dx) % chips) * CORES + (n % CORES + dc) % CORES
         return lax.ppermute(a, "nodes", [(n, to(n)) for n in range(nodes)])
 
-    def shift(a, dz=0, dy=0):
-        to = lambda b: ((b // ROWS + dz) % depth) * ROWS + (b % ROWS + dy) % ROWS
+    def shift(a, dz):
+        to = lambda b: ((b // ROWS + dz) % depth) * ROWS + b % ROWS
         return lax.ppermute(a, "batch", [(b, to(b)) for b in range(batch)])
+
+    def swap(a, mask):
+        return lax.ppermute(a, "batch", [(b, b ^ mask) for b in range(batch)])
+
+    def shift_by_core(a, dz):
+        pairs = []
+        for n in range(nodes):
+            for b in range(batch):
+                z = (b // ROWS + (dz if n % CORES == 0 else -dz)) % depth
+                pairs.append((n * batch + b, n * batch + z * ROWS + b % ROWS))
+        return lax.ppermute(a, ("nodes", "batch"), pairs)
 
     def gather(a):
         out = []
@@ -431,35 +447,36 @@
         return out
 
     got = gather(leaves)
-    row = [shift(leaves, dy=t) for t in range(1, ROWS)]
-    packed = pack(row)
+    one = swap(leaves, 1)
+    pair = pack([leaves, one])
+    two = swap(pair, 3)
+    packed = pack([one, two])
     pieces = gather(packed)
 
     w, bias = fold(block_child, block_parent, block_count, block_weight, pg, qd)
     sum_values, fx, e, r, pk = forward(prod_child, got, w, bias, upper_flow)
-    fxs = [fx] + [shift(fx, dy=t) for t in range(1, ROWS)]
+    fxs = [fx] + [swap(fx, t) for t in (1, 3, 2)]
+    *mine, give = backward(prod_child, w, fx, r, e, pk, nodes, ng)
+    given = move(give, 0, 1)
+    k = leaves.shape[0]
+    flows = [a + given[dx * k : (dx + 1) * k] for dx, a in enumerate(mine)]
     ehl, pks = spread(prod_child, e, pk, pieces, hops(nodes), nodes)
 
-    def part(token, *plan):
+    def part(token, *ds):
+        plan = [(d, 0, keep, keep) for d in ds]
         return edges(
             block_child, block_parent, block_count, ehl, pks, bias, fxs, token, plan
         )
 
-    e4p, e4m, e3p, e3m = part(
-        pks, (far, 0, half, keep), (-far, half, half, keep), (3, 0, keep, keep), (-3, 0, keep, keep)
-    )
-    r4p, r4m = shift(e4p, dz=2), shift(e4m, dz=-2)
-    r3p, r3m = shift(e3p, dz=1), shift(e3m, dz=-1)
-    e1p, e1m = part(e3m, (1, 0, keep, keep), (-1, 0, keep, keep))
-    r1p, r1m = shift(e1p, dz=1), shift(e1m, dz=-1)
-    e2p, e2m, e0 = part(e1m, (2, 0, keep, keep), (-2, 0, keep, keep), (0, 0, keep, keep))
-    *mine, give = backward(prod_child, w, fx, r, e, e0, nodes, ng)
-    c2p = join(e2p, r3p, r4p, give, 0)
-    c2m = join(e2m, r3m, r4m, give, half)
-    r2p, r2m = shift(c2p, dz=2), shift(c2m, dz=-2)
-    given = move(give, 0, 1)
-    k = leaves.shape[0]
-    flows = [a + given[dx * k : (dx + 1) * k] for dx, a in enumerate(mine)]
+    (e4,) = part(pks, far)
+    r4 = shift_by_core(e4, 2)
+    e3p, e3m = part(e4, 3, -3)
+    r3p, r3m = shift(e3p, 1), shift(e3m, -1)
+    e1p, e1m, e0 = part(e3m, 1, -1, 0)
+    r1p, r1m = shift(e1p, 1), shift(e1m, -1)
+    e2p, e2m = part(e1m, 2, -2)
+    c2p, c2m = join(e2p, e2m, r3p, r3m, r4)
+    r2p, r2m = shift(c2p, 2), shift(c2m, -2)
     leaf_flow = functools.reduce(
         jnp.add, [flows[0]] + [move(flows[dx], dx) for dx in range(1, chips)]
     )

time: 127 us -> 125 us (0.984)
  the two profiles are of different devices: /device:TPU:2 before, /device:TPU:33 now
where the time goes in v1:
time: 125 us
  starting transfers between devices  47.2 us (38%)
  waiting for transfers between devices  45.7 us (37%)
  Pallas kernels  25.7 us (21%)
  other arithmetic  2.47 us (2%)
  local copies, waits for them, and re-layouts  2.23 us (2%)
  between operations  1.43 us (1%)
    ppermute x18, starting transfers between devices, move(): return lax.ppermute(a, 'nodes', [(n, to(n)) for n in range(nodes)])  23.1 us
    ppermute x5, waiting for transfers between devices, swap(): return lax.ppermute(a, 'batch', [(b, b ^ mask) for b in range(batch)])  18.4 us
    ppermute x6, waiting for transfers between devices, shift(): return lax.ppermute(a, 'batch', [(b, to(b)) for b in range(batch)])  16.9 us
    ppermute x6, starting transfers between devices, shift(): return lax.ppermute(a, 'batch', [(b, to(b)) for b in range(batch)])  12.4 us
    ppermute x18, waiting for transfers between devices, move(): return lax.ppermute(a, 'nodes', [(n, to(n)) for n in range(nodes)])  10.3 us
    ppermute x5, starting transfers between devices, swap(): return lax.ppermute(a, 'batch', [(b, b ^ mask) for b in range(batch)])  8.08 us
    pallas_call x1, Pallas kernels, fold(): pl.pallas_call(fold_kernel, out_shape=(jax.ShapeDtypeStruct((qd, pg, g, g...  7.06 us
    pallas_call x4, Pallas kernels, edges(): pl.pallas_call(kernel, out_shape=[jax.ShapeDtypeStruct((n, g, g), f32) fo...  6.74 us
  transfers between devices with their start and end apart: 30, of which 11 were waited for; matrix products, arithmetic and copies ran while one was open for 1% of the time, Pallas kernels for 21%

profile of v1, /device:TPU:33, one launch (start us, length us, event | category | flops | bytes accessed | tf_op | source)
XLA Modules:
  0.0 124.7 jit_solution(18064649798442741127)
XLA Ops:
  0.6 1.4 %collective-permute-start.11 = (f32[2,128,128]{2,1,0:T(8,128)}, f32[2,128,128]{2,1,0:T(8,128)S(1)}, u32[]{:S(2)}, u32[]{:S(2)}) collective-permute-start(f32[2,128,128]{2,1,0:T(8,128)} %refs_0_.7), channel_id=1, source_target_pairs={{0,1},{1,0},{2,3},{3,2},{4,5},{5,4},{6,7},{7,6},{8,9},{9,8},{10,11... | collective-permute-start | bytes 393224 | tf_op jit(solution)/shard_map/ppermute | solution.py:432
  2.0 3.3 %collective-permute-done.11.refs_1_.refs_0_ = f32[2,128,128]{2,1,0:T(8,128)S(1)} collective-permute-done((f32[2,128,128]{2,1,0:T(8,128)}, f32[2,128,128]{2,1,0:T(8,128)S(1)}, u32[]{:S(2)}, u32[]{:S(2)}) %collective-permute-start.11) | collective-permute-done | bytes 131104 | tf_op jit(solution)/shard_map/ppermute | solution.py:432
  6.2 2.8 %collective-permute-start.12 = (f32[4,128,128]{2,1,0:T(8,128)S(1)}, f32[4,128,128]{2,1,0:T(8,128)S(1)}, u32[]{:S(2)}, u32[]{:S(2)}) collective-permute-start(f32[4,128,128]{2,1,0:T(8,128)S(1)} %pack.2), channel_id=1, source_target_pairs={{0,3},{1,2},{2,1},{3,0},{4,7},{5,6},{6,5},{7,4},{8,11},{9,10},{10,... | collective-permute-start | bytes 786440 | tf_op jit(solution)/shard_map/ppermute | solution.py:432
  9.1 4.9 %collective-permute-done.12.refs_1_ = f32[4,128,128]{2,1,0:T(8,128)S(1)} collective-permute-done((f32[4,128,128]{2,1,0:T(8,128)S(1)}, f32[4,128,128]{2,1,0:T(8,128)S(1)}, u32[]{:S(2)}, u32[]{:S(2)}) %collective-permute-start.12) | collective-permute-done | bytes 262176 | tf_op jit(solution)/shard_map/ppermute | solution.py:432
  14.0 1.3 %collective-permute-start.14 = (f32[6,128,128]{2,1,0:T(8,128)S(1)}, f32[6,128,128]{2,1,0:T(8,128)S(1)}, u32[]{:S(2)}, u32[]{:S(2)}) collective-permute-start(f32[6,128,128]{2,1,0:T(8,128)S(1)} %pack.3.refs_3_), channel_id=1, source_target_pairs={{0,64},{32,96},{64,128},{96,160},{128,192},{160,224},{192,0},{224,... | collective-permute-start | bytes 1179656 | tf_op jit(solution)/shard_map/ppermute | solution.py:425
  15.3 2.5 %collective-permute-start.16 = (f32[6,128,128]{2,1,0:T(8,128)S(1)}, f32[6,128,128]{2,1,0:T(8,128)S(1)}, u32[]{:S(2)}, u32[]{:S(2)}) collective-permute-start(f32[6,128,128]{2,1,0:T(8,128)S(1)} %pack.3.refs_3_), channel_id=1, source_target_pairs={{0,128},{32,160},{64,192},{96,224},{128,0},{160,32},{192,64},{224,... | collective-permute-start | bytes 1179656 | tf_op jit(solution)/shard_map/ppermute | solution.py:425
  17.8 2.9 %collective-permute-start = (f32[2,128,128]{2,1,0:T(8,128)S(1)}, f32[2,128,128]{2,1,0:T(8,128)S(1)}, u32[]{:S(2)}, u32[]{:S(2)}) collective-permute-start(f32[2,128,128]{2,1,0:T(8,128)S(1)} %copy-done), channel_id=1, source_target_pairs={{0,32},{32,0},{64,96},{96,64},{128,160},{160,128},{192,224},{224,1... | collective-permute-start | bytes 393224 | tf_op jit(solution)/shard_map/ppermute | solution.py:425
  20.7 2.3 %collective-permute-start.3 = (f32[2,128,128]{2,1,0:T(8,128)S(1)}, f32[2,128,128]{2,1,0:T(8,128)S(1)}, u32[]{:S(2)}, u32[]{:S(2)}) collective-permute-start(f32[2,128,128]{2,1,0:T(8,128)S(1)} %copy-done), channel_id=1, source_target_pairs={{0,128},{32,160},{64,192},{96,224},{128,0},{160,32},{192,64},{224,... | collective-permute-start | bytes 393224 | tf_op jit(solution)/shard_map/ppermute | solution.py:425
  23.3 9.4 %collective-permute-done.1.refs_2_ = f32[2,128,128]{2,1,0:T(8,128)S(1)} collective-permute-done((f32[2,128,128]{2,1,0:T(8,128)S(1)}, f32[2,128,128]{2,1,0:T(8,128)S(1)}, u32[]{:S(2)}, u32[]{:S(2)}) %collective-permute-start.1) | collective-permute-done | bytes 131104 | tf_op jit(solution)/shard_map/ppermute | solution.py:425
  32.7 6.7 %collective-permute-start.2 = (f32[2,128,128]{2,1,0:T(8,128)S(1)}, f32[2,128,128]{2,1,0:T(8,128)S(1)}, u32[]{:S(2)}, u32[]{:S(2)}) collective-permute-start(f32[2,128,128]{2,1,0:T(8,128)S(1)} %collective-permute-done.1.refs_2_), channel_id=1, source_target_pairs={{0,32},{32,0},{64,96},{96,64},{128,160},{160,128},{192,224},{224,1... | collective-permute-start | bytes 393224 | tf_op jit(solution)/shard_map/ppermute | solution.py:425
  39.5 2.4 %collective-permute-start.4 = (f32[2,128,128]{2,1,0:T(8,128)S(1)}, f32[2,128,128]{2,1,0:T(8,128)S(1)}, u32[]{:S(2)}, u32[]{:S(2)}) collective-permute-start(f32[2,128,128]{2,1,0:T(8,128)S(1)} %collective-permute-done.3.refs_4_), channel_id=1, source_target_pairs={{0,32},{32,0},{64,96},{96,64},{128,160},{160,128},{192,224},{224,1... | collective-permute-start | bytes 393224 | tf_op jit(solution)/shard_map/ppermute | solution.py:425
  45.8 7.1 %fold.1 = (f32[4,16,128,128]{3,2,1,0:T(8,128)S(1)}, f32[64,128]{1,0:T(8,128)S(1)}) custom-call(s32[1,128]{1,0:T(1,128)S(1)} %copy-done.3, s32[1,128]{1,0:T(1,128)S(1)} %copy-done.5, s32[1]{0:T(128)S(6)} %copy.10.count.refs_2_, f32[128,128,128]{2,1,0:T(8,128)} %w_ref.1), custom_call_target="tpu_custom_call" | custom-call | flops 20000000 | bytes 16777216 | tf_op jit(solution)/shard_map/fold/pallas_call | solution.py:78
  52.9 5.6 %forward.1 = (f32[4,128,128]{2,1,0:T(8,128)}, f32[4,136,128]{2,1,0:T(8,128)S(1)}, f32[16,128,128]{2,1,0:T(8,128)S(1)}, f32[64,128]{1,0:T(8,128)S(1)}, f32[16,128]{1,0:T(8,128)S(1)}) custom-call(s32[2,16]{1,0:T(2,128)S(1)} %bitcast.1, f32[2,128,128]{2,1,0:T(8,128)S(1)} %copy-done.1, f32[2,128,128]{2,1,0:T(8,128)S(1)} %collective-permute-done.refs_1_, ...), custom_call_target="tpu_custom_call" | custom-call | flops 1073741824 | bytes 8388608 | tf_op jit(solution)/shard_map/forward/pallas_call | solution.py:150
  58.5 4.0 %backward.1 = (f32[2,128,128]{2,1,0:T(8,128)S(1)}, f32[2,128,128]{2,1,0:T(8,128)S(1)}, f32[2,128,128]{2,1,0:T(8,128)S(1)}, f32[2,128,128]{2,1,0:T(8,128)S(1)}, f32[8,128,128]{2,1,0:T(8,128)S(1)}) custom-call(s32[2,16]{1,0:T(2,128)S(1)} %bitcast.2, f32[4,16,128,128]{3,2,1,0:T(8,128)S(1)} %get-tuple-element.26.refs_8_.w_ref, ...), custom_call_target="tpu_custom_call" | custom-call | flops 1073741824 | bytes 8388608 | tf_op jit(solution)/shard_map/backward/pallas_call | solution.py:225
  63.1 2.7 %collective-permute-start.21 = (f32[4,136,128]{2,1,0:T(8,128)S(1)}, f32[4,136,128]{2,1,0:T(8,128)S(1)}, u32[]{:S(2)}, u32[]{:S(2)}) collective-permute-start(f32[4,136,128]{2,1,0:T(8,128)S(1)} %get-tuple-element.29.fx.refs_6_), channel_id=1, source_target_pairs={{0,3},{1,2},{2,1},{3,0},{4,7},{5,6},{6,5},{7,4},{8,11},{9,10},{10,... | collective-permute-start | bytes 835592 | tf_op jit(solution)/shard_map/ppermute | solution.py:432
  67.0 2.1 %spread.1 = (bf16[16,256,512]{2,1,0:T(8,128)(2,1)S(1)}, f32[4,16,128]{2,1,0:T(8,128)S(1)}) custom-call(s32[2,16]{1,0:T(2,128)S(1)} %bitcast.3, f32[16,128,128]{2,1,0:T(8,128)S(1)} %get-tuple-element.31.e_ref.refs_1_, f32[16,128]{1,0:T(8,128)S(1)} %get-tuple-element.32.token.refs_2_, f32[6,128,128]{2,1,0:T(8,128)S(1)} %pack.3.refs_3_, ...), custom_call_target="tpu_custom_call" | custom-call | flops 10000000 | bytes 10485760 | tf_op jit(solution)/shard_map/spread/pallas_call | solution.py:314
  69.1 1.9 %collective-permute-done.20.refs_7_ = f32[4,136,128]{2,1,0:T(8,128)S(1)} collective-permute-done((f32[4,136,128]{2,1,0:T(8,128)S(1)}, f32[4,136,128]{2,1,0:T(8,128)S(1)}, u32[]{:S(2)}, u32[]{:S(2)}) %collective-permute-start.20) | collective-permute-done | bytes 278560 | tf_op jit(solution)/shard_map/ppermute | solution.py:432
  71.0 6.3 %collective-permute-done.21.refs_8_ = f32[4,136,128]{2,1,0:T(8,128)S(1)} collective-permute-done((f32[4,136,128]{2,1,0:T(8,128)S(1)}, f32[4,136,128]{2,1,0:T(8,128)S(1)}, u32[]{:S(2)}, u32[]{:S(2)}) %collective-permute-start.21) | collective-permute-done | bytes 278560 | tf_op jit(solution)/shard_map/ppermute | solution.py:432
  77.3 2.0 %collective-permute-done.22.refs_9_ = f32[4,136,128]{2,1,0:T(8,128)S(1)} collective-permute-done((f32[4,136,128]{2,1,0:T(8,128)S(1)}, f32[4,136,128]{2,1,0:T(8,128)S(1)}, u32[]{:S(2)}, u32[]{:S(2)}) %collective-permute-start.22) | collective-permute-done | bytes 278560 | tf_op jit(solution)/shard_map/ppermute | solution.py:432
  80.4 1.8 %edges.5 = (f32[4,128,128]{2,1,0:T(8,128)S(1)}, f32[4,128,128]{2,1,0:T(8,128)S(1)}) custom-call(s32[1,128]{1,0:T(1,128)S(1)} %copy-done.4, s32[1,128]{1,0:T(1,128)S(1)} %copy-done.6, s32[1]{0:T(128)S(6)} %copy.10.count.refs_2_, bf16[16,256,512]{2,1,0:T(8,128)(2,1)S(1)} %get-tuple-element.38.refs_3_, f32[4,16,128]{2,1,0:T(8,128)S(1)} %get-tuple-element.39.refs_4_.refs_10_, ...), custom_call_target="tpu_custom_call" | custom-call | flops 536870912 | bytes 6291456 | tf_op jit(solution)/shard_map/edges/pallas_call | solution.py:375
  82.2 1.7 %collective-permute-start.25 = (f32[4,128,128]{2,1,0:T(8,128)S(1)}, f32[4,128,128]{2,1,0:T(8,128)S(1)}, u32[]{:S(2)}, u32[]{:S(2)}) collective-permute-start(f32[4,128,128]{2,1,0:T(8,128)S(1)} %get-tuple-element.46), channel_id=1, source_target_pairs={{0,4},{1,5},{2,6},{3,7},{4,8},{5,9},{6,10},{7,11},{8,12},{9,13},{1... | collective-permute-start | bytes 786440 | tf_op jit(solution)/shard_map/ppermute | solution.py:429
  83.9 3.6 %collective-permute-start.27 = (f32[4,128,128]{2,1,0:T(8,128)S(1)}, f32[4,128,128]{2,1,0:T(8,128)S(1)}, u32[]{:S(2)}, u32[]{:S(2)}) collective-permute-start(f32[4,128,128]{2,1,0:T(8,128)S(1)} %edges.4.refs_10_), channel_id=1, source_target_pairs={{0,8},{1,9},{2,10},{3,11},{4,12},{5,13},{6,14},{7,15},{8,16},{9,17... | collective-permute-start | bytes 786440 | tf_op jit(solution)/shard_map/ppermute | solution.py:440
  87.5 1.4 %collective-permute-start.26 = (f32[4,128,128]{2,1,0:T(8,128)S(1)}, f32[4,128,128]{2,1,0:T(8,128)S(1)}, u32[]{:S(2)}, u32[]{:S(2)}) collective-permute-start(f32[4,128,128]{2,1,0:T(8,128)S(1)} %get-tuple-element.40.refs_10_), channel_id=1, source_target_pairs={{0,28},{1,29},{2,30},{3,31},{4,0},{5,1},{6,2},{7,3},{8,4},{9,5},{1... | collective-permute-start | bytes 786440 | tf_op jit(solution)/shard_map/ppermute | solution.py:429
  89.2 2.8 %collective-permute-start.9 = (f32[2,128,128]{2,1,0:T(8,128)S(1)}, f32[2,128,128]{2,1,0:T(8,128)S(1)}, u32[]{:S(2)}, u32[]{:S(2)}) collective-permute-start(f32[2,128,128]{2,1,0:T(8,128)S(1)} %get-tuple-element.51), channel_id=1, source_target_pairs={{0,128},{32,160},{64,192},{96,224},{128,0},{160,32},{192,64},{224,... | collective-permute-start | bytes 393224 | tf_op jit(solution)/shard_map/ppermute | solution.py:425
  92.0 2.1 %edges.6 = (f32[4,128,128]{2,1,0:T(8,128)S(1)}, f32[4,128,128]{2,1,0:T(8,128)S(1)}, f32[4,128,128]{2,1,0:T(8,128)S(1)}) custom-call(s32[1,128]{1,0:T(1,128)S(1)} %copy-done.4, s32[1,128]{1,0:T(1,128)S(1)} %copy-done.6, s32[1]{0:T(128)S(6)} %copy.10.count.refs_2_, bf16[16,256,512]{2,1,0:T(8,128)(2,1)S(1)} %get-tuple-element.38.refs_3_, ...), custom_call_target="tpu_custom_call" | custom-call | flops 805306368 | bytes 6291456 | tf_op jit(solution)/shard_map/edges/pallas_call | solution.py:375
  94.2 1.8 %edges.7 = (f32[4,128,128]{2,1,0:T(8,128)S(1)}, f32[4,128,128]{2,1,0:T(8,128)S(1)}) custom-call(s32[1,128]{1,0:T(1,128)S(1)} %copy-done.4, s32[1,128]{1,0:T(1,128)S(1)} %copy-done.6, s32[1]{0:T(128)S(6)} %copy.10.count.refs_2_, bf16[16,256,512]{2,1,0:T(8,128)(2,1)S(1)} %get-tuple-element.38.refs_3_, f32[4,16,128]{2,1,0:T(8,128)S(1)} %get-tuple-element.39.refs_4_.refs_10_, ...), custom_call_target="tpu_custom_call" | custom-call | flops 536870912 | bytes 6291456 | tf_op jit(solution)/shard_map/edges/pallas_call | solution.py:375
  97.0 3.6 %collective-permute-start.24 = (f32[4,128,128]{2,1,0:T(8,128)S(1)}, f32[4,128,128]{2,1,0:T(8,128)S(1)}, u32[]{:S(2)}, u32[]{:S(2)}) collective-permute-start(f32[4,128,128]{2,1,0:T(8,128)S(1)} %get-tuple-element.43.refs_10_), channel_id=1, source_target_pairs={{0,28},{1,29},{2,30},{3,31},{4,0},{5,1},{6,2},{7,3},{8,4},{9,5},{1... | collective-permute-start | bytes 786440 | tf_op jit(solution)/shard_map/ppermute | solution.py:429
  101.0 3.0 %collective-permute-start.28 = (f32[4,128,128]{2,1,0:T(8,128)S(1)}, f32[4,128,128]{2,1,0:T(8,128)S(1)}, u32[]{:S(2)}, u32[]{:S(2)}) collective-permute-start(f32[4,128,128]{2,1,0:T(8,128)S(1)} %get-tuple-element.47), channel_id=1, source_target_pairs={{0,8},{1,9},{2,10},{3,11},{4,12},{5,13},{6,14},{7,15},{8,16},{9,17... | collective-permute-start | bytes 786440 | tf_op jit(solution)/shard_map/ppermute | solution.py:429
  104.0 2.4 %collective-permute-start.29 = (f32[4,128,128]{2,1,0:T(8,128)S(1)}, f32[4,128,128]{2,1,0:T(8,128)S(1)}, u32[]{:S(2)}, u32[]{:S(2)}) collective-permute-start(f32[4,128,128]{2,1,0:T(8,128)S(1)} %get-tuple-element.48), channel_id=1, source_target_pairs={{0,24},{1,25},{2,26},{3,27},{4,28},{5,29},{6,30},{7,31},{8,0},{9,1... | collective-permute-start | bytes 786440 | tf_op jit(solution)/shard_map/ppermute | solution.py:429
  107.6 2.7 %collective-permute-done.23 = f32[4,128,128]{2,1,0:T(8,128)S(1)} collective-permute-done((f32[4,128,128]{2,1,0:T(8,128)S(1)}, f32[4,128,128]{2,1,0:T(8,128)S(1)}, u32[]{:S(2)}, u32[]{:S(2)}) %collective-permute-start.23) | collective-permute-done | bytes 262176 | tf_op jit(solution)/shard_map/ppermute | solution.py:429
  110.3 12.6 %collective-permute-done.28 = f32[4,128,128]{2,1,0:T(8,128)S(1)} collective-permute-done((f32[4,128,128]{2,1,0:T(8,128)S(1)}, f32[4,128,128]{2,1,0:T(8,128)S(1)}, u32[]{:S(2)}, u32[]{:S(2)}) %collective-permute-start.28) | collective-permute-done | bytes 262176 | tf_op jit(solution)/shard_map/ppermute | solution.py:429
  123.0 1.7 %add_multiply_fusion = f32[4,128,128]{2,1,0:T(8,128)} fusion(f32[4,128,128]{2,1,0:T(8,128)S(1)} %collective-permute-done.28, f32[4,128,128]{2,1,0:T(8,128)S(1)} %collective-permute-done.29, f32[4,128,128]{2,1,0:T(8,128)S(1)} %collective-permute-done.24, f32[4,128,128]{2,1,0:T(8,128)S(1)} %get-tuple-element.41, f32[4,128,128]{2,1,0:T(8,128)S(1)} %collective-permute-done.23, ...), kind=kLoop, calls=%fused_computation | loop fusion | flops 327680 | bytes 1835012 | tf_op jit(solution)/shard_map/mul | solution.py:484
  (58 shorter events, 10.3 us)
Async XLA Ops:
  0.6 4.7 %collective-permute-start.11 = (f32[2,128,128]{2,1,0:T(8,128)}, f32[2,128,128]{2,1,0:T(8,128)S(1)}, u32[]{:S(2)}, u32[]{:S(2)}) collective-permute-start(f32[2,128,128]{2,1,0:T(8,128)} %refs_0_.7), channel_id=1, source_target_pairs={{0,1},{1,0},{2,3},{3,2},{4,5},{5,4},{6,7},{7,6},{8,9},{9,8},{10,11... | collective-permute-start | bytes 393224 | tf_op jit(solution)/shard_map/ppermute | solution.py:432
  6.2 46.6 %copy-start.2 = (f32[4,128,128]{2,1,0:T(8,128)S(1)}, f32[4,128,128]{2,1,0:T(8,128)}, u32[]{:S(2)}) copy-start(f32[4,128,128]{2,1,0:T(8,128)} %refs_10_.1) | copy-start | bytes 786436
  6.2 46.6 %copy-start.7 = (s32[16,2]{0,1:T(2,128)S(1)}, s32[16,2]{0,1:T(2,128)}, u32[]{:S(2)}) copy-start(s32[16,2]{0,1:T(2,128)} %param.8) | copy-start | bytes 388
  6.2 7.8 %collective-permute-start.12 = (f32[4,128,128]{2,1,0:T(8,128)S(1)}, f32[4,128,128]{2,1,0:T(8,128)S(1)}, u32[]{:S(2)}, u32[]{:S(2)}) collective-permute-start(f32[4,128,128]{2,1,0:T(8,128)S(1)} %pack.2), channel_id=1, source_target_pairs={{0,3},{1,2},{2,1},{3,0},{4,7},{5,6},{6,5},{7,4},{8,11},{9,10},{10,... | collective-permute-start | bytes 786440 | tf_op jit(solution)/shard_map/ppermute | solution.py:432
  14.0 29.2 %collective-permute-start.14 = (f32[6,128,128]{2,1,0:T(8,128)S(1)}, f32[6,128,128]{2,1,0:T(8,128)S(1)}, u32[]{:S(2)}, u32[]{:S(2)}) collective-permute-start(f32[6,128,128]{2,1,0:T(8,128)S(1)} %pack.3.refs_3_), channel_id=1, source_target_pairs={{0,64},{32,96},{64,128},{96,160},{128,192},{160,224},{192,0},{224,... | collective-permute-start | bytes 1179656 | tf_op jit(solution)/shard_map/ppermute | solution.py:425
  15.3 28.1 %collective-permute-start.16 = (f32[6,128,128]{2,1,0:T(8,128)S(1)}, f32[6,128,128]{2,1,0:T(8,128)S(1)}, u32[]{:S(2)}, u32[]{:S(2)}) collective-permute-start(f32[6,128,128]{2,1,0:T(8,128)S(1)} %pack.3.refs_3_), channel_id=1, source_target_pairs={{0,128},{32,160},{64,192},{96,224},{128,0},{160,32},{192,64},{224,... | collective-permute-start | bytes 1179656 | tf_op jit(solution)/shard_map/ppermute | solution.py:425
  17.8 5.2 %collective-permute-start = (f32[2,128,128]{2,1,0:T(8,128)S(1)}, f32[2,128,128]{2,1,0:T(8,128)S(1)}, u32[]{:S(2)}, u32[]{:S(2)}) collective-permute-start(f32[2,128,128]{2,1,0:T(8,128)S(1)} %copy-done), channel_id=1, source_target_pairs={{0,32},{32,0},{64,96},{96,64},{128,160},{160,128},{192,224},{224,1... | collective-permute-start | bytes 393224 | tf_op jit(solution)/shard_map/ppermute | solution.py:425
  20.7 12.1 %collective-permute-start.1 = (f32[2,128,128]{2,1,0:T(8,128)S(1)}, f32[2,128,128]{2,1,0:T(8,128)S(1)}, u32[]{:S(2)}, u32[]{:S(2)}) collective-permute-start(f32[2,128,128]{2,1,0:T(8,128)S(1)} %copy-done), channel_id=1, source_target_pairs={{0,64},{32,96},{64,128},{96,160},{128,192},{160,224},{192,0},{224,... | collective-permute-start | bytes 393224 | tf_op jit(solution)/shard_map/ppermute | solution.py:425
  20.7 18.8 %collective-permute-start.3 = (f32[2,128,128]{2,1,0:T(8,128)S(1)}, f32[2,128,128]{2,1,0:T(8,128)S(1)}, u32[]{:S(2)}, u32[]{:S(2)}) collective-permute-start(f32[2,128,128]{2,1,0:T(8,128)S(1)} %copy-done), channel_id=1, source_target_pairs={{0,128},{32,160},{64,192},{96,224},{128,0},{160,32},{192,64},{224,... | collective-permute-start | bytes 393224 | tf_op jit(solution)/shard_map/ppermute | solution.py:425
  23.0 18.9 %collective-permute-start.5 = (f32[2,128,128]{2,1,0:T(8,128)S(1)}, f32[2,128,128]{2,1,0:T(8,128)S(1)}, u32[]{:S(2)}, u32[]{:S(2)}) collective-permute-start(f32[2,128,128]{2,1,0:T(8,128)S(1)} %copy-done), channel_id=1, source_target_pairs={{0,192},{32,224},{64,0},{96,32},{128,64},{160,96},{192,128},{224,1... | collective-permute-start | bytes 393224 | tf_op jit(solution)/shard_map/ppermute | solution.py:425
  32.7 9.2 %collective-permute-start.2 = (f32[2,128,128]{2,1,0:T(8,128)S(1)}, f32[2,128,128]{2,1,0:T(8,128)S(1)}, u32[]{:S(2)}, u32[]{:S(2)}) collective-permute-start(f32[2,128,128]{2,1,0:T(8,128)S(1)} %collective-permute-done.1.refs_2_), channel_id=1, source_target_pairs={{0,32},{32,0},{64,96},{96,64},{128,160},{160,128},{192,224},{224,1... | collective-permute-start | bytes 393224 | tf_op jit(solution)/shard_map/ppermute | solution.py:425
  39.5 3.4 %collective-permute-start.4 = (f32[2,128,128]{2,1,0:T(8,128)S(1)}, f32[2,128,128]{2,1,0:T(8,128)S(1)}, u32[]{:S(2)}, u32[]{:S(2)}) collective-permute-start(f32[2,128,128]{2,1,0:T(8,128)S(1)} %collective-permute-done.3.refs_4_), channel_id=1, source_target_pairs={{0,32},{32,0},{64,96},{96,64},{128,160},{160,128},{192,224},{224,1... | collective-permute-start | bytes 393224 | tf_op jit(solution)/shard_map/ppermute | solution.py:425
  41.9 20.7 %collective-permute-start.18 = (f32[6,128,128]{2,1,0:T(8,128)S(1)}, f32[6,128,128]{2,1,0:T(8,128)S(1)}, u32[]{:S(2)}, u32[]{:S(2)}) collective-permute-start(f32[6,128,128]{2,1,0:T(8,128)S(1)} %pack.3.refs_3_), channel_id=1, source_target_pairs={{0,192},{32,224},{64,0},{96,32},{128,64},{160,96},{192,128},{224,1... | collective-permute-start | bytes 1179656 | tf_op jit(solution)/shard_map/ppermute | solution.py:425
  41.9 10.9 %collective-permute-start.6 = (f32[2,128,128]{2,1,0:T(8,128)S(1)}, f32[2,128,128]{2,1,0:T(8,128)S(1)}, u32[]{:S(2)}, u32[]{:S(2)}) collective-permute-start(f32[2,128,128]{2,1,0:T(8,128)S(1)} %collective-permute-done.5.refs_6_), channel_id=1, source_target_pairs={{0,32},{32,0},{64,96},{96,64},{128,160},{160,128},{192,224},{224,1... | collective-permute-start | bytes 393224 | tf_op jit(solution)/shard_map/ppermute | solution.py:425
  42.9 20.2 %collective-permute-start.13 = (f32[6,128,128]{2,1,0:T(8,128)S(1)}, f32[6,128,128]{2,1,0:T(8,128)S(1)}, u32[]{:S(2)}, u32[]{:S(2)}) collective-permute-start(f32[6,128,128]{2,1,0:T(8,128)S(1)} %pack.3.refs_3_), channel_id=1, source_target_pairs={{0,32},{32,0},{64,96},{96,64},{128,160},{160,128},{192,224},{224,1... | collective-permute-start | bytes 1179656 | tf_op jit(solution)/shard_map/ppermute | solution.py:425
  43.3 19.8 %collective-permute-start.15 = (f32[6,128,128]{2,1,0:T(8,128)S(1)}, f32[6,128,128]{2,1,0:T(8,128)S(1)}, u32[]{:S(2)}, u32[]{:S(2)}) collective-permute-start(f32[6,128,128]{2,1,0:T(8,128)S(1)} %collective-permute-done.14.refs_5_), channel_id=1, source_target_pairs={{0,32},{32,0},{64,96},{96,64},{128,160},{160,128},{192,224},{224,1... | collective-permute-start | bytes 1179656 | tf_op jit(solution)/shard_map/ppermute | solution.py:425
  43.4 22.4 %collective-permute-start.17 = (f32[6,128,128]{2,1,0:T(8,128)S(1)}, f32[6,128,128]{2,1,0:T(8,128)S(1)}, u32[]{:S(2)}, u32[]{:S(2)}) collective-permute-start(f32[6,128,128]{2,1,0:T(8,128)S(1)} %collective-permute-done.16.refs_7_), channel_id=1, source_target_pairs={{0,32},{32,0},{64,96},{96,64},{128,160},{160,128},{192,224},{224,1... | collective-permute-start | bytes 1179656 | tf_op jit(solution)/shard_map/ppermute | solution.py:425
  62.5 26.4 %collective-permute-start.7 = (f32[8,128,128]{2,1,0:T(8,128)S(1)}, f32[8,128,128]{2,1,0:T(8,128)S(1)}, u32[]{:S(2)}, u32[]{:S(2)}) collective-permute-start(f32[8,128,128]{2,1,0:T(8,128)S(1)} %get-tuple-element.34), channel_id=1, source_target_pairs={{0,32},{32,0},{64,96},{96,64},{128,160},{160,128},{192,224},{224,1... | collective-permute-start | bytes 1572872 | tf_op jit(solution)/shard_map/ppermute | solution.py:425
  62.6 4.4 %collective-permute-start.19 = (f32[6,128,128]{2,1,0:T(8,128)S(1)}, f32[6,128,128]{2,1,0:T(8,128)S(1)}, u32[]{:S(2)}, u32[]{:S(2)}) collective-permute-start(f32[6,128,128]{2,1,0:T(8,128)S(1)} %collective-permute-done.18.refs_9_), channel_id=1, source_target_pairs={{0,32},{32,0},{64,96},{96,64},{128,160},{160,128},{192,224},{224,1... | collective-permute-start | bytes 1179656 | tf_op jit(solution)/shard_map/ppermute | solution.py:425
  63.1 7.9 %collective-permute-start.20 = (f32[4,136,128]{2,1,0:T(8,128)S(1)}, f32[4,136,128]{2,1,0:T(8,128)S(1)}, u32[]{:S(2)}, u32[]{:S(2)}) collective-permute-start(f32[4,136,128]{2,1,0:T(8,128)S(1)} %get-tuple-element.29.fx.refs_6_), channel_id=1, source_target_pairs={{0,1},{1,0},{2,3},{3,2},{4,5},{5,4},{6,7},{7,6},{8,9},{9,8},{10,11... | collective-permute-start | bytes 835592 | tf_op jit(solution)/shard_map/ppermute | solution.py:432
  63.1 14.2 %collective-permute-start.21 = (f32[4,136,128]{2,1,0:T(8,128)S(1)}, f32[4,136,128]{2,1,0:T(8,128)S(1)}, u32[]{:S(2)}, u32[]{:S(2)}) collective-permute-start(f32[4,136,128]{2,1,0:T(8,128)S(1)} %get-tuple-element.29.fx.refs_6_), channel_id=1, source_target_pairs={{0,3},{1,2},{2,1},{3,0},{4,7},{5,6},{6,5},{7,4},{8,11},{9,10},{10,... | collective-permute-start | bytes 835592 | tf_op jit(solution)/shard_map/ppermute | solution.py:432
  65.8 13.5 %collective-permute-start.22 = (f32[4,136,128]{2,1,0:T(8,128)S(1)}, f32[4,136,128]{2,1,0:T(8,128)S(1)}, u32[]{:S(2)}, u32[]{:S(2)}) collective-permute-start(f32[4,136,128]{2,1,0:T(8,128)S(1)} %get-tuple-element.29.fx.refs_6_), channel_id=1, source_target_pairs={{0,2},{1,3},{2,0},{3,1},{4,6},{5,7},{6,4},{7,5},{8,10},{9,11},{10,... | collective-permute-start | bytes 835592 | tf_op jit(solution)/shard_map/ppermute | solution.py:432
  82.2 9.8 %collective-permute-start.25 = (f32[4,128,128]{2,1,0:T(8,128)S(1)}, f32[4,128,128]{2,1,0:T(8,128)S(1)}, u32[]{:S(2)}, u32[]{:S(2)}) collective-permute-start(f32[4,128,128]{2,1,0:T(8,128)S(1)} %get-tuple-element.46), channel_id=1, source_target_pairs={{0,4},{1,5},{2,6},{3,7},{4,8},{5,9},{6,10},{7,11},{8,12},{9,13},{1... | collective-permute-start | bytes 786440 | tf_op jit(solution)/shard_map/ppermute | solution.py:429
  83.9 16.7 %collective-permute-start.27 = (f32[4,128,128]{2,1,0:T(8,128)S(1)}, f32[4,128,128]{2,1,0:T(8,128)S(1)}, u32[]{:S(2)}, u32[]{:S(2)}) collective-permute-start(f32[4,128,128]{2,1,0:T(8,128)S(1)} %edges.4.refs_10_), channel_id=1, source_target_pairs={{0,8},{1,9},{2,10},{3,11},{4,12},{5,13},{6,14},{7,15},{8,16},{9,17... | collective-permute-start | bytes 786440 | tf_op jit(solution)/shard_map/ppermute | solution.py:440
  87.5 9.5 %collective-permute-start.26 = (f32[4,128,128]{2,1,0:T(8,128)S(1)}, f32[4,128,128]{2,1,0:T(8,128)S(1)}, u32[]{:S(2)}, u32[]{:S(2)}) collective-permute-start(f32[4,128,128]{2,1,0:T(8,128)S(1)} %get-tuple-element.40.refs_10_), channel_id=1, source_target_pairs={{0,28},{1,29},{2,30},{3,31},{4,0},{5,1},{6,2},{7,3},{8,4},{9,5},{1... | collective-permute-start | bytes 786440 | tf_op jit(solution)/shard_map/ppermute | solution.py:429
  88.9 12.1 %collective-permute-start.10 = (f32[2,128,128]{2,1,0:T(8,128)S(1)}, f32[2,128,128]{2,1,0:T(8,128)S(1)}, u32[]{:S(2)}, u32[]{:S(2)}) collective-permute-start(f32[2,128,128]{2,1,0:T(8,128)S(1)} %get-tuple-element.50), channel_id=1, source_target_pairs={{0,192},{32,224},{64,0},{96,32},{128,64},{160,96},{192,128},{224,1... | collective-permute-start | bytes 393224 | tf_op jit(solution)/shard_map/ppermute | solution.py:425
  89.2 14.8 %collective-permute-start.9 = (f32[2,128,128]{2,1,0:T(8,128)S(1)}, f32[2,128,128]{2,1,0:T(8,128)S(1)}, u32[]{:S(2)}, u32[]{:S(2)}) collective-permute-start(f32[2,128,128]{2,1,0:T(8,128)S(1)} %get-tuple-element.51), channel_id=1, source_target_pairs={{0,128},{32,160},{64,192},{96,224},{128,0},{160,32},{192,64},{224,... | collective-permute-start | bytes 393224 | tf_op jit(solution)/shard_map/ppermute | solution.py:425
  92.0 14.4 %collective-permute-start.8 = (f32[2,128,128]{2,1,0:T(8,128)S(1)}, f32[2,128,128]{2,1,0:T(8,128)S(1)}, u32[]{:S(2)}, u32[]{:S(2)}) collective-permute-start(f32[2,128,128]{2,1,0:T(8,128)S(1)} %get-tuple-element.49), channel_id=1, source_target_pairs={{0,64},{32,96},{64,128},{96,160},{128,192},{160,224},{192,0},{224,... | collective-permute-start | bytes 393224 | tf_op jit(solution)/shard_map/ppermute | solution.py:425
  97.0 10.5 %collective-permute-start.24 = (f32[4,128,128]{2,1,0:T(8,128)S(1)}, f32[4,128,128]{2,1,0:T(8,128)S(1)}, u32[]{:S(2)}, u32[]{:S(2)}) collective-permute-start(f32[4,128,128]{2,1,0:T(8,128)S(1)} %get-tuple-element.43.refs_10_), channel_id=1, source_target_pairs={{0,28},{1,29},{2,30},{3,31},{4,0},{5,1},{6,2},{7,3},{8,4},{9,5},{1... | collective-permute-start | bytes 786440 | tf_op jit(solution)/shard_map/ppermute | solution.py:429
  100.6 9.7 %collective-permute-start.23 = (f32[4,128,128]{2,1,0:T(8,128)S(1)}, f32[4,128,128]{2,1,0:T(8,128)S(1)}, u32[]{:S(2)}, u32[]{:S(2)}) collective-permute-start(f32[4,128,128]{2,1,0:T(8,128)S(1)} %get-tuple-element.42), channel_id=1, source_target_pairs={{0,4},{1,5},{2,6},{3,7},{4,8},{5,9},{6,10},{7,11},{8,12},{9,13},{1... | collective-permute-start | bytes 786440 | tf_op jit(solution)/shard_map/ppermute | solution.py:429
  101.0 21.9 %collective-permute-start.28 = (f32[4,128,128]{2,1,0:T(8,128)S(1)}, f32[4,128,128]{2,1,0:T(8,128)S(1)}, u32[]{:S(2)}, u32[]{:S(2)}) collective-permute-start(f32[4,128,128]{2,1,0:T(8,128)S(1)} %get-tuple-element.47), channel_id=1, source_target_pairs={{0,8},{1,9},{2,10},{3,11},{4,12},{5,13},{6,14},{7,15},{8,16},{9,17... | collective-permute-start | bytes 786440 | tf_op jit(solution)/shard_map/ppermute | solution.py:429
  104.0 18.9 %collective-permute-start.29 = (f32[4,128,128]{2,1,0:T(8,128)S(1)}, f32[4,128,128]{2,1,0:T(8,128)S(1)}, u32[]{:S(2)}, u32[]{:S(2)}) collective-permute-start(f32[4,128,128]{2,1,0:T(8,128)S(1)} %get-tuple-element.48), channel_id=1, source_target_pairs={{0,24},{1,25},{2,26},{3,27},{4,28},{5,29},{6,30},{7,31},{8,0},{9,1... | collective-permute-start | bytes 786440 | tf_op jit(solution)/shard_map/ppermute | solution.py:429
  (6 other events, 101.8 us)

commit v2 on v1

v2 whole, which is shorter than its diff:
```python
import functools

import jax
import jax.numpy as jnp
from jax import lax
from jax.experimental import pallas as pl
from jax.experimental.pallas import tpu as pltpu
from jax.sharding import PartitionSpec as P


very_low = -1e30
f32, bf16 = jnp.float32, jnp.bfloat16
CORES = 2
ROWS = 4
VMEM = pltpu.VMEM
SMEM = pltpu.SMEM


def parts(x):
    hi = x.astype(bf16)
    lo = (x - hi.astype(f32)).astype(bf16)
    return hi, lo


def quadrants(x):
    g = x.shape[0] // 2
    return (x[:g, :g] + x[:g, g:]) + (x[g:, :g] + x[g:, g:])


def node_at(dx, dc, nodes):
    me = lax.axis_index("nodes")
    x, core = me // CORES, me % CORES
    chips = nodes // CORES
    return ((x + dx) % chips) * CORES + (core + dc) % CORES


def hops(nodes):
    return [(dx, dc) for dx in range(nodes // CORES) for dc in range(CORES)]


def vmem_specs(n):
    return [pl.BlockSpec(memory_space=VMEM)] * n


def fold_kernel(each, count, slots_any, w_hbm, acc, bias, w, slots, sems, sem):
    pg = acc.shape[1]
    steps = w.shape[0] // each
    index = pltpu.make_async_copy(slots_any, slots, sem)
    index.start()
    copies = []
    for j in range(steps):
        at = pl.ds(j * each, each)
        copies.append(pltpu.make_async_copy(w_hbm.at[at], w.at[at], sems.at[j]))
        copies[j].start()

    bias[...] = jnp.full(bias.shape, very_low, f32)

    def clear(c, carry):
        for q in range(acc.shape[0]):
            acc[q, c] = jnp.zeros(acc.shape[2:], f32)
        return carry

    lax.fori_loop(0, pg, clear, 0)
    index.wait()
    for j in range(steps):
        copies[j].wait()

        def add(t, carry, j=j):
            b = j * each + t
            c, q = slots[0, b], slots[1, b]
            live = b < count[0]
            acc[q, c] += w[b] * live.astype(f32)
            row = pl.ds(q * pg + c, 1)
            bias[row, :] = jnp.where(live, 0.0, bias[row, :])
            return carry

        lax.fori_loop(0, each, add, 0, unroll=4)


def fold(slots, block_count, block_weight, pg, qd):
    blocks, g, _ = block_weight.shape
    each = 16
    return pl.pallas_call(
        functools.partial(fold_kernel, each),
        out_shape=(
            jax.ShapeDtypeStruct((qd, pg, g, g), f32),
            jax.ShapeDtypeStruct((qd * pg, g), f32),
        ),
        in_specs=[
            pl.BlockSpec(memory_space=SMEM),
            pl.BlockSpec(memory_space=pl.ANY),
            pl.BlockSpec(memory_space=pltpu.HBM),
        ],
        out_specs=tuple(vmem_specs(2)),
        scratch_shapes=[
            VMEM((blocks, g, g), f32),
            SMEM(slots.shape, jnp.int32),
            pltpu.SemaphoreType.DMA((blocks // each,)),
            pltpu.SemaphoreType.DMA,
        ],
        compiler_params=pltpu.CompilerParams(vmem_limit_bytes=46 << 20),
        cost_estimate=pl.CostEstimate(flops=20_000_000, bytes_accessed=16 << 20, transcendentals=0),
        name="fold",
    )(block_count, slots, block_weight)


def forward_kernel(nodes, prod_child, *refs):
    n = nodes
    got = refs[:n]
    w_ref, bias, up, sv, fx, e_ref, r_ref, pk, lv, whl, shl = refs[n:]
    pg, g, s = e_ref.shape
    for k, (dx, dc) in enumerate(hops(n)):
        src = node_at(-dx, -dc, n)
        each = got[k].shape[0]
        lv[pl.ds(src * each, each)] = got[k][...]

    def product(p, carry):
        x = lv[prod_child[0, p]] + lv[prod_child[1, p]]
        m = jnp.max(x, axis=0, keepdims=True)
        pk[pl.ds(p, 1), :] = m
        e_ref[p] = jnp.exp(x - m)
        return carry

    lax.fori_loop(0, pg, product, 0, unroll=2)
    for q in range(up.shape[0]):
        biased = pk[...] + bias[q * pg : (q + 1) * pg]
        top = jnp.max(biased, axis=0, keepdims=True)
        r_ref[q * pg : (q + 1) * pg] = jnp.exp(biased - top)

        def scaled(c, carry, q=q):
            at = pl.ds(pl.multiple_of(c * g, g), g)
            hi, lo = parts(w_ref[q, c])
            whl[q % 2, 0:g, at] = hi
            whl[q % 2, g : 2 * g, at] = lo
            hi, lo = parts(e_ref[c] * r_ref[pl.ds(q * pg + c, 1), :])
            shl[q % 2, at, 0:s] = hi
            shl[q % 2, at, s : 2 * s] = lo
            return carry

        lax.fori_loop(0, pg, scaled, 0, unroll=2)
        total = quadrants(jnp.dot(whl[q % 2], shl[q % 2], preferred_element_type=f32))
        sv[q] = top + jnp.log(total)
        fx[q, 0:g] = up[q] / total
        fx[q, g:] = jnp.broadcast_to(top, (8, s))


def forward(prod_child, got, w, bias, up):
    nodes = len(got)
    qd, g, s = up.shape
    pg = prod_child.shape[1]
    return pl.pallas_call(
        functools.partial(forward_kernel, nodes),
        out_shape=(
            jax.ShapeDtypeStruct((qd, g, s), f32),
            jax.ShapeDtypeStruct((qd, g + 8, s), f32),
            jax.ShapeDtypeStruct((pg, g, s), f32),
            jax.ShapeDtypeStruct((qd * pg, s), f32),
            jax.ShapeDtypeStruct((pg, s), f32),
        ),
        in_specs=[pl.BlockSpec(memory_space=SMEM)] + vmem_specs(nodes + 3),
        out_specs=tuple(vmem_specs(5)),
        scratch_shapes=[
            VMEM((got[0].shape[0] * nodes, g, s), f32),
            VMEM((2, 2 * g, pg * g), bf16),
            VMEM((2, pg * g, 2 * s), bf16),
        ],
        compiler_params=pltpu.CompilerParams(vmem_limit_bytes=20 << 20),
        cost_estimate=pl.CostEstimate(
            flops=2 * qd * 4 * g * s * pg * g, bytes_accessed=8 << 20, transcendentals=pg * g * s
        ),
        name="forward",
    )(prod_child, *got, w, bias, up)


def backward_kernel(nodes, each, prod_child, w_ref, fx, r_ref, e_ref, *refs):
    chips = nodes // CORES
    keep, give, (lf, thl, ghl) = refs[:chips], refs[chips], refs[chips + 1 :]
    qd = fx.shape[0]
    pg, g, s = e_ref.shape
    lf[...] = jnp.zeros(lf.shape, f32)

    def some(step, carry):
        for t in range(each):
            c = step * each + t
            for q in range(qd):
                at = slice(q * g, (q + 1) * g)
                hi, lo = parts(w_ref[q, c].T)
                thl[t, 0:g, at] = hi
                thl[t, g : 2 * g, at] = lo
                hi, lo = parts(fx[q, 0:g] * r_ref[pl.ds(q * pg + c, 1), :])
                ghl[t, at, 0:s] = hi
                ghl[t, at, s : 2 * s] = lo
        for t in range(each):
            c = step * each + t
            back = quadrants(jnp.dot(thl[t], ghl[t], preferred_element_type=f32))
            flow = back * e_ref[c]
            lf[prod_child[0, c]] += flow
            lf[prod_child[1, c]] += flow
        return carry

    lax.fori_loop(0, pg // each, some, 0)
    for dx in range(chips):
        k = keep[0].shape[0]
        keep[dx][...] = lf[pl.ds(node_at(dx, 0, nodes) * k, k)]
        give[dx * k : (dx + 1) * k] = lf[pl.ds(node_at(dx, 1, nodes) * k, k)]


def backward(prod_child, w, fx, r, e, nodes, ng):
    pg, g, s = e.shape
    qd = fx.shape[0]
    chips = nodes // CORES
    each = 4
    k = ng // nodes
    return pl.pallas_call(
        functools.partial(backward_kernel, nodes, each),
        out_shape=[jax.ShapeDtypeStruct((k, g, s), f32)] * chips
        + [jax.ShapeDtypeStruct((k * chips, g, s), f32)],
        in_specs=[pl.BlockSpec(memory_space=SMEM)] + vmem_specs(4),
        out_specs=vmem_specs(chips + 1),
        scratch_shapes=[
            VMEM((ng, g, s), f32),
            VMEM((each, 2 * g, qd * g), bf16),
            VMEM((each, qd * g, 2 * s), bf16),
        ],
        compiler_params=pltpu.CompilerParams(vmem_limit_bytes=20 << 20),
        cost_estimate=pl.CostEstimate(
            flops=2 * qd * 4 * g * s * pg * g, bytes_accessed=8 << 20, transcendentals=0
        ),
        name="backward",
    )(prod_child, w, fx, r, e)


def pack_kernel(*refs):
    at = 0
    for a in refs[:-1]:
        k = a.shape[0]
        refs[-1][at : at + k] = a[...]
        at += k


def pack(arrays):
    n = sum(a.shape[0] for a in arrays)
    return pl.pallas_call(
        pack_kernel,
        out_shape=jax.ShapeDtypeStruct((n,) + arrays[0].shape[1:], f32),
        in_specs=vmem_specs(len(arrays)),
        out_specs=vmem_specs(1)[0],
        compiler_params=pltpu.CompilerParams(vmem_limit_bytes=4 << 20),
        cost_estimate=pl.CostEstimate(flops=0, bytes_accessed=1 << 20, transcendentals=0),
        name="pack",
    )(*arrays)


def spread_kernel(offsets, prod_child, token, e_own, pk_own, *refs):
    pieces, (ehl, pk) = refs[: len(offsets)], refs[len(offsets) : -1]
    lv = refs[-1]
    pg, g, s = e_own.shape
    sets = lv.shape[0]
    each = pieces[0].shape[0] // sets
    nodes = lv.shape[1] // each
    for (dx, dc), piece in zip(offsets, pieces):
        src = node_at(-dx, -dc, nodes)
        for t in range(sets):
            lv[t, pl.ds(src * each, each)] = piece[t * each : (t + 1) * each]

    def product(p, carry):
        hi, lo = parts(e_own[p])
        ehl[p, 0:g, 0:s] = hi
        ehl[p, g : 2 * g, 0:s] = lo
        pk[0, pl.ds(p, 1), :] = pk_own[pl.ds(p, 1), :]
        a, b = prod_child[0, p], prod_child[1, p]
        for t in range(sets):
            x = lv[t, a] + lv[t, b]
            m = jnp.max(x, axis=0, keepdims=True)
            at = slice((t + 1) * s, (t + 2) * s)
            pk[t + 1, pl.ds(p, 1), :] = m
            hi, lo = parts(jnp.exp(x - m))
            ehl[p, 0:g, at] = hi
            ehl[p, g : 2 * g, at] = lo
        return carry

    lax.fori_loop(0, pg, product, 0, unroll=2)


def spread(prod_child, e, pk, pieces, offsets, nodes, token):
    pg, g, s = e.shape
    sets = ROWS - 1
    each = pieces[0].shape[0] // sets

    def kernel(*refs):
        spread_kernel(offsets, *refs)

    return pl.pallas_call(
        kernel,
        out_shape=(
            jax.ShapeDtypeStruct((pg, 2 * g, (sets + 1) * s), bf16),
            jax.ShapeDtypeStruct((sets + 1, pg, s), f32),
        ),
        in_specs=[pl.BlockSpec(memory_space=SMEM), pl.BlockSpec(memory_space=pl.ANY)]
        + vmem_specs(2 + len(pieces)),
        out_specs=tuple(vmem_specs(2)),
        scratch_shapes=[VMEM((sets, nodes * each, g, s), f32)],
        compiler_params=pltpu.CompilerParams(vmem_limit_bytes=20 << 20),
        cost_estimate=pl.CostEstimate(
            flops=10_000_000, bytes_accessed=10 << 20, transcendentals=pg * g * s * sets
        ),
        name="spread",
    )(prod_child, token, e, pk, *pieces)


def edges_kernel(plan, slots, count, ehl, pk, bias, *refs):
    rows = ROWS
    fxs, refs = refs[:rows], refs[rows:]
    outs, (r, lhs) = refs[1:-2], refs[-2:]
    qd, s = fxs[0].shape[0], fxs[0].shape[2]
    g = fxs[0].shape[1] - 8
    pg = pk.shape[1]
    batch = lax.axis_index("batch")
    z, y = batch // ROWS, batch % ROWS
    depth = lax.axis_size("batch") // ROWS
    for q in range(qd):
        for t in range(rows):
            top = fxs[t][q, g : g + 1]
            here = slice(q * pg, (q + 1) * pg)
            r[t, here, :] = jnp.exp((pk[t] + bias[here, :]) - top)
    for (d, k0, n, keep), out in zip(plan, outs):
        base = ((z + d + depth) % depth * ROWS + y) * keep + k0
        for k in range(n):
            b = base + k
            c, q = slots[0, b], slots[1, b]
            live = (b < count[0]).astype(f32)
            for t in range(rows):
                at = slice(t * s, (t + 1) * s)
                hi, lo = parts(fxs[t][q, 0:g] * (r[t, pl.ds(q * pg + c, 1), :] * live))
                lhs[k, 0:g, at] = hi
                lhs[k, g : 2 * g, at] = lo
        for k in range(n):
            c = slots[0, base + k]
            out[k] = quadrants(
                lax.dot_general(
                    lhs[k], ehl[c], (((1,), (1,)), ((), ())), preferred_element_type=f32
                )
            )


def edges(slots, count, ehl, pk, bias, fxs, token, plan):
    g = ehl.shape[1] // 2
    pg, width = pk.shape[1], ehl.shape[2]
    qd = fxs[0].shape[0]
    total = sum(n for _, _, n, _ in plan)

    def kernel(*refs):
        edges_kernel(plan, *refs)

    return pl.pallas_call(
        kernel,
        out_shape=[jax.ShapeDtypeStruct((n, g, g), f32) for _, _, n, _ in plan],
        in_specs=[pl.BlockSpec(memory_space=SMEM)] * 2
        + vmem_specs(3 + len(fxs))
        + [pl.BlockSpec(memory_space=pl.ANY)],
        out_specs=vmem_specs(len(plan)),
        scratch_shapes=[
            VMEM((len(fxs), qd * pg, width // len(fxs)), f32),
            VMEM((max(n for _, _, n, _ in plan), 2 * g, width), bf16),
        ],
        compiler_params=pltpu.CompilerParams(vmem_limit_bytes=20 << 20),
        cost_estimate=pl.CostEstimate(
            flops=2 * total * 4 * g * g * width, bytes_accessed=6 << 20, transcendentals=0
        ),
        name="edges",
    )(slots, count, ehl, pk, bias, *fxs, token)


def join_kernel(ap, am, bp, bm, c_ref, outp, outm):
    first = (lax.axis_index("nodes") % CORES == 0).astype(f32)
    outp[...] = (ap[...] + bp[...]) + c_ref[...] * first
    outm[...] = (am[...] + bm[...]) + c_ref[...] * (1.0 - first)


def join(ap, am, bp, bm, c):
    return pl.pallas_call(
        join_kernel,
        out_shape=[jax.ShapeDtypeStruct(ap.shape, f32)] * 2,
        in_specs=vmem_specs(5),
        out_specs=vmem_specs(2),
        compiler_params=pltpu.CompilerParams(vmem_limit_bytes=4 << 20),
        cost_estimate=pl.CostEstimate(flops=400_000, bytes_accessed=2 << 20, transcendentals=0),
        name="join",
    )(ap, am, bp, bm, c)


def near_kernel(w_hbm, a_ref, b_ref, c_ref, near, w, sem):
    keep = w.shape[0]
    own = w_hbm.at[pl.ds(lax.axis_index("batch") * keep, keep)]
    copy = pltpu.make_async_copy(own, w, sem)
    copy.start()
    copy.wait()
    near[...] = w[...] * (a_ref[...] + b_ref[...] + c_ref[...])


def weigh_near(w, a, b, c):
    return pl.pallas_call(
        near_kernel,
        out_shape=[jax.ShapeDtypeStruct(a.shape, f32)] * 2,
        in_specs=[pl.BlockSpec(memory_space=pltpu.HBM)] + vmem_specs(3),
        out_specs=vmem_specs(2),
        scratch_shapes=[pltpu.SemaphoreType.DMA],
        compiler_params=pltpu.CompilerParams(vmem_limit_bytes=50 << 20),
        cost_estimate=pl.CostEstimate(flops=200_000, bytes_accessed=1 << 20, transcendentals=0),
        name="near",
    )(w, a, b, c)


def last_kernel(near, w, a_ref, b_ref, out):
    out[...] = near[...] + w[...] * (a_ref[...] + b_ref[...])


def weigh_last(near, w, a, b):
    return pl.pallas_call(
        last_kernel,
        out_shape=jax.ShapeDtypeStruct(a.shape, f32),
        in_specs=vmem_specs(4),
        out_specs=vmem_specs(1)[0],
        compiler_params=pltpu.CompilerParams(vmem_limit_bytes=4 << 20),
        cost_estimate=pl.CostEstimate(flops=200_000, bytes_accessed=1 << 20, transcendentals=0),
        name="last",
    )(near, w, a, b)


def body(leaves, prod_child, block_weight, block_child, block_parent, block_count, upper_flow):
    prod_child = prod_child.T
    slots = jnp.concatenate([block_child, block_parent])
    nodes = lax.axis_size("nodes")
    batch = lax.axis_size("batch")
    chips, depth = nodes // CORES, batch // ROWS
    ng = leaves.shape[0] * nodes
    pg = prod_child.shape[1]
    qd = upper_flow.shape[0]
    keep = block_weight.shape[0] // batch
    far = depth // 2

    def move(a, dx=0, dc=0):
        to = lambda n: ((n // CORES + dx) % chips) * CORES + (n % CORES + dc) % CORES
        return lax.ppermute(a, "nodes", [(n, to(n)) for n in range(nodes)])

    def shift(a, dz):
        to = lambda b: ((b // ROWS + dz) % depth) * ROWS + b % ROWS
        return lax.ppermute(a, "batch", [(b, to(b)) for b in range(batch)])

    def swap(a, mask):
        return lax.ppermute(a, "batch", [(b, b ^ mask) for b in range(batch)])

    def shift_by_core(a, dz):
        pairs = []
        for n in range(nodes):
            for b in range(batch):
                z = (b // ROWS + (dz if n % CORES == 0 else -dz)) % depth
                pairs.append((n * batch + b, n * batch + z * ROWS + b % ROWS))
        return lax.ppermute(a, ("nodes", "batch"), pairs)

    def gather(a):
        out = []
        for dx in range(chips):
            got = move(a, dx) if dx else a
            out += [got, move(got, 0, 1)]
        return out

    got = gather(leaves)
    one = swap(leaves, 1)
    pair = pack([leaves, one])
    two = swap(pair, 3)
    packed = pack([one, two])
    pieces = gather(packed)

    w, bias = fold(slots, block_count, block_weight, pg, qd)
    sum_values, fx, e, r, pk = forward(prod_child, got, w, bias, upper_flow)
    fxs = [fx] + [swap(fx, t) for t in (1, 3, 2)]
    *mine, give = backward(prod_child, w, fx, r, e, nodes, ng)
    given = move(give, 0, 1)
    k = leaves.shape[0]
    flows = [a + given[dx * k : (dx + 1) * k] for dx, a in enumerate(mine)]
    ehl, pks = spread(prod_child, e, pk, pieces, hops(nodes), nodes, flows[1])

    def part(token, *ds):
        plan = [(d, 0, keep, keep) for d in ds]
        return edges(slots, block_count, ehl, pks, bias, fxs, token, plan)

    (e4,) = part(pks, far)
    r4 = shift_by_core(e4, 2)
    e3p, e3m = part(e4, 3, -3)
    r3p, r3m = shift(e3p, 1), shift(e3m, -1)
    e1p, e1m, e0 = part(e3m, 1, -1, 0)
    r1p, r1m = shift(e1p, 1), shift(e1m, -1)
    e2p, e2m = part(e1m, 2, -2)
    c2p, c2m = join(e2p, e2m, r3p, r3m, r4)
    r2p, r2m = shift(c2p, 2), shift(c2m, -2)
    leaf_flow = functools.reduce(
        jnp.add, [flows[0]] + [move(flows[dx], dx) for dx in range(1, chips)]
    )
    near, own = weigh_near(block_weight, e0, r1p, r1m)
    param_flow = weigh_last(near, own, r2p, r2m)
    return sum_values, leaf_flow, param_flow


def solution(mesh):
    placed = (
        P("nodes", None, "batch"),
        P(),
        P("nodes", None, None),
        P("nodes", None),
        P("nodes", None),
        P("nodes"),
        P("nodes", None, "batch"),
    )
    return jax.shard_map(
        body,
        mesh=mesh,
        in_specs=placed,
        out_specs=(
            P("nodes", None, "batch"),
            P("nodes", None, "batch"),
            P(("nodes", "batch"), None, None),
        ),
        check_vma=False,
    )
```

time: 125 us -> 116 us (0.928)
  the two profiles are of different devices: /device:TPU:33 before, /device:TPU:2 now
where the time goes in v2:
time: 116 us; the launch traced here: 115 us
  waiting for transfers between devices  51 us (44%)
  starting transfers between devices  35 us (30%)
  Pallas kernels  25.8 us (22%)
  between operations  1.47 us (1%)
  other arithmetic  1.44 us (1%)
    ppermute x18, waiting for transfers between devices, move(): return lax.ppermute(a, 'nodes', [(n, to(n)) for n in range(nodes)])  21.6 us
    ppermute x6, waiting for transfers between devices, shift(): return lax.ppermute(a, 'batch', [(b, to(b)) for b in range(batch)])  15.4 us
    ppermute x5, waiting for transfers between devices, swap(): return lax.ppermute(a, 'batch', [(b, b ^ mask) for b in range(batch)])  14 us
    ppermute x18, starting transfers between devices, move(): return lax.ppermute(a, 'nodes', [(n, to(n)) for n in range(nodes)])  13.3 us
    ppermute x6, starting transfers between devices, shift(): return lax.ppermute(a, 'batch', [(b, to(b)) for b in range(batch)])  12.9 us
    ppermute x5, starting transfers between devices, swap(): return lax.ppermute(a, 'batch', [(b, b ^ mask) for b in range(batch)])  8.86 us
    pallas_call x1, Pallas kernels, forward(): pl.pallas_call(functools.partial(forward_kernel, nodes), out_shape=(jax.S...  6.87 us
    pallas_call x4, Pallas kernels, edges(): pl.pallas_call(kernel, out_shape=[jax.ShapeDtypeStruct((n, g, g), f32) fo...  6.79 us
  transfers between devices with their start and end apart: 30, of which 12 were waited for; matrix products, arithmetic and copies ran while one was open for 1% of the time, Pallas kernels for 19%

profile of v2, /device:TPU:2, one launch (start us, length us, event | category | flops | bytes accessed | tf_op | source)
XLA Modules:
  0.0 114.8 jit_solution(7884165889812944618)
XLA Ops:
  0.6 1.7 %collective-permute-start.11 = (f32[2,128,128]{2,1,0:T(8,128)}, f32[2,128,128]{2,1,0:T(8,128)S(1)}, u32[]{:S(2)}, u32[]{:S(2)}) collective-permute-start(f32[2,128,128]{2,1,0:T(8,128)} %refs_0_.3), channel_id=1, source_target_pairs={{0,1},{1,0},{2,3},{3,2},{4,5},{5,4},{6,7},{7,6},{8,9},{9,8},{10,11... | collective-permute-start | bytes 393224 | tf_op jit(solution)/shard_map/ppermute | solution.py:451
  2.3 3.9 %collective-permute-done.11.refs_1_.refs_0_ = f32[2,128,128]{2,1,0:T(8,128)S(1)} collective-permute-done((f32[2,128,128]{2,1,0:T(8,128)}, f32[2,128,128]{2,1,0:T(8,128)S(1)}, u32[]{:S(2)}, u32[]{:S(2)}) %collective-permute-start.11) | collective-permute-done | bytes 131104 | tf_op jit(solution)/shard_map/ppermute | solution.py:451
  7.1 3.1 %collective-permute-start.12 = (f32[4,128,128]{2,1,0:T(8,128)S(1)}, f32[4,128,128]{2,1,0:T(8,128)S(1)}, u32[]{:S(2)}, u32[]{:S(2)}) collective-permute-start(f32[4,128,128]{2,1,0:T(8,128)S(1)} %pack.2), channel_id=1, source_target_pairs={{0,3},{1,2},{2,1},{3,0},{4,7},{5,6},{6,5},{7,4},{8,11},{9,10},{10,... | collective-permute-start | bytes 786440 | tf_op jit(solution)/shard_map/ppermute | solution.py:451
  10.2 1.5 %collective-permute-start.1 = (f32[2,128,128]{2,1,0:T(8,128)}, f32[2,128,128]{2,1,0:T(8,128)S(1)}, u32[]{:S(2)}, u32[]{:S(2)}) collective-permute-start(f32[2,128,128]{2,1,0:T(8,128)} %refs_0_.3), channel_id=1, source_target_pairs={{0,64},{32,96},{64,128},{96,160},{128,192},{160,224},{192,0},{224,... | collective-permute-start | bytes 393224 | tf_op jit(solution)/shard_map/ppermute | solution.py:444
  12.8 2.2 %collective-permute-start.5 = (f32[2,128,128]{2,1,0:T(8,128)}, f32[2,128,128]{2,1,0:T(8,128)S(1)}, u32[]{:S(2)}, u32[]{:S(2)}) collective-permute-start(f32[2,128,128]{2,1,0:T(8,128)} %refs_0_.3), channel_id=1, source_target_pairs={{0,192},{32,224},{64,0},{96,32},{128,64},{160,96},{192,128},{224,1... | collective-permute-start | bytes 393224 | tf_op jit(solution)/shard_map/ppermute | solution.py:444
  15.0 1.6 %collective-permute-done.1.refs_2_ = f32[2,128,128]{2,1,0:T(8,128)S(1)} collective-permute-done((f32[2,128,128]{2,1,0:T(8,128)}, f32[2,128,128]{2,1,0:T(8,128)S(1)}, u32[]{:S(2)}, u32[]{:S(2)}) %collective-permute-start.1) | collective-permute-done | bytes 131104 | tf_op jit(solution)/shard_map/ppermute | solution.py:444
  16.6 2.2 %collective-permute-done.3.refs_4_ = f32[2,128,128]{2,1,0:T(8,128)S(1)} collective-permute-done((f32[2,128,128]{2,1,0:T(8,128)}, f32[2,128,128]{2,1,0:T(8,128)S(1)}, u32[]{:S(2)}, u32[]{:S(2)}) %collective-permute-start.3) | collective-permute-done | bytes 131104 | tf_op jit(solution)/shard_map/ppermute | solution.py:444
  20.1 1.4 %collective-permute-start.14 = (f32[6,128,128]{2,1,0:T(8,128)S(1)}, f32[6,128,128]{2,1,0:T(8,128)S(1)}, u32[]{:S(2)}, u32[]{:S(2)}) collective-permute-start(f32[6,128,128]{2,1,0:T(8,128)S(1)} %pack.3.refs_4_), channel_id=1, source_target_pairs={{0,64},{32,96},{64,128},{96,160},{128,192},{160,224},{192,0},{224,... | collective-permute-start | bytes 1179656 | tf_op jit(solution)/shard_map/ppermute | solution.py:444
  22.2 3.7 %fold.1 = (f32[4,16,128,128]{3,2,1,0:T(8,128)S(1)}, f32[64,128]{1,0:T(8,128)S(1)}) custom-call(s32[1]{0:T(128)S(6)} %copy.10.count.refs_1_, s32[2,128]{1,0:T(2,128)S(1)} %pad_add_fusion.slots_any.refs_0_, f32[128,128,128]{2,1,0:T(8,128)} %w_hbm.3), custom_call_target="tpu_custom_call" | custom-call | flops 20000000 | bytes 16777216 | tf_op jit(solution)/shard_map/fold/pallas_call | solution.py:83
  25.9 6.9 %forward.1 = (f32[4,128,128]{2,1,0:T(8,128)}, f32[4,136,128]{2,1,0:T(8,128)S(1)}, f32[16,128,128]{2,1,0:T(8,128)S(1)}, f32[64,128]{1,0:T(8,128)S(1)}, f32[16,128]{1,0:T(8,128)S(1)}) custom-call(s32[2,16]{1,0:T(2,128)S(1)} %bitcast.1, f32[2,128,128]{2,1,0:T(8,128)} %refs_0_.3, f32[2,128,128]{2,1,0:T(8,128)S(1)} %collective-permute-done.refs_1_, ...), custom_call_target="tpu_custom_call" | custom-call | flops 1073741824 | bytes 8388608 | tf_op jit(solution)/shard_map/forward/pallas_call | solution.py:151
  32.8 3.7 %backward.1 = (f32[2,128,128]{2,1,0:T(8,128)S(1)}, f32[2,128,128]{2,1,0:T(8,128)S(1)}, f32[2,128,128]{2,1,0:T(8,128)S(1)}, f32[2,128,128]{2,1,0:T(8,128)S(1)}, f32[8,128,128]{2,1,0:T(8,128)S(1)}) custom-call(s32[2,16]{1,0:T(2,128)S(1)} %bitcast.2, f32[4,16,128,128]{3,2,1,0:T(8,128)S(1)} %get-tuple-element.28.refs_8_.w_ref, ...), custom_call_target="tpu_custom_call" | custom-call | flops 1073741824 | bytes 8388608 | tf_op jit(solution)/shard_map/backward/pallas_call | solution.py:214
  36.7 1.8 %collective-permute-start.16 = (f32[6,128,128]{2,1,0:T(8,128)S(1)}, f32[6,128,128]{2,1,0:T(8,128)S(1)}, u32[]{:S(2)}, u32[]{:S(2)}) collective-permute-start(f32[6,128,128]{2,1,0:T(8,128)S(1)} %pack.3.refs_4_), channel_id=1, source_target_pairs={{0,128},{32,160},{64,192},{96,224},{128,0},{160,32},{192,64},{224,... | collective-permute-start | bytes 1179656 | tf_op jit(solution)/shard_map/ppermute | solution.py:444
  38.5 1.7 %collective-permute-start.18 = (f32[6,128,128]{2,1,0:T(8,128)S(1)}, f32[6,128,128]{2,1,0:T(8,128)S(1)}, u32[]{:S(2)}, u32[]{:S(2)}) collective-permute-start(f32[6,128,128]{2,1,0:T(8,128)S(1)} %pack.3.refs_4_), channel_id=1, source_target_pairs={{0,192},{32,224},{64,0},{96,32},{128,64},{160,96},{192,128},{224,1... | collective-permute-start | bytes 1179656 | tf_op jit(solution)/shard_map/ppermute | solution.py:444
  40.8 9.5 %collective-permute-done.16.refs_8_ = f32[6,128,128]{2,1,0:T(8,128)S(1)} collective-permute-done((f32[6,128,128]{2,1,0:T(8,128)S(1)}, f32[6,128,128]{2,1,0:T(8,128)S(1)}, u32[]{:S(2)}, u32[]{:S(2)}) %collective-permute-start.16) | collective-permute-done | bytes 393248 | tf_op jit(solution)/shard_map/ppermute | solution.py:444
  50.3 7.7 %collective-permute-done.18.refs_10_ = f32[6,128,128]{2,1,0:T(8,128)S(1)} collective-permute-done((f32[6,128,128]{2,1,0:T(8,128)S(1)}, f32[6,128,128]{2,1,0:T(8,128)S(1)}, u32[]{:S(2)}, u32[]{:S(2)}) %collective-permute-start.18) | collective-permute-done | bytes 393248 | tf_op jit(solution)/shard_map/ppermute | solution.py:444
  59.2 2.9 %collective-permute-start.22 = (f32[4,136,128]{2,1,0:T(8,128)S(1)}, f32[4,136,128]{2,1,0:T(8,128)S(1)}, u32[]{:S(2)}, u32[]{:S(2)}) collective-permute-start(f32[4,136,128]{2,1,0:T(8,128)S(1)} %get-tuple-element.31.fx.refs_5_), channel_id=1, source_target_pairs={{0,2},{1,3},{2,0},{3,1},{4,6},{5,7},{6,4},{7,5},{8,10},{9,11},{10,... | collective-permute-start | bytes 835592 | tf_op jit(solution)/shard_map/ppermute | solution.py:451
  62.2 2.0 %spread.1 = (bf16[16,256,512]{2,1,0:T(8,128)(2,1)S(1)}, f32[4,16,128]{2,1,0:T(8,128)S(1)}) custom-call(s32[2,16]{1,0:T(2,128)S(1)} %bitcast.3, f32[2,128,128]{2,1,0:T(8,128)S(1)} %get-tuple-element.53.refs_1_, f32[16,128,128]{2,1,0:T(8,128)S(1)} %get-tuple-element.33.e_ref.refs_2_, f32[16,128]{1,0:T(8,128)S(1)} %get-tuple-element.39.refs_3_, ...), custom_call_target="tpu_custom_call" | custom-call | flops 10000000 | bytes 10485760 | tf_op jit(solution)/shard_map/spread/pallas_call | solution.py:293
  64.2 3.3 %collective-permute-done.20.refs_6_ = f32[4,136,128]{2,1,0:T(8,128)S(1)} collective-permute-done((f32[4,136,128]{2,1,0:T(8,128)S(1)}, f32[4,136,128]{2,1,0:T(8,128)S(1)}, u32[]{:S(2)}, u32[]{:S(2)}) %collective-permute-start.20) | collective-permute-done | bytes 278560 | tf_op jit(solution)/shard_map/ppermute | solution.py:451
  67.5 6.8 %collective-permute-done.21.refs_7_ = f32[4,136,128]{2,1,0:T(8,128)S(1)} collective-permute-done((f32[4,136,128]{2,1,0:T(8,128)S(1)}, f32[4,136,128]{2,1,0:T(8,128)S(1)}, u32[]{:S(2)}, u32[]{:S(2)}) %collective-permute-start.21) | collective-permute-done | bytes 278560 | tf_op jit(solution)/shard_map/ppermute | solution.py:451
  75.4 1.8 %edges.5 = (f32[4,128,128]{2,1,0:T(8,128)S(1)}, f32[4,128,128]{2,1,0:T(8,128)S(1)}) custom-call(s32[2,128]{1,0:T(2,128)S(1)} %pad_add_fusion.slots_any.refs_0_, s32[1]{0:T(128)S(6)} %copy.10.count.refs_1_, bf16[16,256,512]{2,1,0:T(8,128)(2,1)S(1)} %get-tuple-element.40.refs_2_, f32[4,16,128]{2,1,0:T(8,128)S(1)} %get-tuple-element.41.refs_3_.refs_9_, ...), custom_call_target="tpu_custom_call" | custom-call | flops 536870912 | bytes 6291456 | tf_op jit(solution)/shard_map/edges/pallas_call | solution.py:355
  77.2 2.0 %collective-permute-start.25 = (f32[4,128,128]{2,1,0:T(8,128)S(1)}, f32[4,128,128]{2,1,0:T(8,128)S(1)}, u32[]{:S(2)}, u32[]{:S(2)}) collective-permute-start(f32[4,128,128]{2,1,0:T(8,128)S(1)} %get-tuple-element.50), channel_id=1, source_target_pairs={{0,4},{1,5},{2,6},{3,7},{4,8},{5,9},{6,10},{7,11},{8,12},{9,13},{1... | collective-permute-start | bytes 786440 | tf_op jit(solution)/shard_map/ppermute | solution.py:448
  79.2 4.0 %collective-permute-start.26 = (f32[4,128,128]{2,1,0:T(8,128)S(1)}, f32[4,128,128]{2,1,0:T(8,128)S(1)}, u32[]{:S(2)}, u32[]{:S(2)}) collective-permute-start(f32[4,128,128]{2,1,0:T(8,128)S(1)} %get-tuple-element.42.refs_9_), channel_id=1, source_target_pairs={{0,28},{1,29},{2,30},{3,31},{4,0},{5,1},{6,2},{7,3},{8,4},{9,5},{1... | collective-permute-start | bytes 786440 | tf_op jit(solution)/shard_map/ppermute | solution.py:448
  83.7 1.6 %collective-permute-start.9 = (f32[2,128,128]{2,1,0:T(8,128)S(1)}, f32[2,128,128]{2,1,0:T(8,128)S(1)}, u32[]{:S(2)}, u32[]{:S(2)}) collective-permute-start(f32[2,128,128]{2,1,0:T(8,128)S(1)} %get-tuple-element.55), channel_id=1, source_target_pairs={{0,128},{32,160},{64,192},{96,224},{128,0},{160,32},{192,64},{224,... | collective-permute-start | bytes 393224 | tf_op jit(solution)/shard_map/ppermute | solution.py:444
  85.3 3.9 %collective-permute-done.25.bp = f32[4,128,128]{2,1,0:T(8,128)S(1)} collective-permute-done((f32[4,128,128]{2,1,0:T(8,128)S(1)}, f32[4,128,128]{2,1,0:T(8,128)S(1)}, u32[]{:S(2)}, u32[]{:S(2)}) %collective-permute-start.25) | collective-permute-done | bytes 262176 | tf_op jit(solution)/shard_map/ppermute | solution.py:448
  89.8 2.1 %edges.6 = (f32[4,128,128]{2,1,0:T(8,128)S(1)}, f32[4,128,128]{2,1,0:T(8,128)S(1)}, f32[4,128,128]{2,1,0:T(8,128)S(1)}) custom-call(s32[2,128]{1,0:T(2,128)S(1)} %pad_add_fusion.slots_any.refs_0_, s32[1]{0:T(128)S(6)} %copy.10.count.refs_1_, bf16[16,256,512]{2,1,0:T(8,128)(2,1)S(1)} %get-tuple-element.40.refs_2_, ...), custom_call_target="tpu_custom_call" | custom-call | flops 805306368 | bytes 6291456 | tf_op jit(solution)/shard_map/edges/pallas_call | solution.py:355
  92.0 1.8 %edges.7 = (f32[4,128,128]{2,1,0:T(8,128)S(1)}, f32[4,128,128]{2,1,0:T(8,128)S(1)}) custom-call(s32[2,128]{1,0:T(2,128)S(1)} %pad_add_fusion.slots_any.refs_0_, s32[1]{0:T(128)S(6)} %copy.10.count.refs_1_, bf16[16,256,512]{2,1,0:T(8,128)(2,1)S(1)} %get-tuple-element.40.refs_2_, f32[4,16,128]{2,1,0:T(8,128)S(1)} %get-tuple-element.41.refs_3_.refs_9_, ...), custom_call_target="tpu_custom_call" | custom-call | flops 536870912 | bytes 6291456 | tf_op jit(solution)/shard_map/edges/pallas_call | solution.py:355
  93.8 2.7 %collective-permute-start.24 = (f32[4,128,128]{2,1,0:T(8,128)S(1)}, f32[4,128,128]{2,1,0:T(8,128)S(1)}, u32[]{:S(2)}, u32[]{:S(2)}) collective-permute-start(f32[4,128,128]{2,1,0:T(8,128)S(1)} %get-tuple-element.45.refs_9_), channel_id=1, source_target_pairs={{0,28},{1,29},{2,30},{3,31},{4,0},{5,1},{6,2},{7,3},{8,4},{9,5},{1... | collective-permute-start | bytes 786440 | tf_op jit(solution)/shard_map/ppermute | solution.py:448
  96.5 2.5 %collective-permute-start.28 = (f32[4,128,128]{2,1,0:T(8,128)S(1)}, f32[4,128,128]{2,1,0:T(8,128)S(1)}, u32[]{:S(2)}, u32[]{:S(2)}) collective-permute-start(f32[4,128,128]{2,1,0:T(8,128)S(1)} %get-tuple-element.51), channel_id=1, source_target_pairs={{0,8},{1,9},{2,10},{3,11},{4,12},{5,13},{6,14},{7,15},{8,16},{9,17... | collective-permute-start | bytes 786440 | tf_op jit(solution)/shard_map/ppermute | solution.py:448
  99.1 1.7 %collective-permute-start.29 = (f32[4,128,128]{2,1,0:T(8,128)S(1)}, f32[4,128,128]{2,1,0:T(8,128)S(1)}, u32[]{:S(2)}, u32[]{:S(2)}) collective-permute-start(f32[4,128,128]{2,1,0:T(8,128)S(1)} %get-tuple-element.52), channel_id=1, source_target_pairs={{0,24},{1,25},{2,26},{3,27},{4,28},{5,29},{6,30},{7,31},{8,0},{9,1... | collective-permute-start | bytes 786440 | tf_op jit(solution)/shard_map/ppermute | solution.py:448
  101.5 3.7 %collective-permute-done.23.b_ref = f32[4,128,128]{2,1,0:T(8,128)S(1)} collective-permute-done((f32[4,128,128]{2,1,0:T(8,128)S(1)}, f32[4,128,128]{2,1,0:T(8,128)S(1)}, u32[]{:S(2)}, u32[]{:S(2)}) %collective-permute-start.23) | collective-permute-done | bytes 262176 | tf_op jit(solution)/shard_map/ppermute | solution.py:448
  106.2 5.9 %collective-permute-done.28.a_ref = f32[4,128,128]{2,1,0:T(8,128)S(1)} collective-permute-done((f32[4,128,128]{2,1,0:T(8,128)S(1)}, f32[4,128,128]{2,1,0:T(8,128)S(1)}, u32[]{:S(2)}, u32[]{:S(2)}) %collective-permute-start.28) | collective-permute-done | bytes 262176 | tf_op jit(solution)/shard_map/ppermute | solution.py:448
  112.1 2.0 %collective-permute-done.29.b_ref = f32[4,128,128]{2,1,0:T(8,128)S(1)} collective-permute-done((f32[4,128,128]{2,1,0:T(8,128)S(1)}, f32[4,128,128]{2,1,0:T(8,128)S(1)}, u32[]{:S(2)}, u32[]{:S(2)}) %collective-permute-start.29) | collective-permute-done | bytes 262176 | tf_op jit(solution)/shard_map/ppermute | solution.py:448
  (48 shorter events, 10.3 us)
Async XLA Ops:
  0.6 5.5 %collective-permute-start.11 = (f32[2,128,128]{2,1,0:T(8,128)}, f32[2,128,128]{2,1,0:T(8,128)S(1)}, u32[]{:S(2)}, u32[]{:S(2)}) collective-permute-start(f32[2,128,128]{2,1,0:T(8,128)} %refs_0_.3), channel_id=1, source_target_pairs={{0,1},{1,0},{2,3},{3,2},{4,5},{5,4},{6,7},{7,6},{8,9},{9,8},{10,11... | collective-permute-start | bytes 393224 | tf_op jit(solution)/shard_map/ppermute | solution.py:451
  7.1 12.9 %collective-permute-start.12 = (f32[4,128,128]{2,1,0:T(8,128)S(1)}, f32[4,128,128]{2,1,0:T(8,128)S(1)}, u32[]{:S(2)}, u32[]{:S(2)}) collective-permute-start(f32[4,128,128]{2,1,0:T(8,128)S(1)} %pack.2), channel_id=1, source_target_pairs={{0,3},{1,2},{2,1},{3,0},{4,7},{5,6},{6,5},{7,4},{8,11},{9,10},{10,... | collective-permute-start | bytes 786440 | tf_op jit(solution)/shard_map/ppermute | solution.py:451
  10.2 6.4 %collective-permute-start.1 = (f32[2,128,128]{2,1,0:T(8,128)}, f32[2,128,128]{2,1,0:T(8,128)S(1)}, u32[]{:S(2)}, u32[]{:S(2)}) collective-permute-start(f32[2,128,128]{2,1,0:T(8,128)} %refs_0_.3), channel_id=1, source_target_pairs={{0,64},{32,96},{64,128},{96,160},{128,192},{160,224},{192,0},{224,... | collective-permute-start | bytes 393224 | tf_op jit(solution)/shard_map/ppermute | solution.py:444
  11.7 7.1 %collective-permute-start.3 = (f32[2,128,128]{2,1,0:T(8,128)}, f32[2,128,128]{2,1,0:T(8,128)S(1)}, u32[]{:S(2)}, u32[]{:S(2)}) collective-permute-start(f32[2,128,128]{2,1,0:T(8,128)} %refs_0_.3), channel_id=1, source_target_pairs={{0,128},{32,160},{64,192},{96,224},{128,0},{160,32},{192,64},{224,... | collective-permute-start | bytes 393224 | tf_op jit(solution)/shard_map/ppermute | solution.py:444
  12.8 6.6 %collective-permute-start.5 = (f32[2,128,128]{2,1,0:T(8,128)}, f32[2,128,128]{2,1,0:T(8,128)S(1)}, u32[]{:S(2)}, u32[]{:S(2)}) collective-permute-start(f32[2,128,128]{2,1,0:T(8,128)} %refs_0_.3), channel_id=1, source_target_pairs={{0,192},{32,224},{64,0},{96,32},{128,64},{160,96},{192,128},{224,1... | collective-permute-start | bytes 393224 | tf_op jit(solution)/shard_map/ppermute | solution.py:444
  14.9 10.9 %collective-permute-start = (f32[2,128,128]{2,1,0:T(8,128)}, f32[2,128,128]{2,1,0:T(8,128)S(1)}, u32[]{:S(2)}, u32[]{:S(2)}) collective-permute-start(f32[2,128,128]{2,1,0:T(8,128)} %refs_0_.3), channel_id=1, source_target_pairs={{0,32},{32,0},{64,96},{96,64},{128,160},{160,128},{192,224},{224,1... | collective-permute-start | bytes 393224 | tf_op jit(solution)/shard_map/ppermute | solution.py:444
  16.6 9.3 %collective-permute-start.2 = (f32[2,128,128]{2,1,0:T(8,128)S(1)}, f32[2,128,128]{2,1,0:T(8,128)S(1)}, u32[]{:S(2)}, u32[]{:S(2)}) collective-permute-start(f32[2,128,128]{2,1,0:T(8,128)S(1)} %collective-permute-done.1.refs_2_), channel_id=1, source_target_pairs={{0,32},{32,0},{64,96},{96,64},{128,160},{160,128},{192,224},{224,1... | collective-permute-start | bytes 393224 | tf_op jit(solution)/shard_map/ppermute | solution.py:444
  18.8 7.1 %collective-permute-start.4 = (f32[2,128,128]{2,1,0:T(8,128)S(1)}, f32[2,128,128]{2,1,0:T(8,128)S(1)}, u32[]{:S(2)}, u32[]{:S(2)}) collective-permute-start(f32[2,128,128]{2,1,0:T(8,128)S(1)} %collective-permute-done.3.refs_4_), channel_id=1, source_target_pairs={{0,32},{32,0},{64,96},{96,64},{128,160},{160,128},{192,224},{224,1... | collective-permute-start | bytes 393224 | tf_op jit(solution)/shard_map/ppermute | solution.py:444
  19.4 6.5 %collective-permute-start.6 = (f32[2,128,128]{2,1,0:T(8,128)S(1)}, f32[2,128,128]{2,1,0:T(8,128)S(1)}, u32[]{:S(2)}, u32[]{:S(2)}) collective-permute-start(f32[2,128,128]{2,1,0:T(8,128)S(1)} %collective-permute-done.5.refs_6_), channel_id=1, source_target_pairs={{0,32},{32,0},{64,96},{96,64},{128,160},{160,128},{192,224},{224,1... | collective-permute-start | bytes 393224 | tf_op jit(solution)/shard_map/ppermute | solution.py:444
  20.1 20.2 %collective-permute-start.14 = (f32[6,128,128]{2,1,0:T(8,128)S(1)}, f32[6,128,128]{2,1,0:T(8,128)S(1)}, u32[]{:S(2)}, u32[]{:S(2)}) collective-permute-start(f32[6,128,128]{2,1,0:T(8,128)S(1)} %pack.3.refs_4_), channel_id=1, source_target_pairs={{0,64},{32,96},{64,128},{96,160},{128,192},{160,224},{192,0},{224,... | collective-permute-start | bytes 1179656 | tf_op jit(solution)/shard_map/ppermute | solution.py:444
  22.1 3.7 %copy-start = (f32[4,128,128]{2,1,0:T(8,128)S(1)}, f32[4,128,128]{2,1,0:T(8,128)}, u32[]{:S(2)}) copy-start(f32[4,128,128]{2,1,0:T(8,128)} %refs_10_.1) | copy-start | bytes 786436
  22.1 3.7 %copy-start.1 = (s32[16,2]{0,1:T(2,128)S(1)}, s32[16,2]{0,1:T(2,128)}, u32[]{:S(2)}) copy-start(s32[16,2]{0,1:T(2,128)} %param.8) | copy-start | bytes 388
  36.4 21.6 %collective-permute-start.7 = (f32[8,128,128]{2,1,0:T(8,128)S(1)}, f32[8,128,128]{2,1,0:T(8,128)S(1)}, u32[]{:S(2)}, u32[]{:S(2)}) collective-permute-start(f32[8,128,128]{2,1,0:T(8,128)S(1)} %get-tuple-element.35), channel_id=1, source_target_pairs={{0,32},{32,0},{64,96},{96,64},{128,160},{160,128},{192,224},{224,1... | collective-permute-start | bytes 1572872 | tf_op jit(solution)/shard_map/ppermute | solution.py:444
  36.7 13.5 %collective-permute-start.16 = (f32[6,128,128]{2,1,0:T(8,128)S(1)}, f32[6,128,128]{2,1,0:T(8,128)S(1)}, u32[]{:S(2)}, u32[]{:S(2)}) collective-permute-start(f32[6,128,128]{2,1,0:T(8,128)S(1)} %pack.3.refs_4_), channel_id=1, source_target_pairs={{0,128},{32,160},{64,192},{96,224},{128,0},{160,32},{192,64},{224,... | collective-permute-start | bytes 1179656 | tf_op jit(solution)/shard_map/ppermute | solution.py:444
  38.5 19.4 %collective-permute-start.18 = (f32[6,128,128]{2,1,0:T(8,128)S(1)}, f32[6,128,128]{2,1,0:T(8,128)S(1)}, u32[]{:S(2)}, u32[]{:S(2)}) collective-permute-start(f32[6,128,128]{2,1,0:T(8,128)S(1)} %pack.3.refs_4_), channel_id=1, source_target_pairs={{0,192},{32,224},{64,0},{96,32},{128,64},{160,96},{192,128},{224,1... | collective-permute-start | bytes 1179656 | tf_op jit(solution)/shard_map/ppermute | solution.py:444
  40.3 17.9 %collective-permute-start.13 = (f32[6,128,128]{2,1,0:T(8,128)S(1)}, f32[6,128,128]{2,1,0:T(8,128)S(1)}, u32[]{:S(2)}, u32[]{:S(2)}) collective-permute-start(f32[6,128,128]{2,1,0:T(8,128)S(1)} %pack.3.refs_4_), channel_id=1, source_target_pairs={{0,32},{32,0},{64,96},{96,64},{128,160},{160,128},{192,224},{224,1... | collective-permute-start | bytes 1179656 | tf_op jit(solution)/shard_map/ppermute | solution.py:444
  40.3 18.9 %collective-permute-start.15 = (f32[6,128,128]{2,1,0:T(8,128)S(1)}, f32[6,128,128]{2,1,0:T(8,128)S(1)}, u32[]{:S(2)}, u32[]{:S(2)}) collective-permute-start(f32[6,128,128]{2,1,0:T(8,128)S(1)} %collective-permute-done.14.refs_6_), channel_id=1, source_target_pairs={{0,32},{32,0},{64,96},{96,64},{128,160},{160,128},{192,224},{224,1... | collective-permute-start | bytes 1179656 | tf_op jit(solution)/shard_map/ppermute | solution.py:444
  50.3 11.9 %collective-permute-start.17 = (f32[6,128,128]{2,1,0:T(8,128)S(1)}, f32[6,128,128]{2,1,0:T(8,128)S(1)}, u32[]{:S(2)}, u32[]{:S(2)}) collective-permute-start(f32[6,128,128]{2,1,0:T(8,128)S(1)} %collective-permute-done.16.refs_8_), channel_id=1, source_target_pairs={{0,32},{32,0},{64,96},{96,64},{128,160},{160,128},{192,224},{224,1... | collective-permute-start | bytes 1179656 | tf_op jit(solution)/shard_map/ppermute | solution.py:444
  58.0 4.2 %collective-permute-start.19 = (f32[6,128,128]{2,1,0:T(8,128)S(1)}, f32[6,128,128]{2,1,0:T(8,128)S(1)}, u32[]{:S(2)}, u32[]{:S(2)}) collective-permute-start(f32[6,128,128]{2,1,0:T(8,128)S(1)} %collective-permute-done.18.refs_10_), channel_id=1, source_target_pairs={{0,32},{32,0},{64,96},{96,64},{128,160},{160,128},{192,224},{224,1... | collective-permute-start | bytes 1179656 | tf_op jit(solution)/shard_map/ppermute | solution.py:444
  58.0 9.5 %collective-permute-start.20 = (f32[4,136,128]{2,1,0:T(8,128)S(1)}, f32[4,136,128]{2,1,0:T(8,128)S(1)}, u32[]{:S(2)}, u32[]{:S(2)}) collective-permute-start(f32[4,136,128]{2,1,0:T(8,128)S(1)} %get-tuple-element.31.fx.refs_5_), channel_id=1, source_target_pairs={{0,1},{1,0},{2,3},{3,2},{4,5},{5,4},{6,7},{7,6},{8,9},{9,8},{10,11... | collective-permute-start | bytes 835592 | tf_op jit(solution)/shard_map/ppermute | solution.py:451
  58.2 16.2 %collective-permute-start.21 = (f32[4,136,128]{2,1,0:T(8,128)S(1)}, f32[4,136,128]{2,1,0:T(8,128)S(1)}, u32[]{:S(2)}, u32[]{:S(2)}) collective-permute-start(f32[4,136,128]{2,1,0:T(8,128)S(1)} %get-tuple-element.31.fx.refs_5_), channel_id=1, source_target_pairs={{0,3},{1,2},{2,1},{3,0},{4,7},{5,6},{6,5},{7,4},{8,11},{9,10},{10,... | collective-permute-start | bytes 835592 | tf_op jit(solution)/shard_map/ppermute | solution.py:451
  59.2 15.1 %collective-permute-start.22 = (f32[4,136,128]{2,1,0:T(8,128)S(1)}, f32[4,136,128]{2,1,0:T(8,128)S(1)}, u32[]{:S(2)}, u32[]{:S(2)}) collective-permute-start(f32[4,136,128]{2,1,0:T(8,128)S(1)} %get-tuple-element.31.fx.refs_5_), channel_id=1, source_target_pairs={{0,2},{1,3},{2,0},{3,1},{4,6},{5,7},{6,4},{7,5},{8,10},{9,11},{10,... | collective-permute-start | bytes 835592 | tf_op jit(solution)/shard_map/ppermute | solution.py:451
  77.2 12.0 %collective-permute-start.25 = (f32[4,128,128]{2,1,0:T(8,128)S(1)}, f32[4,128,128]{2,1,0:T(8,128)S(1)}, u32[]{:S(2)}, u32[]{:S(2)}) collective-permute-start(f32[4,128,128]{2,1,0:T(8,128)S(1)} %get-tuple-element.50), channel_id=1, source_target_pairs={{0,4},{1,5},{2,6},{3,7},{4,8},{5,9},{6,10},{7,11},{8,12},{9,13},{1... | collective-permute-start | bytes 786440 | tf_op jit(solution)/shard_map/ppermute | solution.py:448
  79.2 14.5 %collective-permute-start.26 = (f32[4,128,128]{2,1,0:T(8,128)S(1)}, f32[4,128,128]{2,1,0:T(8,128)S(1)}, u32[]{:S(2)}, u32[]{:S(2)}) collective-permute-start(f32[4,128,128]{2,1,0:T(8,128)S(1)} %get-tuple-element.42.refs_9_), channel_id=1, source_target_pairs={{0,28},{1,29},{2,30},{3,31},{4,0},{5,1},{6,2},{7,3},{8,4},{9,5},{1... | collective-permute-start | bytes 786440 | tf_op jit(solution)/shard_map/ppermute | solution.py:448
  83.2 13.2 %collective-permute-start.27 = (f32[4,128,128]{2,1,0:T(8,128)S(1)}, f32[4,128,128]{2,1,0:T(8,128)S(1)}, u32[]{:S(2)}, u32[]{:S(2)}) collective-permute-start(f32[4,128,128]{2,1,0:T(8,128)S(1)} %edges.4.refs_9_), channel_id=1, source_target_pairs={{0,8},{1,9},{2,10},{3,11},{4,12},{5,13},{6,14},{7,15},{8,16},{9,17... | collective-permute-start | bytes 786440 | tf_op jit(solution)/shard_map/ppermute | solution.py:459
  83.2 13.3 %collective-permute-start.10 = (f32[2,128,128]{2,1,0:T(8,128)S(1)}, f32[2,128,128]{2,1,0:T(8,128)S(1)}, u32[]{:S(2)}, u32[]{:S(2)}) collective-permute-start(f32[2,128,128]{2,1,0:T(8,128)S(1)} %get-tuple-element.54), channel_id=1, source_target_pairs={{0,192},{32,224},{64,0},{96,32},{128,64},{160,96},{192,128},{224,1... | collective-permute-start | bytes 393224 | tf_op jit(solution)/shard_map/ppermute | solution.py:444
  83.7 15.4 %collective-permute-start.9 = (f32[2,128,128]{2,1,0:T(8,128)S(1)}, f32[2,128,128]{2,1,0:T(8,128)S(1)}, u32[]{:S(2)}, u32[]{:S(2)}) collective-permute-start(f32[2,128,128]{2,1,0:T(8,128)S(1)} %get-tuple-element.55), channel_id=1, source_target_pairs={{0,128},{32,160},{64,192},{96,224},{128,0},{160,32},{192,64},{224,... | collective-permute-start | bytes 393224 | tf_op jit(solution)/shard_map/ppermute | solution.py:444
  89.2 11.6 %collective-permute-start.8 = (f32[2,128,128]{2,1,0:T(8,128)S(1)}, f32[2,128,128]{2,1,0:T(8,128)S(1)}, u32[]{:S(2)}, u32[]{:S(2)}) collective-permute-start(f32[2,128,128]{2,1,0:T(8,128)S(1)} %get-tuple-element.53.refs_1_), channel_id=1, source_target_pairs={{0,64},{32,96},{64,128},{96,160},{128,192},{160,224},{192,0},{224,... | collective-permute-start | bytes 393224 | tf_op jit(solution)/shard_map/ppermute | solution.py:444
  93.8 11.4 %collective-permute-start.24 = (f32[4,128,128]{2,1,0:T(8,128)S(1)}, f32[4,128,128]{2,1,0:T(8,128)S(1)}, u32[]{:S(2)}, u32[]{:S(2)}) collective-permute-start(f32[4,128,128]{2,1,0:T(8,128)S(1)} %get-tuple-element.45.refs_9_), channel_id=1, source_target_pairs={{0,28},{1,29},{2,30},{3,31},{4,0},{5,1},{6,2},{7,3},{8,4},{9,5},{1... | collective-permute-start | bytes 786440 | tf_op jit(solution)/shard_map/ppermute | solution.py:448
  96.4 8.7 %collective-permute-start.23 = (f32[4,128,128]{2,1,0:T(8,128)S(1)}, f32[4,128,128]{2,1,0:T(8,128)S(1)}, u32[]{:S(2)}, u32[]{:S(2)}) collective-permute-start(f32[4,128,128]{2,1,0:T(8,128)S(1)} %get-tuple-element.44), channel_id=1, source_target_pairs={{0,4},{1,5},{2,6},{3,7},{4,8},{5,9},{6,10},{7,11},{8,12},{9,13},{1... | collective-permute-start | bytes 786440 | tf_op jit(solution)/shard_map/ppermute | solution.py:448
  96.5 15.5 %collective-permute-start.28 = (f32[4,128,128]{2,1,0:T(8,128)S(1)}, f32[4,128,128]{2,1,0:T(8,128)S(1)}, u32[]{:S(2)}, u32[]{:S(2)}) collective-permute-start(f32[4,128,128]{2,1,0:T(8,128)S(1)} %get-tuple-element.51), channel_id=1, source_target_pairs={{0,8},{1,9},{2,10},{3,11},{4,12},{5,13},{6,14},{7,15},{8,16},{9,17... | collective-permute-start | bytes 786440 | tf_op jit(solution)/shard_map/ppermute | solution.py:448
  99.1 15.0 %collective-permute-start.29 = (f32[4,128,128]{2,1,0:T(8,128)S(1)}, f32[4,128,128]{2,1,0:T(8,128)S(1)}, u32[]{:S(2)}, u32[]{:S(2)}) collective-permute-start(f32[4,128,128]{2,1,0:T(8,128)S(1)} %get-tuple-element.52), channel_id=1, source_target_pairs={{0,24},{1,25},{2,26},{3,27},{4,28},{5,29},{6,30},{7,31},{8,0},{9,1... | collective-permute-start | bytes 786440 | tf_op jit(solution)/shard_map/ppermute | solution.py:448

commit v3 on v2

--- a/solution.py
+++ b/solution.py
@@ -107,12 +107,13 @@
 def forward_kernel(nodes, prod_child, *refs):
     n = nodes
     got = refs[:n]
-    w_ref, bias, up, sv, fx, e_ref, r_ref, pk, lv, whl, shl = refs[n:]
+    w_ref, bias, up, sv_hbm, fx, e_ref, r_ref, pk, lv, whl, shl, sv, sems = refs[n:]
     pg, g, s = e_ref.shape
+    qd = up.shape[0]
+    each = lv.shape[0] // n
     for k, (dx, dc) in enumerate(hops(n)):
         src = node_at(-dx, -dc, n)
-        each = got[k].shape[0]
-        lv[pl.ds(src * each, each)] = got[k][...]
+        lv[pl.ds(src * each, each)] = got[k][0:each]
 
     def product(p, carry):
         x = lv[prod_child[0, p]] + lv[prod_child[1, p]]
@@ -122,29 +123,43 @@
         return carry
 
     lax.fori_loop(0, pg, product, 0, unroll=2)
-    for q in range(up.shape[0]):
-        biased = pk[...] + bias[q * pg : (q + 1) * pg]
+    tops = []
+    for q in range(qd):
+        here = slice(q * pg, (q + 1) * pg)
+        biased = pk[...] + bias[here]
         top = jnp.max(biased, axis=0, keepdims=True)
-        r_ref[q * pg : (q + 1) * pg] = jnp.exp(biased - top)
-
-        def scaled(c, carry, q=q):
-            at = pl.ds(pl.multiple_of(c * g, g), g)
+        r_ref[here] = jnp.exp(biased - top)
+        tops.append(top)
+
+    def scaled(q):
+        for c in range(pg):
+            at = slice(c * g, (c + 1) * g)
             hi, lo = parts(w_ref[q, c])
             whl[q % 2, 0:g, at] = hi
             whl[q % 2, g : 2 * g, at] = lo
-            hi, lo = parts(e_ref[c] * r_ref[pl.ds(q * pg + c, 1), :])
+            k = q * pg + c
+            hi, lo = parts(e_ref[c] * r_ref[k : k + 1, :])
             shl[q % 2, at, 0:s] = hi
             shl[q % 2, at, s : 2 * s] = lo
-            return carry
-
-        lax.fori_loop(0, pg, scaled, 0, unroll=2)
+
+    scaled(0)
+    copies = []
+    for q in range(qd):
         total = quadrants(jnp.dot(whl[q % 2], shl[q % 2], preferred_element_type=f32))
-        sv[q] = top + jnp.log(total)
+        if q + 1 < qd:
+            scaled(q + 1)
+        sv[q] = tops[q] + jnp.log(total)
         fx[q, 0:g] = up[q] / total
-        fx[q, g:] = jnp.broadcast_to(top, (8, s))
-
-
-def forward(prod_child, got, w, bias, up):
+        fx[q, g:] = jnp.broadcast_to(tops[q], (8, s))
+        copies.append(pltpu.make_async_copy(sv.at[q], sv_hbm.at[q], sems.at[q]))
+        if q > 0:
+            copies[q - 1].start()
+    copies[-1].start()
+    for copy in copies:
+        copy.wait()
+
+
+def forward(prod_child, got, w, bias, up, ng):
     nodes = len(got)
     qd, g, s = up.shape
     pg = prod_child.shape[1]
@@ -158,11 +173,13 @@
             jax.ShapeDtypeStruct((pg, s), f32),
         ),
         in_specs=[pl.BlockSpec(memory_space=SMEM)] + vmem_specs(nodes + 3),
-        out_specs=tuple(vmem_specs(5)),
+        out_specs=(pl.BlockSpec(memory_space=pltpu.HBM), *vmem_specs(4)),
         scratch_shapes=[
-            VMEM((got[0].shape[0] * nodes, g, s), f32),
+            VMEM((ng, g, s), f32),
             VMEM((2, 2 * g, pg * g), bf16),
             VMEM((2, pg * g, 2 * s), bf16),
+            VMEM((qd, g, s), f32),
+            pltpu.SemaphoreType.DMA((qd,)),
         ],
         compiler_params=pltpu.CompilerParams(vmem_limit_bytes=20 << 20),
         cost_estimate=pl.CostEstimate(
@@ -323,10 +340,13 @@
             top = fxs[t][q, g : g + 1]
             here = slice(q * pg, (q + 1) * pg)
             r[t, here, :] = jnp.exp((pk[t] + bias[here, :]) - top)
-    for (d, k0, n, keep), out in zip(plan, outs):
-        base = ((z + d + depth) % depth * ROWS + y) * keep + k0
-        for k in range(n):
-            b = base + k
+    for ds, out in zip(plan, outs):
+        keep = out.shape[0] // len(ds)
+        places = []
+        for d in ds:
+            first = ((z + d + depth) % depth * ROWS + y) * keep
+            places += [first + k for k in range(keep)]
+        for k, b in enumerate(places):
             c, q = slots[0, b], slots[1, b]
             live = (b < count[0]).astype(f32)
             for t in range(rows):
@@ -334,8 +354,8 @@
                 hi, lo = parts(fxs[t][q, 0:g] * (r[t, pl.ds(q * pg + c, 1), :] * live))
                 lhs[k, 0:g, at] = hi
                 lhs[k, g : 2 * g, at] = lo
-        for k in range(n):
-            c = slots[0, base + k]
+        for k, b in enumerate(places):
+            c = slots[0, b]
             out[k] = quadrants(
                 lax.dot_general(
                     lhs[k], ehl[c], (((1,), (1,)), ((), ())), preferred_element_type=f32
@@ -343,29 +363,29 @@
             )
 
 
-def edges(slots, count, ehl, pk, bias, fxs, token, plan):
+def edges(slots, count, ehl, pk, bias, fxs, token, plan, keep):
     g = ehl.shape[1] // 2
     pg, width = pk.shape[1], ehl.shape[2]
     qd = fxs[0].shape[0]
-    total = sum(n for _, _, n, _ in plan)
+    counts = [keep * len(ds) for ds in plan]
 
     def kernel(*refs):
         edges_kernel(plan, *refs)
 
     return pl.pallas_call(
         kernel,
-        out_shape=[jax.ShapeDtypeStruct((n, g, g), f32) for _, _, n, _ in plan],
+        out_shape=[jax.ShapeDtypeStruct((n, g, g), f32) for n in counts],
         in_specs=[pl.BlockSpec(memory_space=SMEM)] * 2
         + vmem_specs(3 + len(fxs))
         + [pl.BlockSpec(memory_space=pl.ANY)],
         out_specs=vmem_specs(len(plan)),
         scratch_shapes=[
             VMEM((len(fxs), qd * pg, width // len(fxs)), f32),
-            VMEM((max(n for _, _, n, _ in plan), 2 * g, width), bf16),
+            VMEM((max(counts), 2 * g, width), bf16),
         ],
         compiler_params=pltpu.CompilerParams(vmem_limit_bytes=20 << 20),
         cost_estimate=pl.CostEstimate(
-            flops=2 * total * 4 * g * g * width, bytes_accessed=6 << 20, transcendentals=0
+            flops=2 * sum(counts) * 4 * g * g * width, bytes_accessed=6 << 20, transcendentals=0
         ),
         name="edges",
     )(slots, count, ehl, pk, bias, *fxs, token)
@@ -373,8 +393,9 @@
 
 def join_kernel(ap, am, bp, bm, c_ref, outp, outm):
     first = (lax.axis_index("nodes") % CORES == 0).astype(f32)
-    outp[...] = (ap[...] + bp[...]) + c_ref[...] * first
-    outm[...] = (am[...] + bm[...]) + c_ref[...] * (1.0 - first)
+    n = ap.shape[0]
+    outp[...] = (ap[...] + bp[0:n]) + c_ref[...] * first
+    outm[...] = (am[...] + bm[0:n]) + c_ref[...] * (1.0 - first)
 
 
 def join(ap, am, bp, bm, c):
@@ -395,7 +416,7 @@
     copy = pltpu.make_async_copy(own, w, sem)
     copy.start()
     copy.wait()
-    near[...] = w[...] * (a_ref[...] + b_ref[...] + c_ref[...])
+    near[...] = w[...] * (a_ref[...] + b_ref[keep:] + c_ref[keep:])
 
 
 def weigh_near(w, a, b, c):
@@ -473,7 +494,7 @@
     pieces = gather(packed)
 
     w, bias = fold(slots, block_count, block_weight, pg, qd)
-    sum_values, fx, e, r, pk = forward(prod_child, got, w, bias, upper_flow)
+    sum_values, fx, e, r, pk = forward(prod_child, [pair] + got[1:], w, bias, upper_flow, ng)
     fxs = [fx] + [swap(fx, t) for t in (1, 3, 2)]
     *mine, give = backward(prod_child, w, fx, r, e, nodes, ng)
     given = move(give, 0, 1)
@@ -481,23 +502,22 @@
     flows = [a + given[dx * k : (dx + 1) * k] for dx, a in enumerate(mine)]
     ehl, pks = spread(prod_child, e, pk, pieces, hops(nodes), nodes, flows[1])
 
-    def part(token, *ds):
-        plan = [(d, 0, keep, keep) for d in ds]
-        return edges(slots, block_count, ehl, pks, bias, fxs, token, plan)
-
-    (e4,) = part(pks, far)
+    def part(token, *plan):
+        return edges(slots, block_count, ehl, pks, bias, fxs, token, plan, keep)
+
+    (e4,) = part(pks, (far,))
     r4 = shift_by_core(e4, 2)
-    e3p, e3m = part(e4, 3, -3)
-    r3p, r3m = shift(e3p, 1), shift(e3m, -1)
-    e1p, e1m, e0 = part(e3m, 1, -1, 0)
-    r1p, r1m = shift(e1p, 1), shift(e1m, -1)
-    e2p, e2m = part(e1m, 2, -2)
-    c2p, c2m = join(e2p, e2m, r3p, r3m, r4)
+    (ep,) = part(e4, (3, 1))
+    rp = shift(ep, 1)
+    (em,) = part(ep, (-3, -1))
+    rm = shift(em, -1)
+    e2p, e2m, e0 = part(em, (2,), (-2,), (0,))
+    c2p, c2m = join(e2p, e2m, rp, rm, r4)
     r2p, r2m = shift(c2p, 2), shift(c2m, -2)
     leaf_flow = functools.reduce(
         jnp.add, [flows[0]] + [move(flows[dx], dx) for dx in range(1, chips)]
     )
-    near, own = weigh_near(block_weight, e0, r1p, r1m)
+    near, own = weigh_near(block_weight, e0, rp, rm)
     param_flow = weigh_last(near, own, r2p, r2m)
     return sum_values, leaf_flow, param_flow
 

time: 116 us -> 120 us (1.034)
  the two profiles are of different devices: /device:TPU:2 before, /device:TPU:65 now
where the time goes in v3:
time: 120 us
  waiting for transfers between devices  55.5 us (46%)
  starting transfers between devices  38.1 us (32%)
  Pallas kernels  23 us (19%)
  between operations  1.5 us (1%)
  other arithmetic  1.43 us (1%)
    ppermute x18, starting transfers between devices, move(): return lax.ppermute(a, 'nodes', [(n, to(n)) for n in range(nodes)])  23.2 us
    ppermute x1, waiting for transfers between devices, shift_by_core(): return lax.ppermute(a, ('nodes', 'batch'), pairs)  16.7 us
    ppermute x18, waiting for transfers between devices, move(): return lax.ppermute(a, 'nodes', [(n, to(n)) for n in range(nodes)])  15 us
    ppermute x5, waiting for transfers between devices, swap(): return lax.ppermute(a, 'batch', [(b, b ^ mask) for b in range(batch)])  13.4 us
    ppermute x4, waiting for transfers between devices, shift(): return lax.ppermute(a, 'batch', [(b, to(b)) for b in range(batch)])  10.4 us
    ppermute x5, starting transfers between devices, swap(): return lax.ppermute(a, 'batch', [(b, b ^ mask) for b in range(batch)])  7.46 us
    pallas_call x4, Pallas kernels, edges(): pl.pallas_call(kernel, out_shape=[jax.ShapeDtypeStruct((n, g, g), f32) fo...  6.13 us
    pallas_call x1, Pallas kernels, forward(): pl.pallas_call(functools.partial(forward_kernel, nodes), out_shape=(jax.S...  4.66 us
  transfers between devices with their start and end apart: 28, of which 8 were waited for; matrix products, arithmetic and copies ran while one was open for 1% of the time, Pallas kernels for 16%

profile of v3, /device:TPU:65, one launch (start us, length us, event | category | flops | bytes accessed | tf_op | source)
XLA Modules:
  0.0 119.5 jit_solution(16686644495101718546)
XLA Ops:
  0.6 1.4 %collective-permute-start = (f32[2,128,128]{2,1,0:T(8,128)}, f32[2,128,128]{2,1,0:T(8,128)S(1)}, u32[]{:S(2)}, u32[]{:S(2)}) collective-permute-start(f32[2,128,128]{2,1,0:T(8,128)} %refs_0_.1), channel_id=1, source_target_pairs={{0,1},{1,0},{2,3},{3,2},{4,5},{5,4},{6,7},{7,6},{8,9},{9,8},{10,11... | collective-permute-start | bytes 393224 | tf_op jit(solution)/shard_map/ppermute | solution.py:472
  2.0 3.3 %collective-permute-done.refs_1_.refs_0_ = f32[2,128,128]{2,1,0:T(8,128)S(1)} collective-permute-done((f32[2,128,128]{2,1,0:T(8,128)}, f32[2,128,128]{2,1,0:T(8,128)S(1)}, u32[]{:S(2)}, u32[]{:S(2)}) %collective-permute-start) | collective-permute-done | bytes 131104 | tf_op jit(solution)/shard_map/ppermute | solution.py:472
  6.2 2.8 %collective-permute-start.12 = (f32[4,128,128]{2,1,0:T(8,128)S(1)}, f32[4,128,128]{2,1,0:T(8,128)S(1)}, u32[]{:S(2)}, u32[]{:S(2)}) collective-permute-start(f32[4,128,128]{2,1,0:T(8,128)S(1)} %pack.2.refs_0_), channel_id=1, source_target_pairs={{0,3},{1,2},{2,1},{3,0},{4,7},{5,6},{6,5},{7,4},{8,11},{9,10},{10,... | collective-permute-start | bytes 786440 | tf_op jit(solution)/shard_map/ppermute | solution.py:472
  9.1 1.2 %collective-permute-start.2 = (f32[2,128,128]{2,1,0:T(8,128)}, f32[2,128,128]{2,1,0:T(8,128)S(1)}, u32[]{:S(2)}, u32[]{:S(2)}) collective-permute-start(f32[2,128,128]{2,1,0:T(8,128)} %refs_0_.1), channel_id=1, source_target_pairs={{0,64},{32,96},{64,128},{96,160},{128,192},{160,224},{192,0},{224,... | collective-permute-start | bytes 393224 | tf_op jit(solution)/shard_map/ppermute | solution.py:465
  10.3 2.5 %collective-permute-start.4 = (f32[2,128,128]{2,1,0:T(8,128)}, f32[2,128,128]{2,1,0:T(8,128)S(1)}, u32[]{:S(2)}, u32[]{:S(2)}) collective-permute-start(f32[2,128,128]{2,1,0:T(8,128)} %refs_0_.1), channel_id=1, source_target_pairs={{0,128},{32,160},{64,192},{96,224},{128,0},{160,32},{192,64},{224,... | collective-permute-start | bytes 393224 | tf_op jit(solution)/shard_map/ppermute | solution.py:465
  12.7 1.2 collective-permute-start.6
  13.9 2.6 %collective-permute-start.1 = (f32[2,128,128]{2,1,0:T(8,128)}, f32[2,128,128]{2,1,0:T(8,128)S(1)}, u32[]{:S(2)}, u32[]{:S(2)}) collective-permute-start(f32[2,128,128]{2,1,0:T(8,128)} %refs_0_.1), channel_id=1, source_target_pairs={{0,32},{32,0},{64,96},{96,64},{128,160},{160,128},{192,224},{224,1... | collective-permute-start | bytes 393224 | tf_op jit(solution)/shard_map/ppermute | solution.py:465
  16.5 2.1 %collective-permute-start.3 = (f32[2,128,128]{2,1,0:T(8,128)S(1)}, f32[2,128,128]{2,1,0:T(8,128)S(1)}, u32[]{:S(2)}, u32[]{:S(2)}) collective-permute-start(f32[2,128,128]{2,1,0:T(8,128)S(1)} %collective-permute-done.2.refs_2_), channel_id=1, source_target_pairs={{0,32},{32,0},{64,96},{96,64},{128,160},{160,128},{192,224},{224,1... | collective-permute-start | bytes 393224 | tf_op jit(solution)/shard_map/ppermute | solution.py:465
  18.7 1.5 %collective-permute-start.5 = (f32[2,128,128]{2,1,0:T(8,128)S(1)}, f32[2,128,128]{2,1,0:T(8,128)S(1)}, u32[]{:S(2)}, u32[]{:S(2)}) collective-permute-start(f32[2,128,128]{2,1,0:T(8,128)S(1)} %collective-permute-done.4.refs_4_), channel_id=1, source_target_pairs={{0,32},{32,0},{64,96},{96,64},{128,160},{160,128},{192,224},{224,1... | collective-permute-start | bytes 393224 | tf_op jit(solution)/shard_map/ppermute | solution.py:465
  22.7 3.7 %fold.1 = (f32[4,16,128,128]{3,2,1,0:T(8,128)S(1)}, f32[64,128]{1,0:T(8,128)S(1)}) custom-call(s32[1]{0:T(128)S(6)} %copy.10.count.refs_1_, s32[2,128]{1,0:T(2,128)S(1)} %pad_add_fusion.slots_any.refs_0_, f32[128,128,128]{2,1,0:T(8,128)} %w_hbm.3), custom_call_target="tpu_custom_call" | custom-call | flops 20000000 | bytes 16777216 | tf_op jit(solution)/shard_map/fold/pallas_call | solution.py:83
  26.5 4.7 %forward.1 = (f32[4,128,128]{2,1,0:T(8,128)}, f32[4,136,128]{2,1,0:T(8,128)S(1)}, f32[16,128,128]{2,1,0:T(8,128)S(1)}, f32[64,128]{1,0:T(8,128)S(1)}, f32[16,128]{1,0:T(8,128)S(1)}) custom-call(s32[2,16]{1,0:T(2,128)S(1)} %bitcast.1, f32[4,128,128]{2,1,0:T(8,128)S(1)} %pack.2.refs_0_, f32[2,128,128]{2,1,0:T(8,128)S(1)} %collective-permute-done.1.refs_1_, ...), custom_call_target="tpu_custom_call" | custom-call | flops 1073741824 | bytes 8388608 | tf_op jit(solution)/shard_map/forward/pallas_call | solution.py:166
  31.1 3.7 %backward.1 = (f32[2,128,128]{2,1,0:T(8,128)S(1)}, f32[2,128,128]{2,1,0:T(8,128)S(1)}, f32[2,128,128]{2,1,0:T(8,128)S(1)}, f32[2,128,128]{2,1,0:T(8,128)S(1)}, f32[8,128,128]{2,1,0:T(8,128)S(1)}) custom-call(s32[2,16]{1,0:T(2,128)S(1)} %bitcast.2, f32[4,16,128,128]{3,2,1,0:T(8,128)S(1)} %get-tuple-element.24.refs_8_.w_ref, ...), custom_call_target="tpu_custom_call" | custom-call | flops 1073741824 | bytes 8388608 | tf_op jit(solution)/shard_map/backward/pallas_call | solution.py:231
  35.2 2.6 %collective-permute-start.16 = (f32[6,128,128]{2,1,0:T(8,128)S(1)}, f32[6,128,128]{2,1,0:T(8,128)S(1)}, u32[]{:S(2)}, u32[]{:S(2)}) collective-permute-start(f32[6,128,128]{2,1,0:T(8,128)S(1)} %pack.3.refs_4_), channel_id=1, source_target_pairs={{0,128},{32,160},{64,192},{96,224},{128,0},{160,32},{192,64},{224,... | collective-permute-start | bytes 1179656 | tf_op jit(solution)/shard_map/ppermute | solution.py:465
  39.4 7.7 %collective-permute-done.16.refs_8_ = f32[6,128,128]{2,1,0:T(8,128)S(1)} collective-permute-done((f32[6,128,128]{2,1,0:T(8,128)S(1)}, f32[6,128,128]{2,1,0:T(8,128)S(1)}, u32[]{:S(2)}, u32[]{:S(2)}) %collective-permute-start.16) | collective-permute-done | bytes 393248 | tf_op jit(solution)/shard_map/ppermute | solution.py:465
  47.1 1.1 collective-permute-start.17
  48.2 7.2 %collective-permute-done.18.refs_10_ = f32[6,128,128]{2,1,0:T(8,128)S(1)} collective-permute-done((f32[6,128,128]{2,1,0:T(8,128)S(1)}, f32[6,128,128]{2,1,0:T(8,128)S(1)}, u32[]{:S(2)}, u32[]{:S(2)}) %collective-permute-start.18) | collective-permute-done | bytes 393248 | tf_op jit(solution)/shard_map/ppermute | solution.py:465
  57.0 2.6 %collective-permute-start.22 = (f32[4,136,128]{2,1,0:T(8,128)S(1)}, f32[4,136,128]{2,1,0:T(8,128)S(1)}, u32[]{:S(2)}, u32[]{:S(2)}) collective-permute-start(f32[4,136,128]{2,1,0:T(8,128)S(1)} %get-tuple-element.27.fx.refs_5_), channel_id=1, source_target_pairs={{0,2},{1,3},{2,0},{3,1},{4,6},{5,7},{6,4},{7,5},{8,10},{9,11},{10,... | collective-permute-start | bytes 835592 | tf_op jit(solution)/shard_map/ppermute | solution.py:472
  59.7 2.0 %spread.1 = (bf16[16,256,512]{2,1,0:T(8,128)(2,1)S(1)}, f32[4,16,128]{2,1,0:T(8,128)S(1)}) custom-call(s32[2,16]{1,0:T(2,128)S(1)} %bitcast.3, f32[2,128,128]{2,1,0:T(8,128)S(1)} %get-tuple-element.45.refs_1_, f32[16,128,128]{2,1,0:T(8,128)S(1)} %get-tuple-element.29.e_ref.refs_2_, f32[16,128]{1,0:T(8,128)S(1)} %get-tuple-element.35.refs_3_, ...), custom_call_target="tpu_custom_call" | custom-call | flops 10000000 | bytes 10485760 | tf_op jit(solution)/shard_map/spread/pallas_call | solution.py:310
  61.8 2.8 %collective-permute-done.20.refs_6_ = f32[4,136,128]{2,1,0:T(8,128)S(1)} collective-permute-done((f32[4,136,128]{2,1,0:T(8,128)S(1)}, f32[4,136,128]{2,1,0:T(8,128)S(1)}, u32[]{:S(2)}, u32[]{:S(2)}) %collective-permute-start.20) | collective-permute-done | bytes 278560 | tf_op jit(solution)/shard_map/ppermute | solution.py:472
  64.6 7.2 %collective-permute-done.21.refs_7_ = f32[4,136,128]{2,1,0:T(8,128)S(1)} collective-permute-done((f32[4,136,128]{2,1,0:T(8,128)S(1)}, f32[4,136,128]{2,1,0:T(8,128)S(1)}, u32[]{:S(2)}, u32[]{:S(2)}) %collective-permute-start.21) | collective-permute-done | bytes 278560 | tf_op jit(solution)/shard_map/ppermute | solution.py:472
  71.8 1.1 edges.4.refs_9_
  72.9 1.5 %edges.5.refs_9_ = f32[8,128,128]{2,1,0:T(8,128)S(1)} custom-call(s32[2,128]{1,0:T(2,128)S(1)} %pad_add_fusion.slots_any.refs_0_, s32[1]{0:T(128)S(6)} %copy.10.count.refs_1_, bf16[16,256,512]{2,1,0:T(8,128)(2,1)S(1)} %get-tuple-element.36.refs_2_, f32[4,16,128]{2,1,0:T(8,128)S(1)} %get-tuple-element.37.refs_3_.refs_9_, ...), custom_call_target="tpu_custom_call" | custom-call | flops 536870912 | bytes 6291456 | tf_op jit(solution)/shard_map/edges/pallas_call | solution.py:375
  74.4 1.7 %collective-permute-start.23 = (f32[8,128,128]{2,1,0:T(8,128)S(1)}, f32[8,128,128]{2,1,0:T(8,128)S(1)}, u32[]{:S(2)}, u32[]{:S(2)}) collective-permute-start(f32[8,128,128]{2,1,0:T(8,128)S(1)} %edges.5.refs_9_), channel_id=1, source_target_pairs={{0,4},{1,5},{2,6},{3,7},{4,8},{5,9},{6,10},{7,11},{8,12},{9,13},{1... | collective-permute-start | bytes 1572872 | tf_op jit(solution)/shard_map/ppermute | solution.py:469
  76.1 1.4 %edges.6.refs_9_ = f32[8,128,128]{2,1,0:T(8,128)S(1)} custom-call(s32[2,128]{1,0:T(2,128)S(1)} %pad_add_fusion.slots_any.refs_0_, s32[1]{0:T(128)S(6)} %copy.10.count.refs_1_, bf16[16,256,512]{2,1,0:T(8,128)(2,1)S(1)} %get-tuple-element.36.refs_2_, f32[4,16,128]{2,1,0:T(8,128)S(1)} %get-tuple-element.37.refs_3_.refs_9_, ...), custom_call_target="tpu_custom_call" | custom-call | flops 536870912 | bytes 6291456 | tf_op jit(solution)/shard_map/edges/pallas_call | solution.py:375
  77.7 3.3 %collective-permute-start.25 = (f32[4,128,128]{2,1,0:T(8,128)S(1)}, f32[4,128,128]{2,1,0:T(8,128)S(1)}, u32[]{:S(2)}, u32[]{:S(2)}) collective-permute-start(f32[4,128,128]{2,1,0:T(8,128)S(1)} %edges.4.refs_9_), channel_id=1, source_target_pairs={{0,8},{1,9},{2,10},{3,11},{4,12},{5,13},{6,14},{7,15},{8,16},{9,17... | collective-permute-start | bytes 786440 | tf_op jit(solution)/shard_map/ppermute | solution.py:480
  81.0 2.3 %collective-permute-start.11 = (f32[2,128,128]{2,1,0:T(8,128)S(1)}, f32[2,128,128]{2,1,0:T(8,128)S(1)}, u32[]{:S(2)}, u32[]{:S(2)}) collective-permute-start(f32[2,128,128]{2,1,0:T(8,128)S(1)} %get-tuple-element.46), channel_id=1, source_target_pairs={{0,192},{32,224},{64,0},{96,32},{128,64},{160,96},{192,128},{224,1... | collective-permute-start | bytes 393224 | tf_op jit(solution)/shard_map/ppermute | solution.py:465
  84.0 16.7 %collective-permute-done.25.c_ref = f32[4,128,128]{2,1,0:T(8,128)S(1)} collective-permute-done((f32[4,128,128]{2,1,0:T(8,128)S(1)}, f32[4,128,128]{2,1,0:T(8,128)S(1)}, u32[]{:S(2)}, u32[]{:S(2)}) %collective-permute-start.25) | collective-permute-done | bytes 262176 | tf_op jit(solution)/shard_map/ppermute | solution.py:480
  100.7 1.2 %collective-permute-start.9 = (f32[2,128,128]{2,1,0:T(8,128)S(1)}, f32[2,128,128]{2,1,0:T(8,128)S(1)}, u32[]{:S(2)}, u32[]{:S(2)}) collective-permute-start(f32[2,128,128]{2,1,0:T(8,128)S(1)} %get-tuple-element.45.refs_1_), channel_id=1, source_target_pairs={{0,64},{32,96},{64,128},{96,160},{128,192},{160,224},{192,0},{224,... | collective-permute-start | bytes 393224 | tf_op jit(solution)/shard_map/ppermute | solution.py:465
  101.9 2.1 %edges.7 = (f32[4,128,128]{2,1,0:T(8,128)S(1)}, f32[4,128,128]{2,1,0:T(8,128)S(1)}, f32[4,128,128]{2,1,0:T(8,128)S(1)}) custom-call(s32[2,128]{1,0:T(2,128)S(1)} %pad_add_fusion.slots_any.refs_0_, s32[1]{0:T(128)S(6)} %copy.10.count.refs_1_, bf16[16,256,512]{2,1,0:T(8,128)(2,1)S(1)} %get-tuple-element.36.refs_2_, ...), custom_call_target="tpu_custom_call" | custom-call | flops 805306368 | bytes 6291456 | tf_op jit(solution)/shard_map/edges/pallas_call | solution.py:375
  104.3 2.4 %collective-permute-start.27 = (f32[4,128,128]{2,1,0:T(8,128)S(1)}, f32[4,128,128]{2,1,0:T(8,128)S(1)}, u32[]{:S(2)}, u32[]{:S(2)}) collective-permute-start(f32[4,128,128]{2,1,0:T(8,128)S(1)} %get-tuple-element.44), channel_id=1, source_target_pairs={{0,24},{1,25},{2,26},{3,27},{4,28},{5,29},{6,30},{7,31},{8,0},{9,1... | collective-permute-start | bytes 786440 | tf_op jit(solution)/shard_map/ppermute | solution.py:469
  108.4 6.7 %collective-permute-done.26.a_ref = f32[4,128,128]{2,1,0:T(8,128)S(1)} collective-permute-done((f32[4,128,128]{2,1,0:T(8,128)S(1)}, f32[4,128,128]{2,1,0:T(8,128)S(1)}, u32[]{:S(2)}, u32[]{:S(2)}) %collective-permute-start.26) | collective-permute-done | bytes 262176 | tf_op jit(solution)/shard_map/ppermute | solution.py:469
  115.1 3.7 %collective-permute-done.27.b_ref = f32[4,128,128]{2,1,0:T(8,128)S(1)} collective-permute-done((f32[4,128,128]{2,1,0:T(8,128)S(1)}, f32[4,128,128]{2,1,0:T(8,128)S(1)}, u32[]{:S(2)}, u32[]{:S(2)}) %collective-permute-start.27) | collective-permute-done | bytes 262176 | tf_op jit(solution)/shard_map/ppermute | solution.py:469
  (44 shorter events, 9.9 us)
Async XLA Ops:
  0.6 4.7 %collective-permute-start = (f32[2,128,128]{2,1,0:T(8,128)}, f32[2,128,128]{2,1,0:T(8,128)S(1)}, u32[]{:S(2)}, u32[]{:S(2)}) collective-permute-start(f32[2,128,128]{2,1,0:T(8,128)} %refs_0_.1), channel_id=1, source_target_pairs={{0,1},{1,0},{2,3},{3,2},{4,5},{5,4},{6,7},{7,6},{8,9},{9,8},{10,11... | collective-permute-start | bytes 393224 | tf_op jit(solution)/shard_map/ppermute | solution.py:472
  6.2 14.7 %collective-permute-start.12 = (f32[4,128,128]{2,1,0:T(8,128)S(1)}, f32[4,128,128]{2,1,0:T(8,128)S(1)}, u32[]{:S(2)}, u32[]{:S(2)}) collective-permute-start(f32[4,128,128]{2,1,0:T(8,128)S(1)} %pack.2.refs_0_), channel_id=1, source_target_pairs={{0,3},{1,2},{2,1},{3,0},{4,7},{5,6},{6,5},{7,4},{8,11},{9,10},{10,... | collective-permute-start | bytes 786440 | tf_op jit(solution)/shard_map/ppermute | solution.py:472
  9.1 7.5 %collective-permute-start.2 = (f32[2,128,128]{2,1,0:T(8,128)}, f32[2,128,128]{2,1,0:T(8,128)S(1)}, u32[]{:S(2)}, u32[]{:S(2)}) collective-permute-start(f32[2,128,128]{2,1,0:T(8,128)} %refs_0_.1), channel_id=1, source_target_pairs={{0,64},{32,96},{64,128},{96,160},{128,192},{160,224},{192,0},{224,... | collective-permute-start | bytes 393224 | tf_op jit(solution)/shard_map/ppermute | solution.py:465
  10.3 8.4 %collective-permute-start.4 = (f32[2,128,128]{2,1,0:T(8,128)}, f32[2,128,128]{2,1,0:T(8,128)S(1)}, u32[]{:S(2)}, u32[]{:S(2)}) collective-permute-start(f32[2,128,128]{2,1,0:T(8,128)} %refs_0_.1), channel_id=1, source_target_pairs={{0,128},{32,160},{64,192},{96,224},{128,0},{160,32},{192,64},{224,... | collective-permute-start | bytes 393224 | tf_op jit(solution)/shard_map/ppermute | solution.py:465
  12.7 7.5 %collective-permute-start.6 = (f32[2,128,128]{2,1,0:T(8,128)}, f32[2,128,128]{2,1,0:T(8,128)S(1)}, u32[]{:S(2)}, u32[]{:S(2)}) collective-permute-start(f32[2,128,128]{2,1,0:T(8,128)} %refs_0_.1), channel_id=1, source_target_pairs={{0,192},{32,224},{64,0},{96,32},{128,64},{160,96},{192,128},{224,1... | collective-permute-start | bytes 393224 | tf_op jit(solution)/shard_map/ppermute | solution.py:465
  13.9 12.5 %collective-permute-start.1 = (f32[2,128,128]{2,1,0:T(8,128)}, f32[2,128,128]{2,1,0:T(8,128)S(1)}, u32[]{:S(2)}, u32[]{:S(2)}) collective-permute-start(f32[2,128,128]{2,1,0:T(8,128)} %refs_0_.1), channel_id=1, source_target_pairs={{0,32},{32,0},{64,96},{96,64},{128,160},{160,128},{192,224},{224,1... | collective-permute-start | bytes 393224 | tf_op jit(solution)/shard_map/ppermute | solution.py:465
  16.5 9.9 %collective-permute-start.3 = (f32[2,128,128]{2,1,0:T(8,128)S(1)}, f32[2,128,128]{2,1,0:T(8,128)S(1)}, u32[]{:S(2)}, u32[]{:S(2)}) collective-permute-start(f32[2,128,128]{2,1,0:T(8,128)S(1)} %collective-permute-done.2.refs_2_), channel_id=1, source_target_pairs={{0,32},{32,0},{64,96},{96,64},{128,160},{160,128},{192,224},{224,1... | collective-permute-start | bytes 393224 | tf_op jit(solution)/shard_map/ppermute | solution.py:465
  18.7 7.8 %collective-permute-start.5 = (f32[2,128,128]{2,1,0:T(8,128)S(1)}, f32[2,128,128]{2,1,0:T(8,128)S(1)}, u32[]{:S(2)}, u32[]{:S(2)}) collective-permute-start(f32[2,128,128]{2,1,0:T(8,128)S(1)} %collective-permute-done.4.refs_4_), channel_id=1, source_target_pairs={{0,32},{32,0},{64,96},{96,64},{128,160},{160,128},{192,224},{224,1... | collective-permute-start | bytes 393224 | tf_op jit(solution)/shard_map/ppermute | solution.py:465
  20.2 6.3 %collective-permute-start.7 = (f32[2,128,128]{2,1,0:T(8,128)S(1)}, f32[2,128,128]{2,1,0:T(8,128)S(1)}, u32[]{:S(2)}, u32[]{:S(2)}) collective-permute-start(f32[2,128,128]{2,1,0:T(8,128)S(1)} %collective-permute-done.6.refs_6_), channel_id=1, source_target_pairs={{0,32},{32,0},{64,96},{96,64},{128,160},{160,128},{192,224},{224,1... | collective-permute-start | bytes 393224 | tf_op jit(solution)/shard_map/ppermute | solution.py:465
  21.0 18.4 %collective-permute-start.14 = (f32[6,128,128]{2,1,0:T(8,128)S(1)}, f32[6,128,128]{2,1,0:T(8,128)S(1)}, u32[]{:S(2)}, u32[]{:S(2)}) collective-permute-start(f32[6,128,128]{2,1,0:T(8,128)S(1)} %pack.3.refs_4_), channel_id=1, source_target_pairs={{0,64},{32,96},{64,128},{96,160},{128,192},{160,224},{192,0},{224,... | collective-permute-start | bytes 1179656 | tf_op jit(solution)/shard_map/ppermute | solution.py:465
  22.7 3.7 %copy-start = (f32[4,128,128]{2,1,0:T(8,128)S(1)}, f32[4,128,128]{2,1,0:T(8,128)}, u32[]{:S(2)}) copy-start(f32[4,128,128]{2,1,0:T(8,128)} %refs_10_.1) | copy-start | bytes 786436
  22.7 3.7 %copy-start.1 = (s32[16,2]{0,1:T(2,128)S(1)}, s32[16,2]{0,1:T(2,128)}, u32[]{:S(2)}) copy-start(s32[16,2]{0,1:T(2,128)} %param.8) | copy-start | bytes 388
  34.8 21.6 %collective-permute-start.8 = (f32[8,128,128]{2,1,0:T(8,128)S(1)}, f32[8,128,128]{2,1,0:T(8,128)S(1)}, u32[]{:S(2)}, u32[]{:S(2)}) collective-permute-start(f32[8,128,128]{2,1,0:T(8,128)S(1)} %get-tuple-element.31), channel_id=1, source_target_pairs={{0,32},{32,0},{64,96},{96,64},{128,160},{160,128},{192,224},{224,1... | collective-permute-start | bytes 1572872 | tf_op jit(solution)/shard_map/ppermute | solution.py:465
  35.2 11.9 %collective-permute-start.16 = (f32[6,128,128]{2,1,0:T(8,128)S(1)}, f32[6,128,128]{2,1,0:T(8,128)S(1)}, u32[]{:S(2)}, u32[]{:S(2)}) collective-permute-start(f32[6,128,128]{2,1,0:T(8,128)S(1)} %pack.3.refs_4_), channel_id=1, source_target_pairs={{0,128},{32,160},{64,192},{96,224},{128,0},{160,32},{192,64},{224,... | collective-permute-start | bytes 1179656 | tf_op jit(solution)/shard_map/ppermute | solution.py:465
  37.7 17.7 %collective-permute-start.18 = (f32[6,128,128]{2,1,0:T(8,128)S(1)}, f32[6,128,128]{2,1,0:T(8,128)S(1)}, u32[]{:S(2)}, u32[]{:S(2)}) collective-permute-start(f32[6,128,128]{2,1,0:T(8,128)S(1)} %pack.3.refs_4_), channel_id=1, source_target_pairs={{0,192},{32,224},{64,0},{96,32},{128,64},{160,96},{192,128},{224,1... | collective-permute-start | bytes 1179656 | tf_op jit(solution)/shard_map/ppermute | solution.py:465
  38.6 17.8 %collective-permute-start.13 = (f32[6,128,128]{2,1,0:T(8,128)S(1)}, f32[6,128,128]{2,1,0:T(8,128)S(1)}, u32[]{:S(2)}, u32[]{:S(2)}) collective-permute-start(f32[6,128,128]{2,1,0:T(8,128)S(1)} %pack.3.refs_4_), channel_id=1, source_target_pairs={{0,32},{32,0},{64,96},{96,64},{128,160},{160,128},{192,224},{224,1... | collective-permute-start | bytes 1179656 | tf_op jit(solution)/shard_map/ppermute | solution.py:465
  39.4 17.6 %collective-permute-start.15 = (f32[6,128,128]{2,1,0:T(8,128)S(1)}, f32[6,128,128]{2,1,0:T(8,128)S(1)}, u32[]{:S(2)}, u32[]{:S(2)}) collective-permute-start(f32[6,128,128]{2,1,0:T(8,128)S(1)} %collective-permute-done.14.refs_6_), channel_id=1, source_target_pairs={{0,32},{32,0},{64,96},{96,64},{128,160},{160,128},{192,224},{224,1... | collective-permute-start | bytes 1179656 | tf_op jit(solution)/shard_map/ppermute | solution.py:465
  47.1 12.6 %collective-permute-start.17 = (f32[6,128,128]{2,1,0:T(8,128)S(1)}, f32[6,128,128]{2,1,0:T(8,128)S(1)}, u32[]{:S(2)}, u32[]{:S(2)}) collective-permute-start(f32[6,128,128]{2,1,0:T(8,128)S(1)} %collective-permute-done.16.refs_8_), channel_id=1, source_target_pairs={{0,32},{32,0},{64,96},{96,64},{128,160},{160,128},{192,224},{224,1... | collective-permute-start | bytes 1179656 | tf_op jit(solution)/shard_map/ppermute | solution.py:465
  55.4 4.3 %collective-permute-start.19 = (f32[6,128,128]{2,1,0:T(8,128)S(1)}, f32[6,128,128]{2,1,0:T(8,128)S(1)}, u32[]{:S(2)}, u32[]{:S(2)}) collective-permute-start(f32[6,128,128]{2,1,0:T(8,128)S(1)} %collective-permute-done.18.refs_10_), channel_id=1, source_target_pairs={{0,32},{32,0},{64,96},{96,64},{128,160},{160,128},{192,224},{224,1... | collective-permute-start | bytes 1179656 | tf_op jit(solution)/shard_map/ppermute | solution.py:465
  56.4 8.2 %collective-permute-start.20 = (f32[4,136,128]{2,1,0:T(8,128)S(1)}, f32[4,136,128]{2,1,0:T(8,128)S(1)}, u32[]{:S(2)}, u32[]{:S(2)}) collective-permute-start(f32[4,136,128]{2,1,0:T(8,128)S(1)} %get-tuple-element.27.fx.refs_5_), channel_id=1, source_target_pairs={{0,1},{1,0},{2,3},{3,2},{4,5},{5,4},{6,7},{7,6},{8,9},{9,8},{10,11... | collective-permute-start | bytes 835592 | tf_op jit(solution)/shard_map/ppermute | solution.py:472
  56.4 15.4 %collective-permute-start.21 = (f32[4,136,128]{2,1,0:T(8,128)S(1)}, f32[4,136,128]{2,1,0:T(8,128)S(1)}, u32[]{:S(2)}, u32[]{:S(2)}) collective-permute-start(f32[4,136,128]{2,1,0:T(8,128)S(1)} %get-tuple-element.27.fx.refs_5_), channel_id=1, source_target_pairs={{0,3},{1,2},{2,1},{3,0},{4,7},{5,6},{6,5},{7,4},{8,11},{9,10},{10,... | collective-permute-start | bytes 835592 | tf_op jit(solution)/shard_map/ppermute | solution.py:472
  57.0 14.8 %collective-permute-start.22 = (f32[4,136,128]{2,1,0:T(8,128)S(1)}, f32[4,136,128]{2,1,0:T(8,128)S(1)}, u32[]{:S(2)}, u32[]{:S(2)}) collective-permute-start(f32[4,136,128]{2,1,0:T(8,128)S(1)} %get-tuple-element.27.fx.refs_5_), channel_id=1, source_target_pairs={{0,2},{1,3},{2,0},{3,1},{4,6},{5,7},{6,4},{7,5},{8,10},{9,11},{10,... | collective-permute-start | bytes 835592 | tf_op jit(solution)/shard_map/ppermute | solution.py:472
  74.4 29.7 %collective-permute-start.23 = (f32[8,128,128]{2,1,0:T(8,128)S(1)}, f32[8,128,128]{2,1,0:T(8,128)S(1)}, u32[]{:S(2)}, u32[]{:S(2)}) collective-permute-start(f32[8,128,128]{2,1,0:T(8,128)S(1)} %edges.5.refs_9_), channel_id=1, source_target_pairs={{0,4},{1,5},{2,6},{3,7},{4,8},{5,9},{6,10},{7,11},{8,12},{9,13},{1... | collective-permute-start | bytes 1572872 | tf_op jit(solution)/shard_map/ppermute | solution.py:469
  77.6 26.5 %collective-permute-start.24 = (f32[8,128,128]{2,1,0:T(8,128)S(1)}, f32[8,128,128]{2,1,0:T(8,128)S(1)}, u32[]{:S(2)}, u32[]{:S(2)}) collective-permute-start(f32[8,128,128]{2,1,0:T(8,128)S(1)} %edges.6.refs_9_), channel_id=1, source_target_pairs={{0,28},{1,29},{2,30},{3,31},{4,0},{5,1},{6,2},{7,3},{8,4},{9,5},{1... | collective-permute-start | bytes 1572872 | tf_op jit(solution)/shard_map/ppermute | solution.py:469
  77.7 23.0 %collective-permute-start.25 = (f32[4,128,128]{2,1,0:T(8,128)S(1)}, f32[4,128,128]{2,1,0:T(8,128)S(1)}, u32[]{:S(2)}, u32[]{:S(2)}) collective-permute-start(f32[4,128,128]{2,1,0:T(8,128)S(1)} %edges.4.refs_9_), channel_id=1, source_target_pairs={{0,8},{1,9},{2,10},{3,11},{4,12},{5,13},{6,14},{7,15},{8,16},{9,17... | collective-permute-start | bytes 786440 | tf_op jit(solution)/shard_map/ppermute | solution.py:480
  81.0 25.7 %collective-permute-start.11 = (f32[2,128,128]{2,1,0:T(8,128)S(1)}, f32[2,128,128]{2,1,0:T(8,128)S(1)}, u32[]{:S(2)}, u32[]{:S(2)}) collective-permute-start(f32[2,128,128]{2,1,0:T(8,128)S(1)} %get-tuple-element.46), channel_id=1, source_target_pairs={{0,192},{32,224},{64,0},{96,32},{128,64},{160,96},{192,128},{224,1... | collective-permute-start | bytes 393224 | tf_op jit(solution)/shard_map/ppermute | solution.py:465
  83.3 23.4 %collective-permute-start.10 = (f32[2,128,128]{2,1,0:T(8,128)S(1)}, f32[2,128,128]{2,1,0:T(8,128)S(1)}, u32[]{:S(2)}, u32[]{:S(2)}) collective-permute-start(f32[2,128,128]{2,1,0:T(8,128)S(1)} %get-tuple-element.47), channel_id=1, source_target_pairs={{0,128},{32,160},{64,192},{96,224},{128,0},{160,32},{192,64},{224,... | collective-permute-start | bytes 393224 | tf_op jit(solution)/shard_map/ppermute | solution.py:465
  100.7 6.0 %collective-permute-start.9 = (f32[2,128,128]{2,1,0:T(8,128)S(1)}, f32[2,128,128]{2,1,0:T(8,128)S(1)}, u32[]{:S(2)}, u32[]{:S(2)}) collective-permute-start(f32[2,128,128]{2,1,0:T(8,128)S(1)} %get-tuple-element.45.refs_1_), channel_id=1, source_target_pairs={{0,64},{32,96},{64,128},{96,160},{128,192},{160,224},{192,0},{224,... | collective-permute-start | bytes 393224 | tf_op jit(solution)/shard_map/ppermute | solution.py:465
  104.2 10.9 %collective-permute-start.26 = (f32[4,128,128]{2,1,0:T(8,128)S(1)}, f32[4,128,128]{2,1,0:T(8,128)S(1)}, u32[]{:S(2)}, u32[]{:S(2)}) collective-permute-start(f32[4,128,128]{2,1,0:T(8,128)S(1)} %get-tuple-element.43), channel_id=1, source_target_pairs={{0,8},{1,9},{2,10},{3,11},{4,12},{5,13},{6,14},{7,15},{8,16},{9,17... | collective-permute-start | bytes 786440 | tf_op jit(solution)/shard_map/ppermute | solution.py:469
  104.3 14.5 %collective-permute-start.27 = (f32[4,128,128]{2,1,0:T(8,128)S(1)}, f32[4,128,128]{2,1,0:T(8,128)S(1)}, u32[]{:S(2)}, u32[]{:S(2)}) collective-permute-start(f32[4,128,128]{2,1,0:T(8,128)S(1)} %get-tuple-element.44), channel_id=1, source_target_pairs={{0,24},{1,25},{2,26},{3,27},{4,28},{5,29},{6,30},{7,31},{8,0},{9,1... | collective-permute-start | bytes 786440 | tf_op jit(solution)/shard_map/ppermute | solution.py:469

commit v4 on v3

--- a/solution.py
+++ b/solution.py
@@ -149,8 +149,7 @@
         if q + 1 < qd:
             scaled(q + 1)
         sv[q] = tops[q] + jnp.log(total)
-        fx[q, 0:g] = up[q] / total
-        fx[q, g:] = jnp.broadcast_to(tops[q], (8, s))
+        fx[q] = up[q] / total
         copies.append(pltpu.make_async_copy(sv.at[q], sv_hbm.at[q], sems.at[q]))
         if q > 0:
             copies[q - 1].start()
@@ -167,7 +166,7 @@
         functools.partial(forward_kernel, nodes),
         out_shape=(
             jax.ShapeDtypeStruct((qd, g, s), f32),
-            jax.ShapeDtypeStruct((qd, g + 8, s), f32),
+            jax.ShapeDtypeStruct((qd, g, s), f32),
             jax.ShapeDtypeStruct((pg, g, s), f32),
             jax.ShapeDtypeStruct((qd * pg, s), f32),
             jax.ShapeDtypeStruct((pg, s), f32),
@@ -204,7 +203,7 @@
                 hi, lo = parts(w_ref[q, c].T)
                 thl[t, 0:g, at] = hi
                 thl[t, g : 2 * g, at] = lo
-                hi, lo = parts(fx[q, 0:g] * r_ref[pl.ds(q * pg + c, 1), :])
+                hi, lo = parts(fx[q] * r_ref[pl.ds(q * pg + c, 1), :])
                 ghl[t, at, 0:s] = hi
                 ghl[t, at, s : 2 * s] = lo
         for t in range(each):
@@ -330,16 +329,16 @@
     fxs, refs = refs[:rows], refs[rows:]
     outs, (r, lhs) = refs[1:-2], refs[-2:]
     qd, s = fxs[0].shape[0], fxs[0].shape[2]
-    g = fxs[0].shape[1] - 8
+    g = fxs[0].shape[1]
     pg = pk.shape[1]
     batch = lax.axis_index("batch")
     z, y = batch // ROWS, batch % ROWS
     depth = lax.axis_size("batch") // ROWS
     for q in range(qd):
         for t in range(rows):
-            top = fxs[t][q, g : g + 1]
             here = slice(q * pg, (q + 1) * pg)
-            r[t, here, :] = jnp.exp((pk[t] + bias[here, :]) - top)
+            biased = pk[t] + bias[here, :]
+            r[t, here, :] = jnp.exp(biased - jnp.max(biased, axis=0, keepdims=True))
     for ds, out in zip(plan, outs):
         keep = out.shape[0] // len(ds)
         places = []
@@ -351,7 +350,7 @@
             live = (b < count[0]).astype(f32)
             for t in range(rows):
                 at = slice(t * s, (t + 1) * s)
-                hi, lo = parts(fxs[t][q, 0:g] * (r[t, pl.ds(q * pg + c, 1), :] * live))
+                hi, lo = parts(fxs[t][q] * (r[t, pl.ds(q * pg + c, 1), :] * live))
                 lhs[k, 0:g, at] = hi
                 lhs[k, g : 2 * g, at] = lo
         for k, b in enumerate(places):
@@ -393,9 +392,8 @@
 
 def join_kernel(ap, am, bp, bm, c_ref, outp, outm):
     first = (lax.axis_index("nodes") % CORES == 0).astype(f32)
-    n = ap.shape[0]
-    outp[...] = (ap[...] + bp[0:n]) + c_ref[...] * first
-    outm[...] = (am[...] + bm[0:n]) + c_ref[...] * (1.0 - first)
+    outp[...] = (ap[...] + bp[...]) + c_ref[...] * first
+    outm[...] = (am[...] + bm[...]) + c_ref[...] * (1.0 - first)
 
 
 def join(ap, am, bp, bm, c):
@@ -410,42 +408,45 @@
     )(ap, am, bp, bm, c)
 
 
-def near_kernel(w_hbm, a_ref, b_ref, c_ref, near, w, sem):
+def near_kernel(w_hbm, a_ref, near, w, sem):
     keep = w.shape[0]
     own = w_hbm.at[pl.ds(lax.axis_index("batch") * keep, keep)]
     copy = pltpu.make_async_copy(own, w, sem)
     copy.start()
     copy.wait()
-    near[...] = w[...] * (a_ref[...] + b_ref[keep:] + c_ref[keep:])
-
-
-def weigh_near(w, a, b, c):
+    near[...] = w[...] * a_ref[...]
+
+
+def weigh_near(w, a):
     return pl.pallas_call(
         near_kernel,
         out_shape=[jax.ShapeDtypeStruct(a.shape, f32)] * 2,
-        in_specs=[pl.BlockSpec(memory_space=pltpu.HBM)] + vmem_specs(3),
+        in_specs=[pl.BlockSpec(memory_space=pltpu.HBM)] + vmem_specs(1),
         out_specs=vmem_specs(2),
         scratch_shapes=[pltpu.SemaphoreType.DMA],
         compiler_params=pltpu.CompilerParams(vmem_limit_bytes=50 << 20),
         cost_estimate=pl.CostEstimate(flops=200_000, bytes_accessed=1 << 20, transcendentals=0),
         name="near",
-    )(w, a, b, c)
-
-
-def last_kernel(near, w, a_ref, b_ref, out):
-    out[...] = near[...] + w[...] * (a_ref[...] + b_ref[...])
-
-
-def weigh_last(near, w, a, b):
+    )(w, a)
+
+
+def last_kernel(near, w, *refs):
+    total = refs[0][...]
+    for a in refs[1:-1]:
+        total += a[...]
+    refs[-1][...] = near[...] + w[...] * total
+
+
+def weigh_last(near, w, *arrived):
     return pl.pallas_call(
         last_kernel,
-        out_shape=jax.ShapeDtypeStruct(a.shape, f32),
-        in_specs=vmem_specs(4),
+        out_shape=jax.ShapeDtypeStruct(w.shape, f32),
+        in_specs=vmem_specs(2 + len(arrived)),
         out_specs=vmem_specs(1)[0],
         compiler_params=pltpu.CompilerParams(vmem_limit_bytes=4 << 20),
-        cost_estimate=pl.CostEstimate(flops=200_000, bytes_accessed=1 << 20, transcendentals=0),
+        cost_estimate=pl.CostEstimate(flops=300_000, bytes_accessed=1 << 20, transcendentals=0),
         name="last",
-    )(near, w, a, b)
+    )(near, w, *arrived)
 
 
 def body(leaves, prod_child, block_weight, block_child, block_parent, block_count, upper_flow):
@@ -507,18 +508,18 @@
 
     (e4,) = part(pks, (far,))
     r4 = shift_by_core(e4, 2)
-    (ep,) = part(e4, (3, 1))
-    rp = shift(ep, 1)
-    (em,) = part(ep, (-3, -1))
-    rm = shift(em, -1)
-    e2p, e2m, e0 = part(em, (2,), (-2,), (0,))
-    c2p, c2m = join(e2p, e2m, rp, rm, r4)
+    e3p, e3m = part(e4, (3,), (-3,))
+    r3p, r3m = shift(e3p, 1), shift(e3m, -1)
+    e1p, e1m, e0 = part(e3m, (1,), (-1,), (0,))
+    r1p, r1m = shift(e1p, 1), shift(e1m, -1)
+    e2p, e2m = part(e1m, (2,), (-2,))
+    c2p, c2m = join(e2p, e2m, r3p, r3m, r4)
     r2p, r2m = shift(c2p, 2), shift(c2m, -2)
     leaf_flow = functools.reduce(
         jnp.add, [flows[0]] + [move(flows[dx], dx) for dx in range(1, chips)]
     )
-    near, own = weigh_near(block_weight, e0, rp, rm)
-    param_flow = weigh_last(near, own, r2p, r2m)
+    near, own = weigh_near(block_weight, e0)
+    param_flow = weigh_last(near, own, r1p, r1m, r2p, r2m)
     return sum_values, leaf_flow, param_flow
 
 

time: 120 us -> 109 us (0.908)
  the two profiles are of different devices: /device:TPU:65 before, /device:TPU:32 now
where the time goes in v4:
time: 109 us
  waiting for transfers between devices  42.3 us (39%)
  starting transfers between devices  39.9 us (37%)
  Pallas kernels  23.6 us (22%)
  between operations  1.49 us (1%)
  other arithmetic  1.44 us (1%)
    ppermute x18, starting transfers between devices, move(): return lax.ppermute(a, 'nodes', [(n, to(n)) for n in range(nodes)])  17.3 us
    ppermute x18, waiting for transfers between devices, move(): return lax.ppermute(a, 'nodes', [(n, to(n)) for n in range(nodes)])  15.7 us
    ppermute x5, waiting for transfers between devices, swap(): return lax.ppermute(a, 'batch', [(b, b ^ mask) for b in range(batch)])  13.3 us
    ppermute x6, waiting for transfers between devices, shift(): return lax.ppermute(a, 'batch', [(b, to(b)) for b in range(batch)])  13.3 us
    ppermute x6, starting transfers between devices, shift(): return lax.ppermute(a, 'batch', [(b, to(b)) for b in range(batch)])  9.31 us
    ppermute x5, starting transfers between devices, swap(): return lax.ppermute(a, 'batch', [(b, b ^ mask) for b in range(batch)])  8.86 us
    pallas_call x4, Pallas kernels, edges(): pl.pallas_call(kernel, out_shape=[jax.ShapeDtypeStruct((n, g, g), f32) fo...  6.76 us
    pallas_call x1, Pallas kernels, forward(): pl.pallas_call(functools.partial(forward_kernel, nodes), out_shape=(jax.S...  4.66 us
  transfers between devices with their start and end apart: 30, of which 10 were waited for; matrix products, arithmetic and copies ran while one was open for 1% of the time, Pallas kernels for 18%

profile of v4, /device:TPU:32, one launch (start us, length us, event | category | flops | bytes accessed | tf_op | source)
XLA Modules:
  0.0 108.7 jit_solution(1007294049741175708)
XLA Ops:
  0.6 1.7 %collective-permute-start = (f32[2,128,128]{2,1,0:T(8,128)}, f32[2,128,128]{2,1,0:T(8,128)S(1)}, u32[]{:S(2)}, u32[]{:S(2)}) collective-permute-start(f32[2,128,128]{2,1,0:T(8,128)} %refs_0_.1), channel_id=1, source_target_pairs={{0,1},{1,0},{2,3},{3,2},{4,5},{5,4},{6,7},{7,6},{8,9},{9,8},{10,11... | collective-permute-start | bytes 393224 | tf_op jit(solution)/shard_map/ppermute | solution.py:473
  2.3 3.9 %collective-permute-done.refs_1_.refs_0_ = f32[2,128,128]{2,1,0:T(8,128)S(1)} collective-permute-done((f32[2,128,128]{2,1,0:T(8,128)}, f32[2,128,128]{2,1,0:T(8,128)S(1)}, u32[]{:S(2)}, u32[]{:S(2)}) %collective-permute-start) | collective-permute-done | bytes 131104 | tf_op jit(solution)/shard_map/ppermute | solution.py:473
  7.1 3.1 %collective-permute-start.12 = (f32[4,128,128]{2,1,0:T(8,128)S(1)}, f32[4,128,128]{2,1,0:T(8,128)S(1)}, u32[]{:S(2)}, u32[]{:S(2)}) collective-permute-start(f32[4,128,128]{2,1,0:T(8,128)S(1)} %pack.2.refs_0_), channel_id=1, source_target_pairs={{0,3},{1,2},{2,1},{3,0},{4,7},{5,6},{6,5},{7,4},{8,11},{9,10},{10,... | collective-permute-start | bytes 786440 | tf_op jit(solution)/shard_map/ppermute | solution.py:473
  10.2 1.5 %collective-permute-start.2 = (f32[2,128,128]{2,1,0:T(8,128)}, f32[2,128,128]{2,1,0:T(8,128)S(1)}, u32[]{:S(2)}, u32[]{:S(2)}) collective-permute-start(f32[2,128,128]{2,1,0:T(8,128)} %refs_0_.1), channel_id=1, source_target_pairs={{0,64},{32,96},{64,128},{96,160},{128,192},{160,224},{192,0},{224,... | collective-permute-start | bytes 393224 | tf_op jit(solution)/shard_map/ppermute | solution.py:466
  11.7 2.7 %collective-permute-start.4 = (f32[2,128,128]{2,1,0:T(8,128)}, f32[2,128,128]{2,1,0:T(8,128)S(1)}, u32[]{:S(2)}, u32[]{:S(2)}) collective-permute-start(f32[2,128,128]{2,1,0:T(8,128)} %refs_0_.1), channel_id=1, source_target_pairs={{0,128},{32,160},{64,192},{96,224},{128,0},{160,32},{192,64},{224,... | collective-permute-start | bytes 393224 | tf_op jit(solution)/shard_map/ppermute | solution.py:466
  14.4 1.4 %collective-permute-start.6 = (f32[2,128,128]{2,1,0:T(8,128)}, f32[2,128,128]{2,1,0:T(8,128)S(1)}, u32[]{:S(2)}, u32[]{:S(2)}) collective-permute-start(f32[2,128,128]{2,1,0:T(8,128)} %refs_0_.1), channel_id=1, source_target_pairs={{0,192},{32,224},{64,0},{96,32},{128,64},{160,96},{192,128},{224,1... | collective-permute-start | bytes 393224 | tf_op jit(solution)/shard_map/ppermute | solution.py:466
  15.8 2.1 %collective-permute-done.2.refs_2_ = f32[2,128,128]{2,1,0:T(8,128)S(1)} collective-permute-done((f32[2,128,128]{2,1,0:T(8,128)}, f32[2,128,128]{2,1,0:T(8,128)S(1)}, u32[]{:S(2)}, u32[]{:S(2)}) %collective-permute-start.2) | collective-permute-done | bytes 131104 | tf_op jit(solution)/shard_map/ppermute | solution.py:466
  18.0 1.5 %collective-permute-done.4.refs_4_ = f32[2,128,128]{2,1,0:T(8,128)S(1)} collective-permute-done((f32[2,128,128]{2,1,0:T(8,128)}, f32[2,128,128]{2,1,0:T(8,128)S(1)}, u32[]{:S(2)}, u32[]{:S(2)}) %collective-permute-start.4) | collective-permute-done | bytes 131104 | tf_op jit(solution)/shard_map/ppermute | solution.py:466
  22.3 3.7 %fold.1 = (f32[4,16,128,128]{3,2,1,0:T(8,128)S(1)}, f32[64,128]{1,0:T(8,128)S(1)}) custom-call(s32[1]{0:T(128)S(6)} %copy.10.count.refs_1_, s32[2,128]{1,0:T(2,128)S(1)} %pad_add_fusion.slots_any.refs_0_, f32[128,128,128]{2,1,0:T(8,128)} %w_hbm.3), custom_call_target="tpu_custom_call" | custom-call | flops 20000000 | bytes 16777216 | tf_op jit(solution)/shard_map/fold/pallas_call | solution.py:83
  26.1 4.7 %forward.1 = (f32[4,128,128]{2,1,0:T(8,128)}, f32[4,128,128]{2,1,0:T(8,128)S(1)}, f32[16,128,128]{2,1,0:T(8,128)S(1)}, f32[64,128]{1,0:T(8,128)S(1)}, f32[16,128]{1,0:T(8,128)S(1)}) custom-call(s32[2,16]{1,0:T(2,128)S(1)} %bitcast.1, f32[4,128,128]{2,1,0:T(8,128)S(1)} %pack.2.refs_0_, f32[2,128,128]{2,1,0:T(8,128)S(1)} %collective-permute-done.1.refs_1_, ...), custom_call_target="tpu_custom_call" | custom-call | flops 1073741824 | bytes 8388608 | tf_op jit(solution)/shard_map/forward/pallas_call | solution.py:165
  30.7 2.9 %collective-permute-start.16 = (f32[6,128,128]{2,1,0:T(8,128)S(1)}, f32[6,128,128]{2,1,0:T(8,128)S(1)}, u32[]{:S(2)}, u32[]{:S(2)}) collective-permute-start(f32[6,128,128]{2,1,0:T(8,128)S(1)} %pack.3.refs_4_), channel_id=1, source_target_pairs={{0,128},{32,160},{64,192},{96,224},{128,0},{160,32},{192,64},{224,... | collective-permute-start | bytes 1179656 | tf_op jit(solution)/shard_map/ppermute | solution.py:466
  33.7 1.1 %collective-permute-start.18 = (f32[6,128,128]{2,1,0:T(8,128)S(1)}, f32[6,128,128]{2,1,0:T(8,128)S(1)}, u32[]{:S(2)}, u32[]{:S(2)}) collective-permute-start(f32[6,128,128]{2,1,0:T(8,128)S(1)} %pack.3.refs_4_), channel_id=1, source_target_pairs={{0,192},{32,224},{64,0},{96,32},{128,64},{160,96},{192,128},{224,1... | collective-permute-start | bytes 1179656 | tf_op jit(solution)/shard_map/ppermute | solution.py:466
  34.8 3.7 %backward.1 = (f32[2,128,128]{2,1,0:T(8,128)S(1)}, f32[2,128,128]{2,1,0:T(8,128)S(1)}, f32[2,128,128]{2,1,0:T(8,128)S(1)}, f32[2,128,128]{2,1,0:T(8,128)S(1)}, f32[8,128,128]{2,1,0:T(8,128)S(1)}) custom-call(s32[2,16]{1,0:T(2,128)S(1)} %bitcast.2, f32[4,16,128,128]{3,2,1,0:T(8,128)S(1)} %get-tuple-element.28.refs_8_.w_ref, ...), custom_call_target="tpu_custom_call" | custom-call | flops 1073741824 | bytes 8388608 | tf_op jit(solution)/shard_map/backward/pallas_call | solution.py:230
  39.4 4.2 %collective-permute-done.16.refs_8_ = f32[6,128,128]{2,1,0:T(8,128)S(1)} collective-permute-done((f32[6,128,128]{2,1,0:T(8,128)S(1)}, f32[6,128,128]{2,1,0:T(8,128)S(1)}, u32[]{:S(2)}, u32[]{:S(2)}) %collective-permute-start.16) | collective-permute-done | bytes 393248 | tf_op jit(solution)/shard_map/ppermute | solution.py:466
  43.6 7.8 %collective-permute-done.18.refs_10_ = f32[6,128,128]{2,1,0:T(8,128)S(1)} collective-permute-done((f32[6,128,128]{2,1,0:T(8,128)S(1)}, f32[6,128,128]{2,1,0:T(8,128)S(1)}, u32[]{:S(2)}, u32[]{:S(2)}) %collective-permute-start.18) | collective-permute-done | bytes 393248 | tf_op jit(solution)/shard_map/ppermute | solution.py:466
  52.5 2.9 %collective-permute-start.22 = (f32[4,128,128]{2,1,0:T(8,128)S(1)}, f32[4,128,128]{2,1,0:T(8,128)S(1)}, u32[]{:S(2)}, u32[]{:S(2)}) collective-permute-start(f32[4,128,128]{2,1,0:T(8,128)S(1)} %get-tuple-element.31.fx.refs_5_), channel_id=1, source_target_pairs={{0,2},{1,3},{2,0},{3,1},{4,6},{5,7},{6,4},{7,5},{8,10},{9,11},{10,... | collective-permute-start | bytes 786440 | tf_op jit(solution)/shard_map/ppermute | solution.py:473
  55.5 2.0 %spread.1 = (bf16[16,256,512]{2,1,0:T(8,128)(2,1)S(1)}, f32[4,16,128]{2,1,0:T(8,128)S(1)}) custom-call(s32[2,16]{1,0:T(2,128)S(1)} %bitcast.3, f32[2,128,128]{2,1,0:T(8,128)S(1)} %get-tuple-element.53.refs_1_, f32[16,128,128]{2,1,0:T(8,128)S(1)} %get-tuple-element.33.e_ref.refs_2_, f32[16,128]{1,0:T(8,128)S(1)} %get-tuple-element.39.refs_3_, ...), custom_call_target="tpu_custom_call" | custom-call | flops 10000000 | bytes 10485760 | tf_op jit(solution)/shard_map/spread/pallas_call | solution.py:309
  57.6 2.9 %collective-permute-done.20.refs_6_ = f32[4,128,128]{2,1,0:T(8,128)S(1)} collective-permute-done((f32[4,128,128]{2,1,0:T(8,128)S(1)}, f32[4,128,128]{2,1,0:T(8,128)S(1)}, u32[]{:S(2)}, u32[]{:S(2)}) %collective-permute-start.20) | collective-permute-done | bytes 262176 | tf_op jit(solution)/shard_map/ppermute | solution.py:473
  60.5 6.5 %collective-permute-done.21.refs_7_ = f32[4,128,128]{2,1,0:T(8,128)S(1)} collective-permute-done((f32[4,128,128]{2,1,0:T(8,128)S(1)}, f32[4,128,128]{2,1,0:T(8,128)S(1)}, u32[]{:S(2)}, u32[]{:S(2)}) %collective-permute-start.21) | collective-permute-done | bytes 262176 | tf_op jit(solution)/shard_map/ppermute | solution.py:473
  67.0 1.1 edges.4.refs_9_
  68.1 1.8 %edges.5 = (f32[4,128,128]{2,1,0:T(8,128)S(1)}, f32[4,128,128]{2,1,0:T(8,128)S(1)}) custom-call(s32[2,128]{1,0:T(2,128)S(1)} %pad_add_fusion.slots_any.refs_0_, s32[1]{0:T(128)S(6)} %copy.10.count.refs_1_, bf16[16,256,512]{2,1,0:T(8,128)(2,1)S(1)} %get-tuple-element.40.refs_2_, f32[4,16,128]{2,1,0:T(8,128)S(1)} %get-tuple-element.41.refs_3_.refs_9_, ...), custom_call_target="tpu_custom_call" | custom-call | flops 536870912 | bytes 6291456 | tf_op jit(solution)/shard_map/edges/pallas_call | solution.py:374
  69.9 2.0 %collective-permute-start.25 = (f32[4,128,128]{2,1,0:T(8,128)S(1)}, f32[4,128,128]{2,1,0:T(8,128)S(1)}, u32[]{:S(2)}, u32[]{:S(2)}) collective-permute-start(f32[4,128,128]{2,1,0:T(8,128)S(1)} %get-tuple-element.50), channel_id=1, source_target_pairs={{0,4},{1,5},{2,6},{3,7},{4,8},{5,9},{6,10},{7,11},{8,12},{9,13},{1... | collective-permute-start | bytes 786440 | tf_op jit(solution)/shard_map/ppermute | solution.py:470
  72.0 4.4 %collective-permute-start.27 = (f32[4,128,128]{2,1,0:T(8,128)S(1)}, f32[4,128,128]{2,1,0:T(8,128)S(1)}, u32[]{:S(2)}, u32[]{:S(2)}) collective-permute-start(f32[4,128,128]{2,1,0:T(8,128)S(1)} %edges.4.refs_9_), channel_id=1, source_target_pairs={{0,8},{1,9},{2,10},{3,11},{4,12},{5,13},{6,14},{7,15},{8,16},{9,17... | collective-permute-start | bytes 786440 | tf_op jit(solution)/shard_map/ppermute | solution.py:481
  76.3 2.6 %collective-permute-start.11 = (f32[2,128,128]{2,1,0:T(8,128)S(1)}, f32[2,128,128]{2,1,0:T(8,128)S(1)}, u32[]{:S(2)}, u32[]{:S(2)}) collective-permute-start(f32[2,128,128]{2,1,0:T(8,128)S(1)} %get-tuple-element.54), channel_id=1, source_target_pairs={{0,192},{32,224},{64,0},{96,32},{128,64},{160,96},{192,128},{224,1... | collective-permute-start | bytes 393224 | tf_op jit(solution)/shard_map/ppermute | solution.py:466
  79.0 1.1 %collective-permute-start.10 = (f32[2,128,128]{2,1,0:T(8,128)S(1)}, f32[2,128,128]{2,1,0:T(8,128)S(1)}, u32[]{:S(2)}, u32[]{:S(2)}) collective-permute-start(f32[2,128,128]{2,1,0:T(8,128)S(1)} %get-tuple-element.55), channel_id=1, source_target_pairs={{0,128},{32,160},{64,192},{96,224},{128,0},{160,32},{192,64},{224,... | collective-permute-start | bytes 393224 | tf_op jit(solution)/shard_map/ppermute | solution.py:466
  80.1 1.6 %collective-permute-start.9 = (f32[2,128,128]{2,1,0:T(8,128)S(1)}, f32[2,128,128]{2,1,0:T(8,128)S(1)}, u32[]{:S(2)}, u32[]{:S(2)}) collective-permute-start(f32[2,128,128]{2,1,0:T(8,128)S(1)} %get-tuple-element.53.refs_1_), channel_id=1, source_target_pairs={{0,64},{32,96},{64,128},{96,160},{128,192},{160,224},{192,0},{224,... | collective-permute-start | bytes 393224 | tf_op jit(solution)/shard_map/ppermute | solution.py:466
  81.7 2.1 %edges.6 = (f32[4,128,128]{2,1,0:T(8,128)S(1)}, f32[4,128,128]{2,1,0:T(8,128)S(1)}, f32[4,128,128]{2,1,0:T(8,128)S(1)}) custom-call(s32[2,128]{1,0:T(2,128)S(1)} %pad_add_fusion.slots_any.refs_0_, s32[1]{0:T(128)S(6)} %copy.10.count.refs_1_, bf16[16,256,512]{2,1,0:T(8,128)(2,1)S(1)} %get-tuple-element.40.refs_2_, ...), custom_call_target="tpu_custom_call" | custom-call | flops 805306368 | bytes 6291456 | tf_op jit(solution)/shard_map/edges/pallas_call | solution.py:374
  83.9 1.8 %edges.7 = (f32[4,128,128]{2,1,0:T(8,128)S(1)}, f32[4,128,128]{2,1,0:T(8,128)S(1)}) custom-call(s32[2,128]{1,0:T(2,128)S(1)} %pad_add_fusion.slots_any.refs_0_, s32[1]{0:T(128)S(6)} %copy.10.count.refs_1_, bf16[16,256,512]{2,1,0:T(8,128)(2,1)S(1)} %get-tuple-element.40.refs_2_, f32[4,16,128]{2,1,0:T(8,128)S(1)} %get-tuple-element.41.refs_3_.refs_9_, ...), custom_call_target="tpu_custom_call" | custom-call | flops 536870912 | bytes 6291456 | tf_op jit(solution)/shard_map/edges/pallas_call | solution.py:374
  85.7 2.2 %collective-permute-start.24 = (f32[4,128,128]{2,1,0:T(8,128)S(1)}, f32[4,128,128]{2,1,0:T(8,128)S(1)}, u32[]{:S(2)}, u32[]{:S(2)}) collective-permute-start(f32[4,128,128]{2,1,0:T(8,128)S(1)} %get-tuple-element.47.refs_9_), channel_id=1, source_target_pairs={{0,28},{1,29},{2,30},{3,31},{4,0},{5,1},{6,2},{7,3},{8,4},{9,5},{1... | collective-permute-start | bytes 786440 | tf_op jit(solution)/shard_map/ppermute | solution.py:470
  88.6 4.4 %collective-permute-start.28 = (f32[4,128,128]{2,1,0:T(8,128)S(1)}, f32[4,128,128]{2,1,0:T(8,128)S(1)}, u32[]{:S(2)}, u32[]{:S(2)}) collective-permute-start(f32[4,128,128]{2,1,0:T(8,128)S(1)} %get-tuple-element.51), channel_id=1, source_target_pairs={{0,8},{1,9},{2,10},{3,11},{4,12},{5,13},{6,14},{7,15},{8,16},{9,17... | collective-permute-start | bytes 786440 | tf_op jit(solution)/shard_map/ppermute | solution.py:470
  94.7 2.3 %collective-permute-done.23.refs_0_ = f32[4,128,128]{2,1,0:T(8,128)S(1)} collective-permute-done((f32[4,128,128]{2,1,0:T(8,128)S(1)}, f32[4,128,128]{2,1,0:T(8,128)S(1)}, u32[]{:S(2)}, u32[]{:S(2)}) %collective-permute-start.23) | collective-permute-done | bytes 262176 | tf_op jit(solution)/shard_map/ppermute | solution.py:470
  96.9 11.0 %collective-permute-done.28.refs_2_ = f32[4,128,128]{2,1,0:T(8,128)S(1)} collective-permute-done((f32[4,128,128]{2,1,0:T(8,128)S(1)}, f32[4,128,128]{2,1,0:T(8,128)S(1)}, u32[]{:S(2)}, u32[]{:S(2)}) %collective-permute-start.28) | collective-permute-done | bytes 262176 | tf_op jit(solution)/shard_map/ppermute | solution.py:470
  (48 shorter events, 8.5 us)
Async XLA Ops:
  0.6 5.5 %collective-permute-start = (f32[2,128,128]{2,1,0:T(8,128)}, f32[2,128,128]{2,1,0:T(8,128)S(1)}, u32[]{:S(2)}, u32[]{:S(2)}) collective-permute-start(f32[2,128,128]{2,1,0:T(8,128)} %refs_0_.1), channel_id=1, source_target_pairs={{0,1},{1,0},{2,3},{3,2},{4,5},{5,4},{6,7},{7,6},{8,9},{9,8},{10,11... | collective-permute-start | bytes 393224 | tf_op jit(solution)/shard_map/ppermute | solution.py:473
  7.1 13.6 %collective-permute-start.12 = (f32[4,128,128]{2,1,0:T(8,128)S(1)}, f32[4,128,128]{2,1,0:T(8,128)S(1)}, u32[]{:S(2)}, u32[]{:S(2)}) collective-permute-start(f32[4,128,128]{2,1,0:T(8,128)S(1)} %pack.2.refs_0_), channel_id=1, source_target_pairs={{0,3},{1,2},{2,1},{3,0},{4,7},{5,6},{6,5},{7,4},{8,11},{9,10},{10,... | collective-permute-start | bytes 786440 | tf_op jit(solution)/shard_map/ppermute | solution.py:473
  10.2 7.8 %collective-permute-start.2 = (f32[2,128,128]{2,1,0:T(8,128)}, f32[2,128,128]{2,1,0:T(8,128)S(1)}, u32[]{:S(2)}, u32[]{:S(2)}) collective-permute-start(f32[2,128,128]{2,1,0:T(8,128)} %refs_0_.1), channel_id=1, source_target_pairs={{0,64},{32,96},{64,128},{96,160},{128,192},{160,224},{192,0},{224,... | collective-permute-start | bytes 393224 | tf_op jit(solution)/shard_map/ppermute | solution.py:466
  11.7 7.8 %collective-permute-start.4 = (f32[2,128,128]{2,1,0:T(8,128)}, f32[2,128,128]{2,1,0:T(8,128)S(1)}, u32[]{:S(2)}, u32[]{:S(2)}) collective-permute-start(f32[2,128,128]{2,1,0:T(8,128)} %refs_0_.1), channel_id=1, source_target_pairs={{0,128},{32,160},{64,192},{96,224},{128,0},{160,32},{192,64},{224,... | collective-permute-start | bytes 393224 | tf_op jit(solution)/shard_map/ppermute | solution.py:466
  14.4 5.2 %collective-permute-start.6 = (f32[2,128,128]{2,1,0:T(8,128)}, f32[2,128,128]{2,1,0:T(8,128)S(1)}, u32[]{:S(2)}, u32[]{:S(2)}) collective-permute-start(f32[2,128,128]{2,1,0:T(8,128)} %refs_0_.1), channel_id=1, source_target_pairs={{0,192},{32,224},{64,0},{96,32},{128,64},{160,96},{192,128},{224,1... | collective-permute-start | bytes 393224 | tf_op jit(solution)/shard_map/ppermute | solution.py:466
  15.8 10.2 %collective-permute-start.1 = (f32[2,128,128]{2,1,0:T(8,128)}, f32[2,128,128]{2,1,0:T(8,128)S(1)}, u32[]{:S(2)}, u32[]{:S(2)}) collective-permute-start(f32[2,128,128]{2,1,0:T(8,128)} %refs_0_.1), channel_id=1, source_target_pairs={{0,32},{32,0},{64,96},{96,64},{128,160},{160,128},{192,224},{224,1... | collective-permute-start | bytes 393224 | tf_op jit(solution)/shard_map/ppermute | solution.py:466
  18.0 8.0 %collective-permute-start.3 = (f32[2,128,128]{2,1,0:T(8,128)S(1)}, f32[2,128,128]{2,1,0:T(8,128)S(1)}, u32[]{:S(2)}, u32[]{:S(2)}) collective-permute-start(f32[2,128,128]{2,1,0:T(8,128)S(1)} %collective-permute-done.2.refs_2_), channel_id=1, source_target_pairs={{0,32},{32,0},{64,96},{96,64},{128,160},{160,128},{192,224},{224,1... | collective-permute-start | bytes 393224 | tf_op jit(solution)/shard_map/ppermute | solution.py:466
  19.5 6.5 %collective-permute-start.5 = (f32[2,128,128]{2,1,0:T(8,128)S(1)}, f32[2,128,128]{2,1,0:T(8,128)S(1)}, u32[]{:S(2)}, u32[]{:S(2)}) collective-permute-start(f32[2,128,128]{2,1,0:T(8,128)S(1)} %collective-permute-done.4.refs_4_), channel_id=1, source_target_pairs={{0,32},{32,0},{64,96},{96,64},{128,160},{160,128},{192,224},{224,1... | collective-permute-start | bytes 393224 | tf_op jit(solution)/shard_map/ppermute | solution.py:466
  19.6 6.5 %collective-permute-start.7 = (f32[2,128,128]{2,1,0:T(8,128)S(1)}, f32[2,128,128]{2,1,0:T(8,128)S(1)}, u32[]{:S(2)}, u32[]{:S(2)}) collective-permute-start(f32[2,128,128]{2,1,0:T(8,128)S(1)} %collective-permute-done.6.refs_6_), channel_id=1, source_target_pairs={{0,32},{32,0},{64,96},{96,64},{128,160},{160,128},{192,224},{224,1... | collective-permute-start | bytes 393224 | tf_op jit(solution)/shard_map/ppermute | solution.py:466
  20.7 18.4 %collective-permute-start.14 = (f32[6,128,128]{2,1,0:T(8,128)S(1)}, f32[6,128,128]{2,1,0:T(8,128)S(1)}, u32[]{:S(2)}, u32[]{:S(2)}) collective-permute-start(f32[6,128,128]{2,1,0:T(8,128)S(1)} %pack.3.refs_4_), channel_id=1, source_target_pairs={{0,64},{32,96},{64,128},{96,160},{128,192},{160,224},{192,0},{224,... | collective-permute-start | bytes 1179656 | tf_op jit(solution)/shard_map/ppermute | solution.py:466
  22.3 3.7 %copy-start = (f32[4,128,128]{2,1,0:T(8,128)S(1)}, f32[4,128,128]{2,1,0:T(8,128)}, u32[]{:S(2)}) copy-start(f32[4,128,128]{2,1,0:T(8,128)} %refs_10_.1) | copy-start | bytes 786436
  22.3 3.7 %copy-start.1 = (s32[16,2]{0,1:T(2,128)S(1)}, s32[16,2]{0,1:T(2,128)}, u32[]{:S(2)}) copy-start(s32[16,2]{0,1:T(2,128)} %param.8) | copy-start | bytes 388
  30.7 12.8 %collective-permute-start.16 = (f32[6,128,128]{2,1,0:T(8,128)S(1)}, f32[6,128,128]{2,1,0:T(8,128)S(1)}, u32[]{:S(2)}, u32[]{:S(2)}) collective-permute-start(f32[6,128,128]{2,1,0:T(8,128)S(1)} %pack.3.refs_4_), channel_id=1, source_target_pairs={{0,128},{32,160},{64,192},{96,224},{128,0},{160,32},{192,64},{224,... | collective-permute-start | bytes 1179656 | tf_op jit(solution)/shard_map/ppermute | solution.py:466
  33.7 17.7 %collective-permute-start.18 = (f32[6,128,128]{2,1,0:T(8,128)S(1)}, f32[6,128,128]{2,1,0:T(8,128)S(1)}, u32[]{:S(2)}, u32[]{:S(2)}) collective-permute-start(f32[6,128,128]{2,1,0:T(8,128)S(1)} %pack.3.refs_4_), channel_id=1, source_target_pairs={{0,192},{32,224},{64,0},{96,32},{128,64},{160,96},{192,128},{224,1... | collective-permute-start | bytes 1179656 | tf_op jit(solution)/shard_map/ppermute | solution.py:466
  38.5 12.8 %collective-permute-start.8 = (f32[8,128,128]{2,1,0:T(8,128)S(1)}, f32[8,128,128]{2,1,0:T(8,128)S(1)}, u32[]{:S(2)}, u32[]{:S(2)}) collective-permute-start(f32[8,128,128]{2,1,0:T(8,128)S(1)} %get-tuple-element.35), channel_id=1, source_target_pairs={{0,32},{32,0},{64,96},{96,64},{128,160},{160,128},{192,224},{224,1... | collective-permute-start | bytes 1572872 | tf_op jit(solution)/shard_map/ppermute | solution.py:466
  38.6 12.9 %collective-permute-start.13 = (f32[6,128,128]{2,1,0:T(8,128)S(1)}, f32[6,128,128]{2,1,0:T(8,128)S(1)}, u32[]{:S(2)}, u32[]{:S(2)}) collective-permute-start(f32[6,128,128]{2,1,0:T(8,128)S(1)} %pack.3.refs_4_), channel_id=1, source_target_pairs={{0,32},{32,0},{64,96},{96,64},{128,160},{160,128},{192,224},{224,1... | collective-permute-start | bytes 1179656 | tf_op jit(solution)/shard_map/ppermute | solution.py:466
  39.1 13.4 %collective-permute-start.15 = (f32[6,128,128]{2,1,0:T(8,128)S(1)}, f32[6,128,128]{2,1,0:T(8,128)S(1)}, u32[]{:S(2)}, u32[]{:S(2)}) collective-permute-start(f32[6,128,128]{2,1,0:T(8,128)S(1)} %collective-permute-done.14.refs_6_), channel_id=1, source_target_pairs={{0,32},{32,0},{64,96},{96,64},{128,160},{160,128},{192,224},{224,1... | collective-permute-start | bytes 1179656 | tf_op jit(solution)/shard_map/ppermute | solution.py:466
  43.6 11.9 %collective-permute-start.17 = (f32[6,128,128]{2,1,0:T(8,128)S(1)}, f32[6,128,128]{2,1,0:T(8,128)S(1)}, u32[]{:S(2)}, u32[]{:S(2)}) collective-permute-start(f32[6,128,128]{2,1,0:T(8,128)S(1)} %collective-permute-done.16.refs_8_), channel_id=1, source_target_pairs={{0,32},{32,0},{64,96},{96,64},{128,160},{160,128},{192,224},{224,1... | collective-permute-start | bytes 1179656 | tf_op jit(solution)/shard_map/ppermute | solution.py:466
  51.3 4.2 %collective-permute-start.19 = (f32[6,128,128]{2,1,0:T(8,128)S(1)}, f32[6,128,128]{2,1,0:T(8,128)S(1)}, u32[]{:S(2)}, u32[]{:S(2)}) collective-permute-start(f32[6,128,128]{2,1,0:T(8,128)S(1)} %collective-permute-done.18.refs_10_), channel_id=1, source_target_pairs={{0,32},{32,0},{64,96},{96,64},{128,160},{160,128},{192,224},{224,1... | collective-permute-start | bytes 1179656 | tf_op jit(solution)/shard_map/ppermute | solution.py:466
  51.3 9.2 %collective-permute-start.20 = (f32[4,128,128]{2,1,0:T(8,128)S(1)}, f32[4,128,128]{2,1,0:T(8,128)S(1)}, u32[]{:S(2)}, u32[]{:S(2)}) collective-permute-start(f32[4,128,128]{2,1,0:T(8,128)S(1)} %get-tuple-element.31.fx.refs_5_), channel_id=1, source_target_pairs={{0,1},{1,0},{2,3},{3,2},{4,5},{5,4},{6,7},{7,6},{8,9},{9,8},{10,11... | collective-permute-start | bytes 786440 | tf_op jit(solution)/shard_map/ppermute | solution.py:473
  51.5 15.5 %collective-permute-start.21 = (f32[4,128,128]{2,1,0:T(8,128)S(1)}, f32[4,128,128]{2,1,0:T(8,128)S(1)}, u32[]{:S(2)}, u32[]{:S(2)}) collective-permute-start(f32[4,128,128]{2,1,0:T(8,128)S(1)} %get-tuple-element.31.fx.refs_5_), channel_id=1, source_target_pairs={{0,3},{1,2},{2,1},{3,0},{4,7},{5,6},{6,5},{7,4},{8,11},{9,10},{10,... | collective-permute-start | bytes 786440 | tf_op jit(solution)/shard_map/ppermute | solution.py:473
  52.5 14.4 %collective-permute-start.22 = (f32[4,128,128]{2,1,0:T(8,128)S(1)}, f32[4,128,128]{2,1,0:T(8,128)S(1)}, u32[]{:S(2)}, u32[]{:S(2)}) collective-permute-start(f32[4,128,128]{2,1,0:T(8,128)S(1)} %get-tuple-element.31.fx.refs_5_), channel_id=1, source_target_pairs={{0,2},{1,3},{2,0},{3,1},{4,6},{5,7},{6,4},{7,5},{8,10},{9,11},{10,... | collective-permute-start | bytes 786440 | tf_op jit(solution)/shard_map/ppermute | solution.py:473
  69.9 10.3 %collective-permute-start.25 = (f32[4,128,128]{2,1,0:T(8,128)S(1)}, f32[4,128,128]{2,1,0:T(8,128)S(1)}, u32[]{:S(2)}, u32[]{:S(2)}) collective-permute-start(f32[4,128,128]{2,1,0:T(8,128)S(1)} %get-tuple-element.50), channel_id=1, source_target_pairs={{0,4},{1,5},{2,6},{3,7},{4,8},{5,9},{6,10},{7,11},{8,12},{9,13},{1... | collective-permute-start | bytes 786440 | tf_op jit(solution)/shard_map/ppermute | solution.py:470
  71.9 13.8 %collective-permute-start.26 = (f32[4,128,128]{2,1,0:T(8,128)S(1)}, f32[4,128,128]{2,1,0:T(8,128)S(1)}, u32[]{:S(2)}, u32[]{:S(2)}) collective-permute-start(f32[4,128,128]{2,1,0:T(8,128)S(1)} %get-tuple-element.42.refs_9_), channel_id=1, source_target_pairs={{0,28},{1,29},{2,30},{3,31},{4,0},{5,1},{6,2},{7,3},{8,4},{9,5},{1... | collective-permute-start | bytes 786440 | tf_op jit(solution)/shard_map/ppermute | solution.py:470
  72.0 15.9 %collective-permute-start.27 = (f32[4,128,128]{2,1,0:T(8,128)S(1)}, f32[4,128,128]{2,1,0:T(8,128)S(1)}, u32[]{:S(2)}, u32[]{:S(2)}) collective-permute-start(f32[4,128,128]{2,1,0:T(8,128)S(1)} %edges.4.refs_9_), channel_id=1, source_target_pairs={{0,8},{1,9},{2,10},{3,11},{4,12},{5,13},{6,14},{7,15},{8,16},{9,17... | collective-permute-start | bytes 786440 | tf_op jit(solution)/shard_map/ppermute | solution.py:481
  76.3 12.2 %collective-permute-start.11 = (f32[2,128,128]{2,1,0:T(8,128)S(1)}, f32[2,128,128]{2,1,0:T(8,128)S(1)}, u32[]{:S(2)}, u32[]{:S(2)}) collective-permute-start(f32[2,128,128]{2,1,0:T(8,128)S(1)} %get-tuple-element.54), channel_id=1, source_target_pairs={{0,192},{32,224},{64,0},{96,32},{128,64},{160,96},{192,128},{224,1... | collective-permute-start | bytes 393224 | tf_op jit(solution)/shard_map/ppermute | solution.py:466
  79.0 14.0 %collective-permute-start.10 = (f32[2,128,128]{2,1,0:T(8,128)S(1)}, f32[2,128,128]{2,1,0:T(8,128)S(1)}, u32[]{:S(2)}, u32[]{:S(2)}) collective-permute-start(f32[2,128,128]{2,1,0:T(8,128)S(1)} %get-tuple-element.55), channel_id=1, source_target_pairs={{0,128},{32,160},{64,192},{96,224},{128,0},{160,32},{192,64},{224,... | collective-permute-start | bytes 393224 | tf_op jit(solution)/shard_map/ppermute | solution.py:466
  80.1 12.8 %collective-permute-start.9 = (f32[2,128,128]{2,1,0:T(8,128)S(1)}, f32[2,128,128]{2,1,0:T(8,128)S(1)}, u32[]{:S(2)}, u32[]{:S(2)}) collective-permute-start(f32[2,128,128]{2,1,0:T(8,128)S(1)} %get-tuple-element.53.refs_1_), channel_id=1, source_target_pairs={{0,64},{32,96},{64,128},{96,160},{128,192},{160,224},{192,0},{224,... | collective-permute-start | bytes 393224 | tf_op jit(solution)/shard_map/ppermute | solution.py:466
  85.7 11.3 %collective-permute-start.24 = (f32[4,128,128]{2,1,0:T(8,128)S(1)}, f32[4,128,128]{2,1,0:T(8,128)S(1)}, u32[]{:S(2)}, u32[]{:S(2)}) collective-permute-start(f32[4,128,128]{2,1,0:T(8,128)S(1)} %get-tuple-element.47.refs_9_), channel_id=1, source_target_pairs={{0,28},{1,29},{2,30},{3,31},{4,0},{5,1},{6,2},{7,3},{8,4},{9,5},{1... | collective-permute-start | bytes 786440 | tf_op jit(solution)/shard_map/ppermute | solution.py:470
  87.9 9.0 %collective-permute-start.23 = (f32[4,128,128]{2,1,0:T(8,128)S(1)}, f32[4,128,128]{2,1,0:T(8,128)S(1)}, u32[]{:S(2)}, u32[]{:S(2)}) collective-permute-start(f32[4,128,128]{2,1,0:T(8,128)S(1)} %get-tuple-element.46), channel_id=1, source_target_pairs={{0,4},{1,5},{2,6},{3,7},{4,8},{5,9},{6,10},{7,11},{8,12},{9,13},{1... | collective-permute-start | bytes 786440 | tf_op jit(solution)/shard_map/ppermute | solution.py:470
  88.6 19.3 %collective-permute-start.28 = (f32[4,128,128]{2,1,0:T(8,128)S(1)}, f32[4,128,128]{2,1,0:T(8,128)S(1)}, u32[]{:S(2)}, u32[]{:S(2)}) collective-permute-start(f32[4,128,128]{2,1,0:T(8,128)S(1)} %get-tuple-element.51), channel_id=1, source_target_pairs={{0,8},{1,9},{2,10},{3,11},{4,12},{5,13},{6,14},{7,15},{8,16},{9,17... | collective-permute-start | bytes 786440 | tf_op jit(solution)/shard_map/ppermute | solution.py:470
  93.0 15.0 %collective-permute-start.29 = (f32[4,128,128]{2,1,0:T(8,128)S(1)}, f32[4,128,128]{2,1,0:T(8,128)S(1)}, u32[]{:S(2)}, u32[]{:S(2)}) collective-permute-start(f32[4,128,128]{2,1,0:T(8,128)S(1)} %get-tuple-element.52), channel_id=1, source_target_pairs={{0,24},{1,25},{2,26},{3,27},{4,28},{5,29},{6,30},{7,31},{8,0},{9,1... | collective-permute-start | bytes 786440 | tf_op jit(solution)/shard_map/ppermute | solution.py:470

commit v5 on v4

--- a/solution.py
+++ b/solution.py
@@ -506,11 +506,13 @@
     def part(token, *plan):
         return edges(slots, block_count, ehl, pks, bias, fxs, token, plan, keep)
 
-    (e4,) = part(pks, (far,))
+    (e3p,) = part(pks, (3,))
+    r3p = shift(e3p, 1)
+    (e3m,) = part(e3p, (-3,))
+    r3m = shift(e3m, -1)
+    (e4,) = part(e3m, (far,))
     r4 = shift_by_core(e4, 2)
-    e3p, e3m = part(e4, (3,), (-3,))
-    r3p, r3m = shift(e3p, 1), shift(e3m, -1)
-    e1p, e1m, e0 = part(e3m, (1,), (-1,), (0,))
+    e1p, e1m, e0 = part(e4, (1,), (-1,), (0,))
     r1p, r1m = shift(e1p, 1), shift(e1m, -1)
     e2p, e2m = part(e1m, (2,), (-2,))
     c2p, c2m = join(e2p, e2m, r3p, r3m, r4)

time: 109 us -> 108 us (level)
  the two profiles are of different devices: /device:TPU:32 before, /device:TPU:35 now
where the time goes in v5:
time: 108 us
  starting transfers between devices  46.3 us (43%)
  waiting for transfers between devices  34.8 us (32%)
  Pallas kernels  24 us (22%)
  between operations  1.49 us (1%)
  other arithmetic  1.45 us (1%)
    ppermute x18, starting transfers between devices, move(): return lax.ppermute(a, 'nodes', [(n, to(n)) for n in range(nodes)])  22.8 us
    ppermute x5, waiting for transfers between devices, swap(): return lax.ppermute(a, 'batch', [(b, b ^ mask) for b in range(batch)])  12.7 us
    ppermute x6, waiting for transfers between devices, shift(): return lax.ppermute(a, 'batch', [(b, to(b)) for b in range(batch)])  11.7 us
    ppermute x6, starting transfers between devices, shift(): return lax.ppermute(a, 'batch', [(b, to(b)) for b in range(batch)])  11 us
    ppermute x18, waiting for transfers between devices, move(): return lax.ppermute(a, 'nodes', [(n, to(n)) for n in range(nodes)])  10.4 us
    ppermute x5, starting transfers between devices, swap(): return lax.ppermute(a, 'batch', [(b, b ^ mask) for b in range(batch)])  7.46 us
    pallas_call x5, Pallas kernels, edges(): pl.pallas_call(kernel, out_shape=[jax.ShapeDtypeStruct((n, g, g), f32) fo...  7.16 us
    ppermute x1, starting transfers between devices, shift_by_core(): return lax.ppermute(a, ('nodes', 'batch'), pairs)  5 us
  transfers between devices with their start and end apart: 30, of which 7 were waited for; matrix products, arithmetic and copies ran while one was open for 1% of the time, Pallas kernels for 20%

profile of v5, /device:TPU:35, one launch (start us, length us, event | category | flops | bytes accessed | tf_op | source)
XLA Modules:
  0.0 108.1 jit_solution(4100836497447479151)
XLA Ops:
  0.6 1.4 %collective-permute-start = (f32[2,128,128]{2,1,0:T(8,128)}, f32[2,128,128]{2,1,0:T(8,128)S(1)}, u32[]{:S(2)}, u32[]{:S(2)}) collective-permute-start(f32[2,128,128]{2,1,0:T(8,128)} %refs_0_.1), channel_id=1, source_target_pairs={{0,1},{1,0},{2,3},{3,2},{4,5},{5,4},{6,7},{7,6},{8,9},{9,8},{10,11... | collective-permute-start | bytes 393224 | tf_op jit(solution)/shard_map/ppermute | solution.py:473
  2.0 3.3 %collective-permute-done.refs_1_.refs_0_ = f32[2,128,128]{2,1,0:T(8,128)S(1)} collective-permute-done((f32[2,128,128]{2,1,0:T(8,128)}, f32[2,128,128]{2,1,0:T(8,128)S(1)}, u32[]{:S(2)}, u32[]{:S(2)}) %collective-permute-start) | collective-permute-done | bytes 131104 | tf_op jit(solution)/shard_map/ppermute | solution.py:473
  6.2 2.8 %collective-permute-start.12 = (f32[4,128,128]{2,1,0:T(8,128)S(1)}, f32[4,128,128]{2,1,0:T(8,128)S(1)}, u32[]{:S(2)}, u32[]{:S(2)}) collective-permute-start(f32[4,128,128]{2,1,0:T(8,128)S(1)} %pack.2.refs_0_), channel_id=1, source_target_pairs={{0,3},{1,2},{2,1},{3,0},{4,7},{5,6},{6,5},{7,4},{8,11},{9,10},{10,... | collective-permute-start | bytes 786440 | tf_op jit(solution)/shard_map/ppermute | solution.py:473
  9.1 1.2 %collective-permute-start.2 = (f32[2,128,128]{2,1,0:T(8,128)}, f32[2,128,128]{2,1,0:T(8,128)S(1)}, u32[]{:S(2)}, u32[]{:S(2)}) collective-permute-start(f32[2,128,128]{2,1,0:T(8,128)} %refs_0_.1), channel_id=1, source_target_pairs={{0,64},{32,96},{64,128},{96,160},{128,192},{160,224},{192,0},{224,... | collective-permute-start | bytes 393224 | tf_op jit(solution)/shard_map/ppermute | solution.py:466
  11.1 1.9 %collective-permute-start.6 = (f32[2,128,128]{2,1,0:T(8,128)}, f32[2,128,128]{2,1,0:T(8,128)S(1)}, u32[]{:S(2)}, u32[]{:S(2)}) collective-permute-start(f32[2,128,128]{2,1,0:T(8,128)} %refs_0_.1), channel_id=1, source_target_pairs={{0,192},{32,224},{64,0},{96,32},{128,64},{160,96},{192,128},{224,1... | collective-permute-start | bytes 393224 | tf_op jit(solution)/shard_map/ppermute | solution.py:466
  13.0 2.6 %collective-permute-start.1 = (f32[2,128,128]{2,1,0:T(8,128)}, f32[2,128,128]{2,1,0:T(8,128)S(1)}, u32[]{:S(2)}, u32[]{:S(2)}) collective-permute-start(f32[2,128,128]{2,1,0:T(8,128)} %refs_0_.1), channel_id=1, source_target_pairs={{0,32},{32,0},{64,96},{96,64},{128,160},{160,128},{192,224},{224,1... | collective-permute-start | bytes 393224 | tf_op jit(solution)/shard_map/ppermute | solution.py:466
  15.6 1.6 %collective-permute-start.3 = (f32[2,128,128]{2,1,0:T(8,128)S(1)}, f32[2,128,128]{2,1,0:T(8,128)S(1)}, u32[]{:S(2)}, u32[]{:S(2)}) collective-permute-start(f32[2,128,128]{2,1,0:T(8,128)S(1)} %collective-permute-done.2.refs_2_), channel_id=1, source_target_pairs={{0,32},{32,0},{64,96},{96,64},{128,160},{160,128},{192,224},{224,1... | collective-permute-start | bytes 393224 | tf_op jit(solution)/shard_map/ppermute | solution.py:466
  17.3 2.2 %collective-permute-start.5 = (f32[2,128,128]{2,1,0:T(8,128)S(1)}, f32[2,128,128]{2,1,0:T(8,128)S(1)}, u32[]{:S(2)}, u32[]{:S(2)}) collective-permute-start(f32[2,128,128]{2,1,0:T(8,128)S(1)} %collective-permute-done.4.refs_4_), channel_id=1, source_target_pairs={{0,32},{32,0},{64,96},{96,64},{128,160},{160,128},{192,224},{224,1... | collective-permute-start | bytes 393224 | tf_op jit(solution)/shard_map/ppermute | solution.py:466
  20.8 1.1 %collective-permute-start.14 = (f32[6,128,128]{2,1,0:T(8,128)S(1)}, f32[6,128,128]{2,1,0:T(8,128)S(1)}, u32[]{:S(2)}, u32[]{:S(2)}) collective-permute-start(f32[6,128,128]{2,1,0:T(8,128)S(1)} %pack.3.refs_4_), channel_id=1, source_target_pairs={{0,64},{32,96},{64,128},{96,160},{128,192},{160,224},{192,0},{224,... | collective-permute-start | bytes 1179656 | tf_op jit(solution)/shard_map/ppermute | solution.py:466
  22.5 3.7 %fold.1 = (f32[4,16,128,128]{3,2,1,0:T(8,128)S(1)}, f32[64,128]{1,0:T(8,128)S(1)}) custom-call(s32[1]{0:T(128)S(6)} %copy.10.count.refs_1_, s32[2,128]{1,0:T(2,128)S(1)} %pad_add_fusion.slots_any.refs_0_, f32[128,128,128]{2,1,0:T(8,128)} %w_hbm.3), custom_call_target="tpu_custom_call" | custom-call | flops 20000000 | bytes 16777216 | tf_op jit(solution)/shard_map/fold/pallas_call | solution.py:83
  26.3 4.7 %forward.1 = (f32[4,128,128]{2,1,0:T(8,128)}, f32[4,128,128]{2,1,0:T(8,128)S(1)}, f32[16,128,128]{2,1,0:T(8,128)S(1)}, f32[64,128]{1,0:T(8,128)S(1)}, f32[16,128]{1,0:T(8,128)S(1)}) custom-call(s32[2,16]{1,0:T(2,128)S(1)} %bitcast.1, f32[4,128,128]{2,1,0:T(8,128)S(1)} %pack.2.refs_0_, f32[2,128,128]{2,1,0:T(8,128)S(1)} %collective-permute-done.1.refs_1_, ...), custom_call_target="tpu_custom_call" | custom-call | flops 1073741824 | bytes 8388608 | tf_op jit(solution)/shard_map/forward/pallas_call | solution.py:165
  31.0 1.3 %collective-permute-start.16 = (f32[6,128,128]{2,1,0:T(8,128)S(1)}, f32[6,128,128]{2,1,0:T(8,128)S(1)}, u32[]{:S(2)}, u32[]{:S(2)}) collective-permute-start(f32[6,128,128]{2,1,0:T(8,128)S(1)} %pack.3.refs_4_), channel_id=1, source_target_pairs={{0,128},{32,160},{64,192},{96,224},{128,0},{160,32},{192,64},{224,... | collective-permute-start | bytes 1179656 | tf_op jit(solution)/shard_map/ppermute | solution.py:466
  32.3 1.8 %collective-permute-start.18 = (f32[6,128,128]{2,1,0:T(8,128)S(1)}, f32[6,128,128]{2,1,0:T(8,128)S(1)}, u32[]{:S(2)}, u32[]{:S(2)}) collective-permute-start(f32[6,128,128]{2,1,0:T(8,128)S(1)} %pack.3.refs_4_), channel_id=1, source_target_pairs={{0,192},{32,224},{64,0},{96,32},{128,64},{160,96},{192,128},{224,1... | collective-permute-start | bytes 1179656 | tf_op jit(solution)/shard_map/ppermute | solution.py:466
  34.0 3.7 %backward.1 = (f32[2,128,128]{2,1,0:T(8,128)S(1)}, f32[2,128,128]{2,1,0:T(8,128)S(1)}, f32[2,128,128]{2,1,0:T(8,128)S(1)}, f32[2,128,128]{2,1,0:T(8,128)S(1)}, f32[8,128,128]{2,1,0:T(8,128)S(1)}) custom-call(s32[2,16]{1,0:T(2,128)S(1)} %bitcast.2, f32[4,16,128,128]{3,2,1,0:T(8,128)S(1)} %get-tuple-element.26.refs_8_.w_ref, ...), custom_call_target="tpu_custom_call" | custom-call | flops 1073741824 | bytes 8388608 | tf_op jit(solution)/shard_map/backward/pallas_call | solution.py:230
  39.2 3.8 %collective-permute-done.16.refs_8_ = f32[6,128,128]{2,1,0:T(8,128)S(1)} collective-permute-done((f32[6,128,128]{2,1,0:T(8,128)S(1)}, f32[6,128,128]{2,1,0:T(8,128)S(1)}, u32[]{:S(2)}, u32[]{:S(2)}) %collective-permute-start.16) | collective-permute-done | bytes 393248 | tf_op jit(solution)/shard_map/ppermute | solution.py:466
  43.0 1.9 %collective-permute-start.17 = (f32[6,128,128]{2,1,0:T(8,128)S(1)}, f32[6,128,128]{2,1,0:T(8,128)S(1)}, u32[]{:S(2)}, u32[]{:S(2)}) collective-permute-start(f32[6,128,128]{2,1,0:T(8,128)S(1)} %collective-permute-done.16.refs_8_), channel_id=1, source_target_pairs={{0,32},{32,0},{64,96},{96,64},{128,160},{160,128},{192,224},{224,1... | collective-permute-start | bytes 1179656 | tf_op jit(solution)/shard_map/ppermute | solution.py:466
  44.9 6.6 %collective-permute-done.18.refs_10_ = f32[6,128,128]{2,1,0:T(8,128)S(1)} collective-permute-done((f32[6,128,128]{2,1,0:T(8,128)S(1)}, f32[6,128,128]{2,1,0:T(8,128)S(1)}, u32[]{:S(2)}, u32[]{:S(2)}) %collective-permute-start.18) | collective-permute-done | bytes 393248 | tf_op jit(solution)/shard_map/ppermute | solution.py:466
  52.9 2.6 %collective-permute-start.22 = (f32[4,128,128]{2,1,0:T(8,128)S(1)}, f32[4,128,128]{2,1,0:T(8,128)S(1)}, u32[]{:S(2)}, u32[]{:S(2)}) collective-permute-start(f32[4,128,128]{2,1,0:T(8,128)S(1)} %get-tuple-element.29.fx.refs_5_), channel_id=1, source_target_pairs={{0,2},{1,3},{2,0},{3,1},{4,6},{5,7},{6,4},{7,5},{8,10},{9,11},{10,... | collective-permute-start | bytes 786440 | tf_op jit(solution)/shard_map/ppermute | solution.py:473
  55.6 2.0 %spread.1 = (bf16[16,256,512]{2,1,0:T(8,128)(2,1)S(1)}, f32[4,16,128]{2,1,0:T(8,128)S(1)}) custom-call(s32[2,16]{1,0:T(2,128)S(1)} %bitcast.3, f32[2,128,128]{2,1,0:T(8,128)S(1)} %get-tuple-element.49.refs_1_, f32[16,128,128]{2,1,0:T(8,128)S(1)} %get-tuple-element.31.e_ref.refs_2_, f32[16,128]{1,0:T(8,128)S(1)} %get-tuple-element.37.refs_3_, ...), custom_call_target="tpu_custom_call" | custom-call | flops 10000000 | bytes 10485760 | tf_op jit(solution)/shard_map/spread/pallas_call | solution.py:309
  57.6 2.5 %collective-permute-done.20.refs_6_ = f32[4,128,128]{2,1,0:T(8,128)S(1)} collective-permute-done((f32[4,128,128]{2,1,0:T(8,128)S(1)}, f32[4,128,128]{2,1,0:T(8,128)S(1)}, u32[]{:S(2)}, u32[]{:S(2)}) %collective-permute-start.20) | collective-permute-done | bytes 262176 | tf_op jit(solution)/shard_map/ppermute | solution.py:473
  60.1 6.9 %collective-permute-done.21.refs_7_ = f32[4,128,128]{2,1,0:T(8,128)S(1)} collective-permute-done((f32[4,128,128]{2,1,0:T(8,128)S(1)}, f32[4,128,128]{2,1,0:T(8,128)S(1)}, u32[]{:S(2)}, u32[]{:S(2)}) %collective-permute-start.21) | collective-permute-done | bytes 262176 | tf_op jit(solution)/shard_map/ppermute | solution.py:473
  68.1 1.7 %collective-permute-start.25 = (f32[4,128,128]{2,1,0:T(8,128)S(1)}, f32[4,128,128]{2,1,0:T(8,128)S(1)}, u32[]{:S(2)}, u32[]{:S(2)}) collective-permute-start(f32[4,128,128]{2,1,0:T(8,128)S(1)} %edges.5.refs_9_), channel_id=1, source_target_pairs={{0,4},{1,5},{2,6},{3,7},{4,8},{5,9},{6,10},{7,11},{8,12},{9,13},{1... | collective-permute-start | bytes 786440 | tf_op jit(solution)/shard_map/ppermute | solution.py:470
  71.0 1.1 %edges.7.refs_9_ = f32[4,128,128]{2,1,0:T(8,128)S(1)} custom-call(s32[2,128]{1,0:T(2,128)S(1)} %pad_add_fusion.slots_any.refs_0_, s32[1]{0:T(128)S(6)} %copy.10.count.refs_1_, bf16[16,256,512]{2,1,0:T(8,128)(2,1)S(1)} %get-tuple-element.38.refs_2_, f32[4,16,128]{2,1,0:T(8,128)S(1)} %get-tuple-element.39.refs_3_.refs_9_, ...), custom_call_target="tpu_custom_call" | custom-call | flops 268435456 | bytes 6291456 | tf_op jit(solution)/shard_map/edges/pallas_call | solution.py:374
  72.1 5.0 %collective-permute-start.27 = (f32[4,128,128]{2,1,0:T(8,128)S(1)}, f32[4,128,128]{2,1,0:T(8,128)S(1)}, u32[]{:S(2)}, u32[]{:S(2)}) collective-permute-start(f32[4,128,128]{2,1,0:T(8,128)S(1)} %edges.7.refs_9_), channel_id=1, source_target_pairs={{0,8},{1,9},{2,10},{3,11},{4,12},{5,13},{6,14},{7,15},{8,16},{9,17... | collective-permute-start | bytes 786440 | tf_op jit(solution)/shard_map/ppermute | solution.py:481
  77.1 1.8 %collective-permute-start.10 = (f32[2,128,128]{2,1,0:T(8,128)S(1)}, f32[2,128,128]{2,1,0:T(8,128)S(1)}, u32[]{:S(2)}, u32[]{:S(2)}) collective-permute-start(f32[2,128,128]{2,1,0:T(8,128)S(1)} %get-tuple-element.51), channel_id=1, source_target_pairs={{0,128},{32,160},{64,192},{96,224},{128,0},{160,32},{192,64},{224,... | collective-permute-start | bytes 393224 | tf_op jit(solution)/shard_map/ppermute | solution.py:466
  78.9 1.8 %collective-permute-start.9 = (f32[2,128,128]{2,1,0:T(8,128)S(1)}, f32[2,128,128]{2,1,0:T(8,128)S(1)}, u32[]{:S(2)}, u32[]{:S(2)}) collective-permute-start(f32[2,128,128]{2,1,0:T(8,128)S(1)} %get-tuple-element.49.refs_1_), channel_id=1, source_target_pairs={{0,64},{32,96},{64,128},{96,160},{128,192},{160,224},{192,0},{224,... | collective-permute-start | bytes 393224 | tf_op jit(solution)/shard_map/ppermute | solution.py:466
  80.6 2.1 %edges.8 = (f32[4,128,128]{2,1,0:T(8,128)S(1)}, f32[4,128,128]{2,1,0:T(8,128)S(1)}, f32[4,128,128]{2,1,0:T(8,128)S(1)}) custom-call(s32[2,128]{1,0:T(2,128)S(1)} %pad_add_fusion.slots_any.refs_0_, s32[1]{0:T(128)S(6)} %copy.10.count.refs_1_, bf16[16,256,512]{2,1,0:T(8,128)(2,1)S(1)} %get-tuple-element.38.refs_2_, ...), custom_call_target="tpu_custom_call" | custom-call | flops 805306368 | bytes 6291456 | tf_op jit(solution)/shard_map/edges/pallas_call | solution.py:374
  82.8 1.8 %edges.9 = (f32[4,128,128]{2,1,0:T(8,128)S(1)}, f32[4,128,128]{2,1,0:T(8,128)S(1)}) custom-call(s32[2,128]{1,0:T(2,128)S(1)} %pad_add_fusion.slots_any.refs_0_, s32[1]{0:T(128)S(6)} %copy.10.count.refs_1_, bf16[16,256,512]{2,1,0:T(8,128)(2,1)S(1)} %get-tuple-element.38.refs_2_, f32[4,16,128]{2,1,0:T(8,128)S(1)} %get-tuple-element.39.refs_3_.refs_9_, ...), custom_call_target="tpu_custom_call" | custom-call | flops 536870912 | bytes 6291456 | tf_op jit(solution)/shard_map/edges/pallas_call | solution.py:374
  85.6 4.5 %collective-permute-start.23 = (f32[4,128,128]{2,1,0:T(8,128)S(1)}, f32[4,128,128]{2,1,0:T(8,128)S(1)}, u32[]{:S(2)}, u32[]{:S(2)}) collective-permute-start(f32[4,128,128]{2,1,0:T(8,128)S(1)} %get-tuple-element.43), channel_id=1, source_target_pairs={{0,4},{1,5},{2,6},{3,7},{4,8},{5,9},{6,10},{7,11},{8,12},{9,13},{1... | collective-permute-start | bytes 786440 | tf_op jit(solution)/shard_map/ppermute | solution.py:470
  90.5 3.4 %collective-permute-start.29 = (f32[4,128,128]{2,1,0:T(8,128)S(1)}, f32[4,128,128]{2,1,0:T(8,128)S(1)}, u32[]{:S(2)}, u32[]{:S(2)}) collective-permute-start(f32[4,128,128]{2,1,0:T(8,128)S(1)} %get-tuple-element.48), channel_id=1, source_target_pairs={{0,24},{1,25},{2,26},{3,27},{4,28},{5,29},{6,30},{7,31},{8,0},{9,1... | collective-permute-start | bytes 786440 | tf_op jit(solution)/shard_map/ppermute | solution.py:470
  95.6 6.3 %collective-permute-done.23.refs_0_ = f32[4,128,128]{2,1,0:T(8,128)S(1)} collective-permute-done((f32[4,128,128]{2,1,0:T(8,128)S(1)}, f32[4,128,128]{2,1,0:T(8,128)S(1)}, u32[]{:S(2)}, u32[]{:S(2)}) %collective-permute-start.23) | collective-permute-done | bytes 262176 | tf_op jit(solution)/shard_map/ppermute | solution.py:470
  101.9 5.4 %collective-permute-done.28.refs_2_ = f32[4,128,128]{2,1,0:T(8,128)S(1)} collective-permute-done((f32[4,128,128]{2,1,0:T(8,128)S(1)}, f32[4,128,128]{2,1,0:T(8,128)S(1)}, u32[]{:S(2)}, u32[]{:S(2)}) %collective-permute-start.28) | collective-permute-done | bytes 262176 | tf_op jit(solution)/shard_map/ppermute | solution.py:470
  (49 shorter events, 12.2 us)
Async XLA Ops:
  0.6 4.7 %collective-permute-start = (f32[2,128,128]{2,1,0:T(8,128)}, f32[2,128,128]{2,1,0:T(8,128)S(1)}, u32[]{:S(2)}, u32[]{:S(2)}) collective-permute-start(f32[2,128,128]{2,1,0:T(8,128)} %refs_0_.1), channel_id=1, source_target_pairs={{0,1},{1,0},{2,3},{3,2},{4,5},{5,4},{6,7},{7,6},{8,9},{9,8},{10,11... | collective-permute-start | bytes 393224 | tf_op jit(solution)/shard_map/ppermute | solution.py:473
  6.2 14.5 %collective-permute-start.12 = (f32[4,128,128]{2,1,0:T(8,128)S(1)}, f32[4,128,128]{2,1,0:T(8,128)S(1)}, u32[]{:S(2)}, u32[]{:S(2)}) collective-permute-start(f32[4,128,128]{2,1,0:T(8,128)S(1)} %pack.2.refs_0_), channel_id=1, source_target_pairs={{0,3},{1,2},{2,1},{3,0},{4,7},{5,6},{6,5},{7,4},{8,11},{9,10},{10,... | collective-permute-start | bytes 786440 | tf_op jit(solution)/shard_map/ppermute | solution.py:473
  9.1 6.6 %collective-permute-start.2 = (f32[2,128,128]{2,1,0:T(8,128)}, f32[2,128,128]{2,1,0:T(8,128)S(1)}, u32[]{:S(2)}, u32[]{:S(2)}) collective-permute-start(f32[2,128,128]{2,1,0:T(8,128)} %refs_0_.1), channel_id=1, source_target_pairs={{0,64},{32,96},{64,128},{96,160},{128,192},{160,224},{192,0},{224,... | collective-permute-start | bytes 393224 | tf_op jit(solution)/shard_map/ppermute | solution.py:466
  10.3 7.0 %collective-permute-start.4 = (f32[2,128,128]{2,1,0:T(8,128)}, f32[2,128,128]{2,1,0:T(8,128)S(1)}, u32[]{:S(2)}, u32[]{:S(2)}) collective-permute-start(f32[2,128,128]{2,1,0:T(8,128)} %refs_0_.1), channel_id=1, source_target_pairs={{0,128},{32,160},{64,192},{96,224},{128,0},{160,32},{192,64},{224,... | collective-permute-start | bytes 393224 | tf_op jit(solution)/shard_map/ppermute | solution.py:466
  11.1 8.4 %collective-permute-start.6 = (f32[2,128,128]{2,1,0:T(8,128)}, f32[2,128,128]{2,1,0:T(8,128)S(1)}, u32[]{:S(2)}, u32[]{:S(2)}) collective-permute-start(f32[2,128,128]{2,1,0:T(8,128)} %refs_0_.1), channel_id=1, source_target_pairs={{0,192},{32,224},{64,0},{96,32},{128,64},{160,96},{192,128},{224,1... | collective-permute-start | bytes 393224 | tf_op jit(solution)/shard_map/ppermute | solution.py:466
  13.0 13.3 %collective-permute-start.1 = (f32[2,128,128]{2,1,0:T(8,128)}, f32[2,128,128]{2,1,0:T(8,128)S(1)}, u32[]{:S(2)}, u32[]{:S(2)}) collective-permute-start(f32[2,128,128]{2,1,0:T(8,128)} %refs_0_.1), channel_id=1, source_target_pairs={{0,32},{32,0},{64,96},{96,64},{128,160},{160,128},{192,224},{224,1... | collective-permute-start | bytes 393224 | tf_op jit(solution)/shard_map/ppermute | solution.py:466
  15.6 10.6 %collective-permute-start.3 = (f32[2,128,128]{2,1,0:T(8,128)S(1)}, f32[2,128,128]{2,1,0:T(8,128)S(1)}, u32[]{:S(2)}, u32[]{:S(2)}) collective-permute-start(f32[2,128,128]{2,1,0:T(8,128)S(1)} %collective-permute-done.2.refs_2_), channel_id=1, source_target_pairs={{0,32},{32,0},{64,96},{96,64},{128,160},{160,128},{192,224},{224,1... | collective-permute-start | bytes 393224 | tf_op jit(solution)/shard_map/ppermute | solution.py:466
  17.3 9.0 %collective-permute-start.5 = (f32[2,128,128]{2,1,0:T(8,128)S(1)}, f32[2,128,128]{2,1,0:T(8,128)S(1)}, u32[]{:S(2)}, u32[]{:S(2)}) collective-permute-start(f32[2,128,128]{2,1,0:T(8,128)S(1)} %collective-permute-done.4.refs_4_), channel_id=1, source_target_pairs={{0,32},{32,0},{64,96},{96,64},{128,160},{160,128},{192,224},{224,1... | collective-permute-start | bytes 393224 | tf_op jit(solution)/shard_map/ppermute | solution.py:466
  19.5 6.8 %collective-permute-start.7 = (f32[2,128,128]{2,1,0:T(8,128)S(1)}, f32[2,128,128]{2,1,0:T(8,128)S(1)}, u32[]{:S(2)}, u32[]{:S(2)}) collective-permute-start(f32[2,128,128]{2,1,0:T(8,128)S(1)} %collective-permute-done.6.refs_6_), channel_id=1, source_target_pairs={{0,32},{32,0},{64,96},{96,64},{128,160},{160,128},{192,224},{224,1... | collective-permute-start | bytes 393224 | tf_op jit(solution)/shard_map/ppermute | solution.py:466
  20.8 18.2 %collective-permute-start.14 = (f32[6,128,128]{2,1,0:T(8,128)S(1)}, f32[6,128,128]{2,1,0:T(8,128)S(1)}, u32[]{:S(2)}, u32[]{:S(2)}) collective-permute-start(f32[6,128,128]{2,1,0:T(8,128)S(1)} %pack.3.refs_4_), channel_id=1, source_target_pairs={{0,64},{32,96},{64,128},{96,160},{128,192},{160,224},{192,0},{224,... | collective-permute-start | bytes 1179656 | tf_op jit(solution)/shard_map/ppermute | solution.py:466
  22.5 3.7 %copy-start = (f32[4,128,128]{2,1,0:T(8,128)S(1)}, f32[4,128,128]{2,1,0:T(8,128)}, u32[]{:S(2)}) copy-start(f32[4,128,128]{2,1,0:T(8,128)} %refs_10_.1) | copy-start | bytes 786436
  22.5 3.7 %copy-start.1 = (s32[16,2]{0,1:T(2,128)S(1)}, s32[16,2]{0,1:T(2,128)}, u32[]{:S(2)}) copy-start(s32[16,2]{0,1:T(2,128)} %param.8) | copy-start | bytes 388
  31.0 12.0 %collective-permute-start.16 = (f32[6,128,128]{2,1,0:T(8,128)S(1)}, f32[6,128,128]{2,1,0:T(8,128)S(1)}, u32[]{:S(2)}, u32[]{:S(2)}) collective-permute-start(f32[6,128,128]{2,1,0:T(8,128)S(1)} %pack.3.refs_4_), channel_id=1, source_target_pairs={{0,128},{32,160},{64,192},{96,224},{128,0},{160,32},{192,64},{224,... | collective-permute-start | bytes 1179656 | tf_op jit(solution)/shard_map/ppermute | solution.py:466
  32.3 19.2 %collective-permute-start.18 = (f32[6,128,128]{2,1,0:T(8,128)S(1)}, f32[6,128,128]{2,1,0:T(8,128)S(1)}, u32[]{:S(2)}, u32[]{:S(2)}) collective-permute-start(f32[6,128,128]{2,1,0:T(8,128)S(1)} %pack.3.refs_4_), channel_id=1, source_target_pairs={{0,192},{32,224},{64,0},{96,32},{128,64},{160,96},{192,128},{224,1... | collective-permute-start | bytes 1179656 | tf_op jit(solution)/shard_map/ppermute | solution.py:466
  37.7 14.5 %collective-permute-start.8 = (f32[8,128,128]{2,1,0:T(8,128)S(1)}, f32[8,128,128]{2,1,0:T(8,128)S(1)}, u32[]{:S(2)}, u32[]{:S(2)}) collective-permute-start(f32[8,128,128]{2,1,0:T(8,128)S(1)} %get-tuple-element.33), channel_id=1, source_target_pairs={{0,32},{32,0},{64,96},{96,64},{128,160},{160,128},{192,224},{224,1... | collective-permute-start | bytes 1572872 | tf_op jit(solution)/shard_map/ppermute | solution.py:466
  38.7 13.6 %collective-permute-start.13 = (f32[6,128,128]{2,1,0:T(8,128)S(1)}, f32[6,128,128]{2,1,0:T(8,128)S(1)}, u32[]{:S(2)}, u32[]{:S(2)}) collective-permute-start(f32[6,128,128]{2,1,0:T(8,128)S(1)} %pack.3.refs_4_), channel_id=1, source_target_pairs={{0,32},{32,0},{64,96},{96,64},{128,160},{160,128},{192,224},{224,1... | collective-permute-start | bytes 1179656 | tf_op jit(solution)/shard_map/ppermute | solution.py:466
  38.9 13.9 %collective-permute-start.15 = (f32[6,128,128]{2,1,0:T(8,128)S(1)}, f32[6,128,128]{2,1,0:T(8,128)S(1)}, u32[]{:S(2)}, u32[]{:S(2)}) collective-permute-start(f32[6,128,128]{2,1,0:T(8,128)S(1)} %collective-permute-done.14.refs_6_), channel_id=1, source_target_pairs={{0,32},{32,0},{64,96},{96,64},{128,160},{160,128},{192,224},{224,1... | collective-permute-start | bytes 1179656 | tf_op jit(solution)/shard_map/ppermute | solution.py:466
  43.0 12.6 %collective-permute-start.17 = (f32[6,128,128]{2,1,0:T(8,128)S(1)}, f32[6,128,128]{2,1,0:T(8,128)S(1)}, u32[]{:S(2)}, u32[]{:S(2)}) collective-permute-start(f32[6,128,128]{2,1,0:T(8,128)S(1)} %collective-permute-done.16.refs_8_), channel_id=1, source_target_pairs={{0,32},{32,0},{64,96},{96,64},{128,160},{160,128},{192,224},{224,1... | collective-permute-start | bytes 1179656 | tf_op jit(solution)/shard_map/ppermute | solution.py:466
  51.5 4.1 %collective-permute-start.19 = (f32[6,128,128]{2,1,0:T(8,128)S(1)}, f32[6,128,128]{2,1,0:T(8,128)S(1)}, u32[]{:S(2)}, u32[]{:S(2)}) collective-permute-start(f32[6,128,128]{2,1,0:T(8,128)S(1)} %collective-permute-done.18.refs_10_), channel_id=1, source_target_pairs={{0,32},{32,0},{64,96},{96,64},{128,160},{160,128},{192,224},{224,1... | collective-permute-start | bytes 1179656 | tf_op jit(solution)/shard_map/ppermute | solution.py:466
  52.2 7.9 %collective-permute-start.20 = (f32[4,128,128]{2,1,0:T(8,128)S(1)}, f32[4,128,128]{2,1,0:T(8,128)S(1)}, u32[]{:S(2)}, u32[]{:S(2)}) collective-permute-start(f32[4,128,128]{2,1,0:T(8,128)S(1)} %get-tuple-element.29.fx.refs_5_), channel_id=1, source_target_pairs={{0,1},{1,0},{2,3},{3,2},{4,5},{5,4},{6,7},{7,6},{8,9},{9,8},{10,11... | collective-permute-start | bytes 786440 | tf_op jit(solution)/shard_map/ppermute | solution.py:473
  52.2 14.7 %collective-permute-start.21 = (f32[4,128,128]{2,1,0:T(8,128)S(1)}, f32[4,128,128]{2,1,0:T(8,128)S(1)}, u32[]{:S(2)}, u32[]{:S(2)}) collective-permute-start(f32[4,128,128]{2,1,0:T(8,128)S(1)} %get-tuple-element.29.fx.refs_5_), channel_id=1, source_target_pairs={{0,3},{1,2},{2,1},{3,0},{4,7},{5,6},{6,5},{7,4},{8,11},{9,10},{10,... | collective-permute-start | bytes 786440 | tf_op jit(solution)/shard_map/ppermute | solution.py:473
  52.9 14.1 %collective-permute-start.22 = (f32[4,128,128]{2,1,0:T(8,128)S(1)}, f32[4,128,128]{2,1,0:T(8,128)S(1)}, u32[]{:S(2)}, u32[]{:S(2)}) collective-permute-start(f32[4,128,128]{2,1,0:T(8,128)S(1)} %get-tuple-element.29.fx.refs_5_), channel_id=1, source_target_pairs={{0,2},{1,3},{2,0},{3,1},{4,6},{5,7},{6,4},{7,5},{8,10},{9,11},{10,... | collective-permute-start | bytes 786440 | tf_op jit(solution)/shard_map/ppermute | solution.py:473
  68.1 10.8 %collective-permute-start.25 = (f32[4,128,128]{2,1,0:T(8,128)S(1)}, f32[4,128,128]{2,1,0:T(8,128)S(1)}, u32[]{:S(2)}, u32[]{:S(2)}) collective-permute-start(f32[4,128,128]{2,1,0:T(8,128)S(1)} %edges.5.refs_9_), channel_id=1, source_target_pairs={{0,4},{1,5},{2,6},{3,7},{4,8},{5,9},{6,10},{7,11},{8,12},{9,13},{1... | collective-permute-start | bytes 786440 | tf_op jit(solution)/shard_map/ppermute | solution.py:470
  70.9 13.7 %collective-permute-start.26 = (f32[4,128,128]{2,1,0:T(8,128)S(1)}, f32[4,128,128]{2,1,0:T(8,128)S(1)}, u32[]{:S(2)}, u32[]{:S(2)}) collective-permute-start(f32[4,128,128]{2,1,0:T(8,128)S(1)} %edges.6.refs_9_), channel_id=1, source_target_pairs={{0,28},{1,29},{2,30},{3,31},{4,0},{5,1},{6,2},{7,3},{8,4},{9,5},{1... | collective-permute-start | bytes 786440 | tf_op jit(solution)/shard_map/ppermute | solution.py:470
  72.1 13.5 %collective-permute-start.27 = (f32[4,128,128]{2,1,0:T(8,128)S(1)}, f32[4,128,128]{2,1,0:T(8,128)S(1)}, u32[]{:S(2)}, u32[]{:S(2)}) collective-permute-start(f32[4,128,128]{2,1,0:T(8,128)S(1)} %edges.7.refs_9_), channel_id=1, source_target_pairs={{0,8},{1,9},{2,10},{3,11},{4,12},{5,13},{6,14},{7,15},{8,16},{9,17... | collective-permute-start | bytes 786440 | tf_op jit(solution)/shard_map/ppermute | solution.py:481
  77.1 13.1 %collective-permute-start.11 = (f32[2,128,128]{2,1,0:T(8,128)S(1)}, f32[2,128,128]{2,1,0:T(8,128)S(1)}, u32[]{:S(2)}, u32[]{:S(2)}) collective-permute-start(f32[2,128,128]{2,1,0:T(8,128)S(1)} %get-tuple-element.50), channel_id=1, source_target_pairs={{0,192},{32,224},{64,0},{96,32},{128,64},{160,96},{192,128},{224,1... | collective-permute-start | bytes 393224 | tf_op jit(solution)/shard_map/ppermute | solution.py:466
  77.1 13.4 %collective-permute-start.10 = (f32[2,128,128]{2,1,0:T(8,128)S(1)}, f32[2,128,128]{2,1,0:T(8,128)S(1)}, u32[]{:S(2)}, u32[]{:S(2)}) collective-permute-start(f32[2,128,128]{2,1,0:T(8,128)S(1)} %get-tuple-element.51), channel_id=1, source_target_pairs={{0,128},{32,160},{64,192},{96,224},{128,0},{160,32},{192,64},{224,... | collective-permute-start | bytes 393224 | tf_op jit(solution)/shard_map/ppermute | solution.py:466
  78.9 15.0 %collective-permute-start.9 = (f32[2,128,128]{2,1,0:T(8,128)S(1)}, f32[2,128,128]{2,1,0:T(8,128)S(1)}, u32[]{:S(2)}, u32[]{:S(2)}) collective-permute-start(f32[2,128,128]{2,1,0:T(8,128)S(1)} %get-tuple-element.49.refs_1_), channel_id=1, source_target_pairs={{0,64},{32,96},{64,128},{96,160},{128,192},{160,224},{192,0},{224,... | collective-permute-start | bytes 393224 | tf_op jit(solution)/shard_map/ppermute | solution.py:466
  84.6 17.3 %collective-permute-start.24 = (f32[4,128,128]{2,1,0:T(8,128)S(1)}, f32[4,128,128]{2,1,0:T(8,128)S(1)}, u32[]{:S(2)}, u32[]{:S(2)}) collective-permute-start(f32[4,128,128]{2,1,0:T(8,128)S(1)} %get-tuple-element.44.refs_9_), channel_id=1, source_target_pairs={{0,28},{1,29},{2,30},{3,31},{4,0},{5,1},{6,2},{7,3},{8,4},{9,5},{1... | collective-permute-start | bytes 786440 | tf_op jit(solution)/shard_map/ppermute | solution.py:470
  85.6 16.2 %collective-permute-start.23 = (f32[4,128,128]{2,1,0:T(8,128)S(1)}, f32[4,128,128]{2,1,0:T(8,128)S(1)}, u32[]{:S(2)}, u32[]{:S(2)}) collective-permute-start(f32[4,128,128]{2,1,0:T(8,128)S(1)} %get-tuple-element.43), channel_id=1, source_target_pairs={{0,4},{1,5},{2,6},{3,7},{4,8},{5,9},{6,10},{7,11},{8,12},{9,13},{1... | collective-permute-start | bytes 786440 | tf_op jit(solution)/shard_map/ppermute | solution.py:470
  90.2 17.1 %collective-permute-start.28 = (f32[4,128,128]{2,1,0:T(8,128)S(1)}, f32[4,128,128]{2,1,0:T(8,128)S(1)}, u32[]{:S(2)}, u32[]{:S(2)}) collective-permute-start(f32[4,128,128]{2,1,0:T(8,128)S(1)} %get-tuple-element.47), channel_id=1, source_target_pairs={{0,8},{1,9},{2,10},{3,11},{4,12},{5,13},{6,14},{7,15},{8,16},{9,17... | collective-permute-start | bytes 786440 | tf_op jit(solution)/shard_map/ppermute | solution.py:470
  90.5 16.8 %collective-permute-start.29 = (f32[4,128,128]{2,1,0:T(8,128)S(1)}, f32[4,128,128]{2,1,0:T(8,128)S(1)}, u32[]{:S(2)}, u32[]{:S(2)}) collective-permute-start(f32[4,128,128]{2,1,0:T(8,128)S(1)} %get-tuple-element.48), channel_id=1, source_target_pairs={{0,24},{1,25},{2,26},{3,27},{4,28},{5,29},{6,30},{7,31},{8,0},{9,1... | collective-permute-start | bytes 786440 | tf_op jit(solution)/shard_map/ppermute | solution.py:470

commit v6 on v4

--- a/solution.py
+++ b/solution.py
@@ -390,22 +390,21 @@
     )(slots, count, ehl, pk, bias, *fxs, token)
 
 
-def join_kernel(ap, am, bp, bm, c_ref, outp, outm):
-    first = (lax.axis_index("nodes") % CORES == 0).astype(f32)
-    outp[...] = (ap[...] + bp[...]) + c_ref[...] * first
-    outm[...] = (am[...] + bm[...]) + c_ref[...] * (1.0 - first)
-
-
-def join(ap, am, bp, bm, c):
-    return pl.pallas_call(
-        join_kernel,
-        out_shape=[jax.ShapeDtypeStruct(ap.shape, f32)] * 2,
-        in_specs=vmem_specs(5),
-        out_specs=vmem_specs(2),
+def join_kernel(core, a, b, c, out):
+    mine = (lax.axis_index("nodes") % CORES == core).astype(f32)
+    out[...] = (a[...] + b[...]) + c[...] * mine
+
+
+def join(a, b, c, core):
+    return pl.pallas_call(
+        functools.partial(join_kernel, core),
+        out_shape=jax.ShapeDtypeStruct(a.shape, f32),
+        in_specs=vmem_specs(3),
+        out_specs=vmem_specs(1)[0],
         compiler_params=pltpu.CompilerParams(vmem_limit_bytes=4 << 20),
-        cost_estimate=pl.CostEstimate(flops=400_000, bytes_accessed=2 << 20, transcendentals=0),
+        cost_estimate=pl.CostEstimate(flops=200_000, bytes_accessed=1 << 20, transcendentals=0),
         name="join",
-    )(ap, am, bp, bm, c)
+    )(a, b, c)
 
 
 def near_kernel(w_hbm, a_ref, near, w, sem):
@@ -513,8 +512,10 @@
     e1p, e1m, e0 = part(e3m, (1,), (-1,), (0,))
     r1p, r1m = shift(e1p, 1), shift(e1m, -1)
     e2p, e2m = part(e1m, (2,), (-2,))
-    c2p, c2m = join(e2p, e2m, r3p, r3m, r4)
-    r2p, r2m = shift(c2p, 2), shift(c2m, -2)
+    c2m = join(e2m, r3m, r4, 1)
+    r2m = shift(c2m, -2)
+    c2p = join(e2p, r3p, r4, 0)
+    r2p = shift(c2p, 2)
     leaf_flow = functools.reduce(
         jnp.add, [flows[0]] + [move(flows[dx], dx) for dx in range(1, chips)]
     )

time: 109 us -> 111 us (1.018)
  the two profiles are of different devices: /device:TPU:32 before, /device:TPU:6 now
where the time goes in v6:
time: 111 us
  waiting for transfers between devices  52 us (47%)
  starting transfers between devices  32.4 us (29%)
  Pallas kernels  23.6 us (21%)
  between operations  1.5 us (1%)
  other arithmetic  1.45 us (1%)
    ppermute x18, waiting for transfers between devices, move(): return lax.ppermute(a, 'nodes', [(n, to(n)) for n in range(nodes)])  20.9 us
    ppermute x6, waiting for transfers between devices, shift(): return lax.ppermute(a, 'batch', [(b, to(b)) for b in range(batch)])  17.8 us
    ppermute x5, waiting for transfers between devices, swap(): return lax.ppermute(a, 'batch', [(b, b ^ mask) for b in range(batch)])  13.3 us
    ppermute x6, starting transfers between devices, shift(): return lax.ppermute(a, 'batch', [(b, to(b)) for b in range(batch)])  10.9 us
    ppermute x18, starting transfers between devices, move(): return lax.ppermute(a, 'nodes', [(n, to(n)) for n in range(nodes)])  9.37 us
    ppermute x5, starting transfers between devices, swap(): return lax.ppermute(a, 'batch', [(b, b ^ mask) for b in range(batch)])  8.86 us
    pallas_call x4, Pallas kernels, edges(): pl.pallas_call(kernel, out_shape=[jax.ShapeDtypeStruct((n, g, g), f32) fo...  6.75 us
    pallas_call x1, Pallas kernels, forward(): pl.pallas_call(functools.partial(forward_kernel, nodes), out_shape=(jax.S...  4.66 us
  transfers between devices with their start and end apart: 30, of which 11 were waited for; matrix products, arithmetic and copies ran while one was open for 1% of the time, Pallas kernels for 17%

profile of v6, /device:TPU:6, one launch (start us, length us, event | category | flops | bytes accessed | tf_op | source)
XLA Modules:
  0.0 110.9 jit_solution(130208641066398505)
XLA Ops:
  0.6 1.7 %collective-permute-start = (f32[2,128,128]{2,1,0:T(8,128)}, f32[2,128,128]{2,1,0:T(8,128)S(1)}, u32[]{:S(2)}, u32[]{:S(2)}) collective-permute-start(f32[2,128,128]{2,1,0:T(8,128)} %refs_0_.1), channel_id=1, source_target_pairs={{0,1},{1,0},{2,3},{3,2},{4,5},{5,4},{6,7},{7,6},{8,9},{9,8},{10,11... | collective-permute-start | bytes 393224 | tf_op jit(solution)/shard_map/ppermute | solution.py:472
  2.3 3.9 %collective-permute-done.refs_1_.refs_0_ = f32[2,128,128]{2,1,0:T(8,128)S(1)} collective-permute-done((f32[2,128,128]{2,1,0:T(8,128)}, f32[2,128,128]{2,1,0:T(8,128)S(1)}, u32[]{:S(2)}, u32[]{:S(2)}) %collective-permute-start) | collective-permute-done | bytes 131104 | tf_op jit(solution)/shard_map/ppermute | solution.py:472
  7.1 3.1 %collective-permute-start.12 = (f32[4,128,128]{2,1,0:T(8,128)S(1)}, f32[4,128,128]{2,1,0:T(8,128)S(1)}, u32[]{:S(2)}, u32[]{:S(2)}) collective-permute-start(f32[4,128,128]{2,1,0:T(8,128)S(1)} %pack.2.refs_0_), channel_id=1, source_target_pairs={{0,3},{1,2},{2,1},{3,0},{4,7},{5,6},{6,5},{7,4},{8,11},{9,10},{10,... | collective-permute-start | bytes 786440 | tf_op jit(solution)/shard_map/ppermute | solution.py:472
  10.7 2.4 %collective-permute-start.4 = (f32[2,128,128]{2,1,0:T(8,128)}, f32[2,128,128]{2,1,0:T(8,128)S(1)}, u32[]{:S(2)}, u32[]{:S(2)}) collective-permute-start(f32[2,128,128]{2,1,0:T(8,128)} %refs_0_.1), channel_id=1, source_target_pairs={{0,128},{32,160},{64,192},{96,224},{128,0},{160,32},{192,64},{224,... | collective-permute-start | bytes 393224 | tf_op jit(solution)/shard_map/ppermute | solution.py:465
  13.1 2.8 %collective-permute-done.2.refs_2_ = f32[2,128,128]{2,1,0:T(8,128)S(1)} collective-permute-done((f32[2,128,128]{2,1,0:T(8,128)}, f32[2,128,128]{2,1,0:T(8,128)S(1)}, u32[]{:S(2)}, u32[]{:S(2)}) %collective-permute-start.2) | collective-permute-done | bytes 131104 | tf_op jit(solution)/shard_map/ppermute | solution.py:465
  15.9 2.2 %collective-permute-done.4.refs_4_ = f32[2,128,128]{2,1,0:T(8,128)S(1)} collective-permute-done((f32[2,128,128]{2,1,0:T(8,128)}, f32[2,128,128]{2,1,0:T(8,128)S(1)}, u32[]{:S(2)}, u32[]{:S(2)}) %collective-permute-start.4) | collective-permute-done | bytes 131104 | tf_op jit(solution)/shard_map/ppermute | solution.py:465
  18.1 1.4 %collective-permute-done.6.refs_6_ = f32[2,128,128]{2,1,0:T(8,128)S(1)} collective-permute-done((f32[2,128,128]{2,1,0:T(8,128)}, f32[2,128,128]{2,1,0:T(8,128)S(1)}, u32[]{:S(2)}, u32[]{:S(2)}) %collective-permute-start.6) | collective-permute-done | bytes 131104 | tf_op jit(solution)/shard_map/ppermute | solution.py:465
  20.2 1.1 collective-permute-start.14
  22.0 3.7 %fold.1 = (f32[4,16,128,128]{3,2,1,0:T(8,128)S(1)}, f32[64,128]{1,0:T(8,128)S(1)}) custom-call(s32[1]{0:T(128)S(6)} %copy.10.count.refs_1_, s32[2,128]{1,0:T(2,128)S(1)} %pad_add_fusion.slots_any.refs_0_, f32[128,128,128]{2,1,0:T(8,128)} %w_hbm.3), custom_call_target="tpu_custom_call" | custom-call | flops 20000000 | bytes 16777216 | tf_op jit(solution)/shard_map/fold/pallas_call | solution.py:83
  25.7 4.7 %forward.1 = (f32[4,128,128]{2,1,0:T(8,128)}, f32[4,128,128]{2,1,0:T(8,128)S(1)}, f32[16,128,128]{2,1,0:T(8,128)S(1)}, f32[64,128]{1,0:T(8,128)S(1)}, f32[16,128]{1,0:T(8,128)S(1)}) custom-call(s32[2,16]{1,0:T(2,128)S(1)} %bitcast.1, f32[4,128,128]{2,1,0:T(8,128)S(1)} %pack.2.refs_0_, f32[2,128,128]{2,1,0:T(8,128)S(1)} %collective-permute-done.1.refs_1_, ...), custom_call_target="tpu_custom_call" | custom-call | flops 1073741824 | bytes 8388608 | tf_op jit(solution)/shard_map/forward/pallas_call | solution.py:165
  30.4 1.7 %collective-permute-start.16 = (f32[6,128,128]{2,1,0:T(8,128)S(1)}, f32[6,128,128]{2,1,0:T(8,128)S(1)}, u32[]{:S(2)}, u32[]{:S(2)}) collective-permute-start(f32[6,128,128]{2,1,0:T(8,128)S(1)} %pack.3.refs_4_), channel_id=1, source_target_pairs={{0,128},{32,160},{64,192},{96,224},{128,0},{160,32},{192,64},{224,... | collective-permute-start | bytes 1179656 | tf_op jit(solution)/shard_map/ppermute | solution.py:465
  32.2 3.7 %backward.1 = (f32[2,128,128]{2,1,0:T(8,128)S(1)}, f32[2,128,128]{2,1,0:T(8,128)S(1)}, f32[2,128,128]{2,1,0:T(8,128)S(1)}, f32[2,128,128]{2,1,0:T(8,128)S(1)}, f32[8,128,128]{2,1,0:T(8,128)S(1)}) custom-call(s32[2,16]{1,0:T(2,128)S(1)} %bitcast.2, f32[4,16,128,128]{3,2,1,0:T(8,128)S(1)} %get-tuple-element.26.refs_8_.w_ref, ...), custom_call_target="tpu_custom_call" | custom-call | flops 1073741824 | bytes 8388608 | tf_op jit(solution)/shard_map/backward/pallas_call | solution.py:230
  36.7 7.2 %collective-permute-done.16.refs_8_ = f32[6,128,128]{2,1,0:T(8,128)S(1)} collective-permute-done((f32[6,128,128]{2,1,0:T(8,128)S(1)}, f32[6,128,128]{2,1,0:T(8,128)S(1)}, u32[]{:S(2)}, u32[]{:S(2)}) %collective-permute-start.16) | collective-permute-done | bytes 393248 | tf_op jit(solution)/shard_map/ppermute | solution.py:465
  44.0 7.2 %collective-permute-done.18.refs_10_ = f32[6,128,128]{2,1,0:T(8,128)S(1)} collective-permute-done((f32[6,128,128]{2,1,0:T(8,128)S(1)}, f32[6,128,128]{2,1,0:T(8,128)S(1)}, u32[]{:S(2)}, u32[]{:S(2)}) %collective-permute-start.18) | collective-permute-done | bytes 393248 | tf_op jit(solution)/shard_map/ppermute | solution.py:465
  52.4 2.9 %collective-permute-start.22 = (f32[4,128,128]{2,1,0:T(8,128)S(1)}, f32[4,128,128]{2,1,0:T(8,128)S(1)}, u32[]{:S(2)}, u32[]{:S(2)}) collective-permute-start(f32[4,128,128]{2,1,0:T(8,128)S(1)} %get-tuple-element.29.fx.refs_5_), channel_id=1, source_target_pairs={{0,2},{1,3},{2,0},{3,1},{4,6},{5,7},{6,4},{7,5},{8,10},{9,11},{10,... | collective-permute-start | bytes 786440 | tf_op jit(solution)/shard_map/ppermute | solution.py:472
  55.4 2.0 %spread.1 = (bf16[16,256,512]{2,1,0:T(8,128)(2,1)S(1)}, f32[4,16,128]{2,1,0:T(8,128)S(1)}) custom-call(s32[2,16]{1,0:T(2,128)S(1)} %bitcast.3, f32[2,128,128]{2,1,0:T(8,128)S(1)} %get-tuple-element.49.refs_1_, f32[16,128,128]{2,1,0:T(8,128)S(1)} %get-tuple-element.31.e_ref.refs_2_, f32[16,128]{1,0:T(8,128)S(1)} %get-tuple-element.37.refs_3_, ...), custom_call_target="tpu_custom_call" | custom-call | flops 10000000 | bytes 10485760 | tf_op jit(solution)/shard_map/spread/pallas_call | solution.py:309
  57.5 2.9 %collective-permute-done.20.refs_6_ = f32[4,128,128]{2,1,0:T(8,128)S(1)} collective-permute-done((f32[4,128,128]{2,1,0:T(8,128)S(1)}, f32[4,128,128]{2,1,0:T(8,128)S(1)}, u32[]{:S(2)}, u32[]{:S(2)}) %collective-permute-start.20) | collective-permute-done | bytes 262176 | tf_op jit(solution)/shard_map/ppermute | solution.py:472
  60.4 6.5 %collective-permute-done.21.refs_7_ = f32[4,128,128]{2,1,0:T(8,128)S(1)} collective-permute-done((f32[4,128,128]{2,1,0:T(8,128)S(1)}, f32[4,128,128]{2,1,0:T(8,128)S(1)}, u32[]{:S(2)}, u32[]{:S(2)}) %collective-permute-start.21) | collective-permute-done | bytes 262176 | tf_op jit(solution)/shard_map/ppermute | solution.py:472
  66.9 1.1 edges.4.refs_9_
  68.0 1.8 %edges.5 = (f32[4,128,128]{2,1,0:T(8,128)S(1)}, f32[4,128,128]{2,1,0:T(8,128)S(1)}) custom-call(s32[2,128]{1,0:T(2,128)S(1)} %pad_add_fusion.slots_any.refs_0_, s32[1]{0:T(128)S(6)} %copy.10.count.refs_1_, bf16[16,256,512]{2,1,0:T(8,128)(2,1)S(1)} %get-tuple-element.38.refs_2_, f32[4,16,128]{2,1,0:T(8,128)S(1)} %get-tuple-element.39.refs_3_.refs_9_, ...), custom_call_target="tpu_custom_call" | custom-call | flops 536870912 | bytes 6291456 | tf_op jit(solution)/shard_map/edges/pallas_call | solution.py:374
  69.7 2.0 %collective-permute-start.25 = (f32[4,128,128]{2,1,0:T(8,128)S(1)}, f32[4,128,128]{2,1,0:T(8,128)S(1)}, u32[]{:S(2)}, u32[]{:S(2)}) collective-permute-start(f32[4,128,128]{2,1,0:T(8,128)S(1)} %get-tuple-element.47), channel_id=1, source_target_pairs={{0,4},{1,5},{2,6},{3,7},{4,8},{5,9},{6,10},{7,11},{8,12},{9,13},{1... | collective-permute-start | bytes 786440 | tf_op jit(solution)/shard_map/ppermute | solution.py:469
  71.7 3.3 %collective-permute-start.26 = (f32[4,128,128]{2,1,0:T(8,128)S(1)}, f32[4,128,128]{2,1,0:T(8,128)S(1)}, u32[]{:S(2)}, u32[]{:S(2)}) collective-permute-start(f32[4,128,128]{2,1,0:T(8,128)S(1)} %edges.4.refs_9_), channel_id=1, source_target_pairs={{0,8},{1,9},{2,10},{3,11},{4,12},{5,13},{6,14},{7,15},{8,16},{9,17... | collective-permute-start | bytes 786440 | tf_op jit(solution)/shard_map/ppermute | solution.py:480
  75.0 1.3 %collective-permute-start.28 = (f32[4,128,128]{2,1,0:T(8,128)S(1)}, f32[4,128,128]{2,1,0:T(8,128)S(1)}, u32[]{:S(2)}, u32[]{:S(2)}) collective-permute-start(f32[4,128,128]{2,1,0:T(8,128)S(1)} %get-tuple-element.40.refs_9_), channel_id=1, source_target_pairs={{0,28},{1,29},{2,30},{3,31},{4,0},{5,1},{6,2},{7,3},{8,4},{9,5},{1... | collective-permute-start | bytes 786440 | tf_op jit(solution)/shard_map/ppermute | solution.py:469
  76.9 1.5 %collective-permute-start.10 = (f32[2,128,128]{2,1,0:T(8,128)S(1)}, f32[2,128,128]{2,1,0:T(8,128)S(1)}, u32[]{:S(2)}, u32[]{:S(2)}) collective-permute-start(f32[2,128,128]{2,1,0:T(8,128)S(1)} %get-tuple-element.51), channel_id=1, source_target_pairs={{0,128},{32,160},{64,192},{96,224},{128,0},{160,32},{192,64},{224,... | collective-permute-start | bytes 393224 | tf_op jit(solution)/shard_map/ppermute | solution.py:465
  78.4 3.3 %collective-permute-done.25.b = f32[4,128,128]{2,1,0:T(8,128)S(1)} collective-permute-done((f32[4,128,128]{2,1,0:T(8,128)S(1)}, f32[4,128,128]{2,1,0:T(8,128)S(1)}, u32[]{:S(2)}, u32[]{:S(2)}) %collective-permute-start.25) | collective-permute-done | bytes 262176 | tf_op jit(solution)/shard_map/ppermute | solution.py:469
  82.3 2.1 %edges.6 = (f32[4,128,128]{2,1,0:T(8,128)S(1)}, f32[4,128,128]{2,1,0:T(8,128)S(1)}, f32[4,128,128]{2,1,0:T(8,128)S(1)}) custom-call(s32[2,128]{1,0:T(2,128)S(1)} %pad_add_fusion.slots_any.refs_0_, s32[1]{0:T(128)S(6)} %copy.10.count.refs_1_, bf16[16,256,512]{2,1,0:T(8,128)(2,1)S(1)} %get-tuple-element.38.refs_2_, ...), custom_call_target="tpu_custom_call" | custom-call | flops 805306368 | bytes 6291456 | tf_op jit(solution)/shard_map/edges/pallas_call | solution.py:374
  84.5 1.8 %edges.7 = (f32[4,128,128]{2,1,0:T(8,128)S(1)}, f32[4,128,128]{2,1,0:T(8,128)S(1)}) custom-call(s32[2,128]{1,0:T(2,128)S(1)} %pad_add_fusion.slots_any.refs_0_, s32[1]{0:T(128)S(6)} %copy.10.count.refs_1_, bf16[16,256,512]{2,1,0:T(8,128)(2,1)S(1)} %get-tuple-element.38.refs_2_, f32[4,16,128]{2,1,0:T(8,128)S(1)} %get-tuple-element.39.refs_3_.refs_9_, ...), custom_call_target="tpu_custom_call" | custom-call | flops 536870912 | bytes 6291456 | tf_op jit(solution)/shard_map/edges/pallas_call | solution.py:374
  86.3 3.3 %collective-permute-start.24 = (f32[4,128,128]{2,1,0:T(8,128)S(1)}, f32[4,128,128]{2,1,0:T(8,128)S(1)}, u32[]{:S(2)}, u32[]{:S(2)}) collective-permute-start(f32[4,128,128]{2,1,0:T(8,128)S(1)} %get-tuple-element.45.refs_9_), channel_id=1, source_target_pairs={{0,28},{1,29},{2,30},{3,31},{4,0},{5,1},{6,2},{7,3},{8,4},{9,5},{1... | collective-permute-start | bytes 786440 | tf_op jit(solution)/shard_map/ppermute | solution.py:469
  89.8 1.2 %collective-permute-start.27 = (f32[4,128,128]{2,1,0:T(8,128)S(1)}, f32[4,128,128]{2,1,0:T(8,128)S(1)}, u32[]{:S(2)}, u32[]{:S(2)}) collective-permute-start(f32[4,128,128]{2,1,0:T(8,128)S(1)} %join.2), channel_id=1, source_target_pairs={{0,8},{1,9},{2,10},{3,11},{4,12},{5,13},{6,14},{7,15},{8,16},{9,17... | collective-permute-start | bytes 786440 | tf_op jit(solution)/shard_map/ppermute | solution.py:469
  91.0 3.0 %collective-permute-start.29 = (f32[4,128,128]{2,1,0:T(8,128)S(1)}, f32[4,128,128]{2,1,0:T(8,128)S(1)}, u32[]{:S(2)}, u32[]{:S(2)}) collective-permute-start(f32[4,128,128]{2,1,0:T(8,128)S(1)} %join.3), channel_id=1, source_target_pairs={{0,24},{1,25},{2,26},{3,27},{4,28},{5,29},{6,30},{7,31},{8,0},{9,1... | collective-permute-start | bytes 786440 | tf_op jit(solution)/shard_map/ppermute | solution.py:469
  95.7 4.8 %collective-permute-done.23.refs_0_ = f32[4,128,128]{2,1,0:T(8,128)S(1)} collective-permute-done((f32[4,128,128]{2,1,0:T(8,128)S(1)}, f32[4,128,128]{2,1,0:T(8,128)S(1)}, u32[]{:S(2)}, u32[]{:S(2)}) %collective-permute-start.23) | collective-permute-done | bytes 262176 | tf_op jit(solution)/shard_map/ppermute | solution.py:469
  100.5 9.7 %collective-permute-done.27.refs_2_ = f32[4,128,128]{2,1,0:T(8,128)S(1)} collective-permute-done((f32[4,128,128]{2,1,0:T(8,128)S(1)}, f32[4,128,128]{2,1,0:T(8,128)S(1)}, u32[]{:S(2)}, u32[]{:S(2)}) %collective-permute-start.27) | collective-permute-done | bytes 262176 | tf_op jit(solution)/shard_map/ppermute | solution.py:469
  (49 shorter events, 8.3 us)
Async XLA Ops:
  0.6 5.5 %collective-permute-start = (f32[2,128,128]{2,1,0:T(8,128)}, f32[2,128,128]{2,1,0:T(8,128)S(1)}, u32[]{:S(2)}, u32[]{:S(2)}) collective-permute-start(f32[2,128,128]{2,1,0:T(8,128)} %refs_0_.1), channel_id=1, source_target_pairs={{0,1},{1,0},{2,3},{3,2},{4,5},{5,4},{6,7},{7,6},{8,9},{9,8},{10,11... | collective-permute-start | bytes 393224 | tf_op jit(solution)/shard_map/ppermute | solution.py:472
  7.1 13.1 %collective-permute-start.12 = (f32[4,128,128]{2,1,0:T(8,128)S(1)}, f32[4,128,128]{2,1,0:T(8,128)S(1)}, u32[]{:S(2)}, u32[]{:S(2)}) collective-permute-start(f32[4,128,128]{2,1,0:T(8,128)S(1)} %pack.2.refs_0_), channel_id=1, source_target_pairs={{0,3},{1,2},{2,1},{3,0},{4,7},{5,6},{6,5},{7,4},{8,11},{9,10},{10,... | collective-permute-start | bytes 786440 | tf_op jit(solution)/shard_map/ppermute | solution.py:472
  10.2 5.7 %collective-permute-start.2 = (f32[2,128,128]{2,1,0:T(8,128)}, f32[2,128,128]{2,1,0:T(8,128)S(1)}, u32[]{:S(2)}, u32[]{:S(2)}) collective-permute-start(f32[2,128,128]{2,1,0:T(8,128)} %refs_0_.1), channel_id=1, source_target_pairs={{0,64},{32,96},{64,128},{96,160},{128,192},{160,224},{192,0},{224,... | collective-permute-start | bytes 393224 | tf_op jit(solution)/shard_map/ppermute | solution.py:465
  10.7 7.4 %collective-permute-start.4 = (f32[2,128,128]{2,1,0:T(8,128)}, f32[2,128,128]{2,1,0:T(8,128)S(1)}, u32[]{:S(2)}, u32[]{:S(2)}) collective-permute-start(f32[2,128,128]{2,1,0:T(8,128)} %refs_0_.1), channel_id=1, source_target_pairs={{0,128},{32,160},{64,192},{96,224},{128,0},{160,32},{192,64},{224,... | collective-permute-start | bytes 393224 | tf_op jit(solution)/shard_map/ppermute | solution.py:465
  13.1 6.4 %collective-permute-start.6 = (f32[2,128,128]{2,1,0:T(8,128)}, f32[2,128,128]{2,1,0:T(8,128)S(1)}, u32[]{:S(2)}, u32[]{:S(2)}) collective-permute-start(f32[2,128,128]{2,1,0:T(8,128)} %refs_0_.1), channel_id=1, source_target_pairs={{0,192},{32,224},{64,0},{96,32},{128,64},{160,96},{192,128},{224,1... | collective-permute-start | bytes 393224 | tf_op jit(solution)/shard_map/ppermute | solution.py:465
  13.1 12.6 %collective-permute-start.1 = (f32[2,128,128]{2,1,0:T(8,128)}, f32[2,128,128]{2,1,0:T(8,128)S(1)}, u32[]{:S(2)}, u32[]{:S(2)}) collective-permute-start(f32[2,128,128]{2,1,0:T(8,128)} %refs_0_.1), channel_id=1, source_target_pairs={{0,32},{32,0},{64,96},{96,64},{128,160},{160,128},{192,224},{224,1... | collective-permute-start | bytes 393224 | tf_op jit(solution)/shard_map/ppermute | solution.py:465
  15.9 9.7 %collective-permute-start.3 = (f32[2,128,128]{2,1,0:T(8,128)S(1)}, f32[2,128,128]{2,1,0:T(8,128)S(1)}, u32[]{:S(2)}, u32[]{:S(2)}) collective-permute-start(f32[2,128,128]{2,1,0:T(8,128)S(1)} %collective-permute-done.2.refs_2_), channel_id=1, source_target_pairs={{0,32},{32,0},{64,96},{96,64},{128,160},{160,128},{192,224},{224,1... | collective-permute-start | bytes 393224 | tf_op jit(solution)/shard_map/ppermute | solution.py:465
  18.1 7.6 %collective-permute-start.5 = (f32[2,128,128]{2,1,0:T(8,128)S(1)}, f32[2,128,128]{2,1,0:T(8,128)S(1)}, u32[]{:S(2)}, u32[]{:S(2)}) collective-permute-start(f32[2,128,128]{2,1,0:T(8,128)S(1)} %collective-permute-done.4.refs_4_), channel_id=1, source_target_pairs={{0,32},{32,0},{64,96},{96,64},{128,160},{160,128},{192,224},{224,1... | collective-permute-start | bytes 393224 | tf_op jit(solution)/shard_map/ppermute | solution.py:465
  19.5 6.2 %collective-permute-start.7 = (f32[2,128,128]{2,1,0:T(8,128)S(1)}, f32[2,128,128]{2,1,0:T(8,128)S(1)}, u32[]{:S(2)}, u32[]{:S(2)}) collective-permute-start(f32[2,128,128]{2,1,0:T(8,128)S(1)} %collective-permute-done.6.refs_6_), channel_id=1, source_target_pairs={{0,32},{32,0},{64,96},{96,64},{128,160},{160,128},{192,224},{224,1... | collective-permute-start | bytes 393224 | tf_op jit(solution)/shard_map/ppermute | solution.py:465
  20.2 16.3 %collective-permute-start.14 = (f32[6,128,128]{2,1,0:T(8,128)S(1)}, f32[6,128,128]{2,1,0:T(8,128)S(1)}, u32[]{:S(2)}, u32[]{:S(2)}) collective-permute-start(f32[6,128,128]{2,1,0:T(8,128)S(1)} %pack.3.refs_4_), channel_id=1, source_target_pairs={{0,64},{32,96},{64,128},{96,160},{128,192},{160,224},{192,0},{224,... | collective-permute-start | bytes 1179656 | tf_op jit(solution)/shard_map/ppermute | solution.py:465
  22.0 3.7 %copy-start = (f32[4,128,128]{2,1,0:T(8,128)S(1)}, f32[4,128,128]{2,1,0:T(8,128)}, u32[]{:S(2)}) copy-start(f32[4,128,128]{2,1,0:T(8,128)} %refs_10_.1) | copy-start | bytes 786436
  22.0 3.7 %copy-start.1 = (s32[16,2]{0,1:T(2,128)S(1)}, s32[16,2]{0,1:T(2,128)}, u32[]{:S(2)}) copy-start(s32[16,2]{0,1:T(2,128)} %param.8) | copy-start | bytes 388
  30.4 13.6 %collective-permute-start.16 = (f32[6,128,128]{2,1,0:T(8,128)S(1)}, f32[6,128,128]{2,1,0:T(8,128)S(1)}, u32[]{:S(2)}, u32[]{:S(2)}) collective-permute-start(f32[6,128,128]{2,1,0:T(8,128)S(1)} %pack.3.refs_4_), channel_id=1, source_target_pairs={{0,128},{32,160},{64,192},{96,224},{128,0},{160,32},{192,64},{224,... | collective-permute-start | bytes 1179656 | tf_op jit(solution)/shard_map/ppermute | solution.py:465
  32.1 19.2 %collective-permute-start.18 = (f32[6,128,128]{2,1,0:T(8,128)S(1)}, f32[6,128,128]{2,1,0:T(8,128)S(1)}, u32[]{:S(2)}, u32[]{:S(2)}) collective-permute-start(f32[6,128,128]{2,1,0:T(8,128)S(1)} %pack.3.refs_4_), channel_id=1, source_target_pairs={{0,192},{32,224},{64,0},{96,32},{128,64},{160,96},{192,128},{224,1... | collective-permute-start | bytes 1179656 | tf_op jit(solution)/shard_map/ppermute | solution.py:465
  35.9 15.4 %collective-permute-start.8 = (f32[8,128,128]{2,1,0:T(8,128)S(1)}, f32[8,128,128]{2,1,0:T(8,128)S(1)}, u32[]{:S(2)}, u32[]{:S(2)}) collective-permute-start(f32[8,128,128]{2,1,0:T(8,128)S(1)} %get-tuple-element.33), channel_id=1, source_target_pairs={{0,32},{32,0},{64,96},{96,64},{128,160},{160,128},{192,224},{224,1... | collective-permute-start | bytes 1572872 | tf_op jit(solution)/shard_map/ppermute | solution.py:465
  36.0 15.4 %collective-permute-start.13 = (f32[6,128,128]{2,1,0:T(8,128)S(1)}, f32[6,128,128]{2,1,0:T(8,128)S(1)}, u32[]{:S(2)}, u32[]{:S(2)}) collective-permute-start(f32[6,128,128]{2,1,0:T(8,128)S(1)} %pack.3.refs_4_), channel_id=1, source_target_pairs={{0,32},{32,0},{64,96},{96,64},{128,160},{160,128},{192,224},{224,1... | collective-permute-start | bytes 1179656 | tf_op jit(solution)/shard_map/ppermute | solution.py:465
  36.5 16.0 %collective-permute-start.15 = (f32[6,128,128]{2,1,0:T(8,128)S(1)}, f32[6,128,128]{2,1,0:T(8,128)S(1)}, u32[]{:S(2)}, u32[]{:S(2)}) collective-permute-start(f32[6,128,128]{2,1,0:T(8,128)S(1)} %collective-permute-done.14.refs_6_), channel_id=1, source_target_pairs={{0,32},{32,0},{64,96},{96,64},{128,160},{160,128},{192,224},{224,1... | collective-permute-start | bytes 1179656 | tf_op jit(solution)/shard_map/ppermute | solution.py:465
  44.0 11.4 %collective-permute-start.17 = (f32[6,128,128]{2,1,0:T(8,128)S(1)}, f32[6,128,128]{2,1,0:T(8,128)S(1)}, u32[]{:S(2)}, u32[]{:S(2)}) collective-permute-start(f32[6,128,128]{2,1,0:T(8,128)S(1)} %collective-permute-done.16.refs_8_), channel_id=1, source_target_pairs={{0,32},{32,0},{64,96},{96,64},{128,160},{160,128},{192,224},{224,1... | collective-permute-start | bytes 1179656 | tf_op jit(solution)/shard_map/ppermute | solution.py:465
  51.2 4.2 %collective-permute-start.19 = (f32[6,128,128]{2,1,0:T(8,128)S(1)}, f32[6,128,128]{2,1,0:T(8,128)S(1)}, u32[]{:S(2)}, u32[]{:S(2)}) collective-permute-start(f32[6,128,128]{2,1,0:T(8,128)S(1)} %collective-permute-done.18.refs_10_), channel_id=1, source_target_pairs={{0,32},{32,0},{64,96},{96,64},{128,160},{160,128},{192,224},{224,1... | collective-permute-start | bytes 1179656 | tf_op jit(solution)/shard_map/ppermute | solution.py:465
  51.2 9.2 %collective-permute-start.20 = (f32[4,128,128]{2,1,0:T(8,128)S(1)}, f32[4,128,128]{2,1,0:T(8,128)S(1)}, u32[]{:S(2)}, u32[]{:S(2)}) collective-permute-start(f32[4,128,128]{2,1,0:T(8,128)S(1)} %get-tuple-element.29.fx.refs_5_), channel_id=1, source_target_pairs={{0,1},{1,0},{2,3},{3,2},{4,5},{5,4},{6,7},{7,6},{8,9},{9,8},{10,11... | collective-permute-start | bytes 786440 | tf_op jit(solution)/shard_map/ppermute | solution.py:472
  51.4 15.5 %collective-permute-start.21 = (f32[4,128,128]{2,1,0:T(8,128)S(1)}, f32[4,128,128]{2,1,0:T(8,128)S(1)}, u32[]{:S(2)}, u32[]{:S(2)}) collective-permute-start(f32[4,128,128]{2,1,0:T(8,128)S(1)} %get-tuple-element.29.fx.refs_5_), channel_id=1, source_target_pairs={{0,3},{1,2},{2,1},{3,0},{4,7},{5,6},{6,5},{7,4},{8,11},{9,10},{10,... | collective-permute-start | bytes 786440 | tf_op jit(solution)/shard_map/ppermute | solution.py:472
  52.4 14.4 %collective-permute-start.22 = (f32[4,128,128]{2,1,0:T(8,128)S(1)}, f32[4,128,128]{2,1,0:T(8,128)S(1)}, u32[]{:S(2)}, u32[]{:S(2)}) collective-permute-start(f32[4,128,128]{2,1,0:T(8,128)S(1)} %get-tuple-element.29.fx.refs_5_), channel_id=1, source_target_pairs={{0,2},{1,3},{2,0},{3,1},{4,6},{5,7},{6,4},{7,5},{8,10},{9,11},{10,... | collective-permute-start | bytes 786440 | tf_op jit(solution)/shard_map/ppermute | solution.py:472
  69.7 12.0 %collective-permute-start.25 = (f32[4,128,128]{2,1,0:T(8,128)S(1)}, f32[4,128,128]{2,1,0:T(8,128)S(1)}, u32[]{:S(2)}, u32[]{:S(2)}) collective-permute-start(f32[4,128,128]{2,1,0:T(8,128)S(1)} %get-tuple-element.47), channel_id=1, source_target_pairs={{0,4},{1,5},{2,6},{3,7},{4,8},{5,9},{6,10},{7,11},{8,12},{9,13},{1... | collective-permute-start | bytes 786440 | tf_op jit(solution)/shard_map/ppermute | solution.py:469
  71.7 14.5 %collective-permute-start.26 = (f32[4,128,128]{2,1,0:T(8,128)S(1)}, f32[4,128,128]{2,1,0:T(8,128)S(1)}, u32[]{:S(2)}, u32[]{:S(2)}) collective-permute-start(f32[4,128,128]{2,1,0:T(8,128)S(1)} %edges.4.refs_9_), channel_id=1, source_target_pairs={{0,8},{1,9},{2,10},{3,11},{4,12},{5,13},{6,14},{7,15},{8,16},{9,17... | collective-permute-start | bytes 786440 | tf_op jit(solution)/shard_map/ppermute | solution.py:480
  75.0 14.6 %collective-permute-start.28 = (f32[4,128,128]{2,1,0:T(8,128)S(1)}, f32[4,128,128]{2,1,0:T(8,128)S(1)}, u32[]{:S(2)}, u32[]{:S(2)}) collective-permute-start(f32[4,128,128]{2,1,0:T(8,128)S(1)} %get-tuple-element.40.refs_9_), channel_id=1, source_target_pairs={{0,28},{1,29},{2,30},{3,31},{4,0},{5,1},{6,2},{7,3},{8,4},{9,5},{1... | collective-permute-start | bytes 786440 | tf_op jit(solution)/shard_map/ppermute | solution.py:469
  76.3 13.4 %collective-permute-start.11 = (f32[2,128,128]{2,1,0:T(8,128)S(1)}, f32[2,128,128]{2,1,0:T(8,128)S(1)}, u32[]{:S(2)}, u32[]{:S(2)}) collective-permute-start(f32[2,128,128]{2,1,0:T(8,128)S(1)} %get-tuple-element.50), channel_id=1, source_target_pairs={{0,192},{32,224},{64,0},{96,32},{128,64},{160,96},{192,128},{224,1... | collective-permute-start | bytes 393224 | tf_op jit(solution)/shard_map/ppermute | solution.py:465
  76.9 14.1 %collective-permute-start.10 = (f32[2,128,128]{2,1,0:T(8,128)S(1)}, f32[2,128,128]{2,1,0:T(8,128)S(1)}, u32[]{:S(2)}, u32[]{:S(2)}) collective-permute-start(f32[2,128,128]{2,1,0:T(8,128)S(1)} %get-tuple-element.51), channel_id=1, source_target_pairs={{0,128},{32,160},{64,192},{96,224},{128,0},{160,32},{192,64},{224,... | collective-permute-start | bytes 393224 | tf_op jit(solution)/shard_map/ppermute | solution.py:465
  81.7 12.3 %collective-permute-start.9 = (f32[2,128,128]{2,1,0:T(8,128)S(1)}, f32[2,128,128]{2,1,0:T(8,128)S(1)}, u32[]{:S(2)}, u32[]{:S(2)}) collective-permute-start(f32[2,128,128]{2,1,0:T(8,128)S(1)} %get-tuple-element.49.refs_1_), channel_id=1, source_target_pairs={{0,64},{32,96},{64,128},{96,160},{128,192},{160,224},{192,0},{224,... | collective-permute-start | bytes 393224 | tf_op jit(solution)/shard_map/ppermute | solution.py:465
  86.3 14.2 %collective-permute-start.24 = (f32[4,128,128]{2,1,0:T(8,128)S(1)}, f32[4,128,128]{2,1,0:T(8,128)S(1)}, u32[]{:S(2)}, u32[]{:S(2)}) collective-permute-start(f32[4,128,128]{2,1,0:T(8,128)S(1)} %get-tuple-element.45.refs_9_), channel_id=1, source_target_pairs={{0,28},{1,29},{2,30},{3,31},{4,0},{5,1},{6,2},{7,3},{8,4},{9,5},{1... | collective-permute-start | bytes 786440 | tf_op jit(solution)/shard_map/ppermute | solution.py:469
  89.6 10.8 %collective-permute-start.23 = (f32[4,128,128]{2,1,0:T(8,128)S(1)}, f32[4,128,128]{2,1,0:T(8,128)S(1)}, u32[]{:S(2)}, u32[]{:S(2)}) collective-permute-start(f32[4,128,128]{2,1,0:T(8,128)S(1)} %get-tuple-element.44), channel_id=1, source_target_pairs={{0,4},{1,5},{2,6},{3,7},{4,8},{5,9},{6,10},{7,11},{8,12},{9,13},{1... | collective-permute-start | bytes 786440 | tf_op jit(solution)/shard_map/ppermute | solution.py:469
  89.8 20.4 %collective-permute-start.27 = (f32[4,128,128]{2,1,0:T(8,128)S(1)}, f32[4,128,128]{2,1,0:T(8,128)S(1)}, u32[]{:S(2)}, u32[]{:S(2)}) collective-permute-start(f32[4,128,128]{2,1,0:T(8,128)S(1)} %join.2), channel_id=1, source_target_pairs={{0,8},{1,9},{2,10},{3,11},{4,12},{5,13},{6,14},{7,15},{8,16},{9,17... | collective-permute-start | bytes 786440 | tf_op jit(solution)/shard_map/ppermute | solution.py:469
  91.0 19.2 %collective-permute-start.29 = (f32[4,128,128]{2,1,0:T(8,128)S(1)}, f32[4,128,128]{2,1,0:T(8,128)S(1)}, u32[]{:S(2)}, u32[]{:S(2)}) collective-permute-start(f32[4,128,128]{2,1,0:T(8,128)S(1)} %join.3), channel_id=1, source_target_pairs={{0,24},{1,25},{2,26},{3,27},{4,28},{5,29},{6,30},{7,31},{8,0},{9,1... | collective-permute-start | bytes 786440 | tf_op jit(solution)/shard_map/ppermute | solution.py:469
